TPU v7x, 128 devices: a whole 4x4x4 slice. The times are simulated.
128 devices in a mesh: clip: 8 (over x, z_lo), head: 16 (over z_hi, y, core).
Axes of the slice: x: 4, y: 4, z: 4 (z_hi: 2, z_lo: 2; z = z_hi * 2 + z_lo), core: 2. Of those that a mesh axis runs over, the one named last changes fastest.
Arguments:
- queries: bfloat16 [16384, 4096], P(('clip', 'head')), may hold values from -6 to 6
- key_rows: bfloat16 [16384, 4096], P(('clip', 'head')), may hold values from -6 to 6
- value_rows: bfloat16 [16384, 4096], P(('clip', 'head')), may hold values from -6 to 6
- query_tangent: bfloat16 [16384, 4096], P(('clip', 'head')), may hold values from -6 to 6
- key_tangent: bfloat16 [16384, 4096], P(('clip', 'head')), may hold values from -6 to 6
- value_tangent: bfloat16 [16384, 4096], P(('clip', 'head')), may hold values from -6 to 6
- partners: int32 [16, 2], replicated, may hold values from 0 to 15, as said below
- cotangent: bfloat16 [16384, 3072], P('clip'), may hold values from -6 to 6
Outputs:
- attended: bfloat16 [16384, 4096], P(('clip', 'head'))
- attended_tangent: bfloat16 [16384, 4096], P(('clip', 'head'))
- weight_grad: float32 [3072, 4096], P('clip', 'head')
Inputs may be any that keep to these rules, and one draw needn't show every extreme that they name: `partners`: for clip c the two entries are distinct clips (c - d) mod 16 with 1 <= d <= 2 + c % 2.
All inputs are finite; a program needn't handle non-finite values.
Results may differ from a plain program's by a relative error of at most 0.0051.
Values may be sent and summed in bfloat16 or wider, within the bound.
No kernel may reach another device: no remote copies, remote signals or barrier semaphores. Data moves between devices by JAX's collectives and lax.ppermute only.
A program may use at most 192 MiB of HBM per device.

v0:
```python
import jax
import jax.numpy as jnp
from jax import lax
from jax.sharding import PartitionSpec as P

HDIM = 128
CLIP = 1024


def shifted(shard, axis, by):
    length = lax.axis_size(axis)
    return lax.ppermute(shard, axis, [(i, (i + by) % length) for i in range(length)])


def as_sent(shard):
    return jax.tree.map(lambda a: a.astype(jnp.bfloat16) if a.dtype == jnp.float32 else a, shard)


def cut_along(shard, dim, length):
    before, after = (shard.shape[:dim], shard.shape[dim + 1 :])
    return jnp.moveaxis(shard.reshape(*before, length, -1, *after), dim, 0)


def sum_at_owner(shard, axis, dim):
    length = lax.axis_size(axis)
    pieces = lax.all_to_all(cut_along(shard, dim, length), axis, 0, 0, tiled=True)
    return jnp.sum(pieces, axis=0)


def attend_block(query_block, qtan_block, key_win, value_win, ktan_win, vtan_win):
    score_scale = query_block.shape[-1] ** (-0.5)
    scores = (
        jnp.einsum("qhd,khd->hqk", query_block, key_win, preferred_element_type=jnp.float32)
        * score_scale
    )
    score_tan = (
        jnp.einsum("qhd,khd->hqk", qtan_block, key_win, preferred_element_type=jnp.float32)
        + jnp.einsum("qhd,khd->hqk", query_block, ktan_win, preferred_element_type=jnp.float32)
    ) * score_scale
    row_max = jnp.max(scores, axis=-1, keepdims=True)
    raw_weights = jnp.exp(scores - row_max)
    row_total = jnp.sum(raw_weights, axis=-1, keepdims=True)
    probability = raw_weights / row_total
    tangent_mean = jnp.sum(probability * score_tan, axis=-1, keepdims=True)
    prob_tangent = probability * (score_tan - tangent_mean)
    prob_low = probability.astype(jnp.bfloat16)
    tangent_low = prob_tangent.astype(jnp.bfloat16)
    result_out = jnp.einsum("hqk,khd->qhd", prob_low, value_win, preferred_element_type=jnp.float32)
    tangent_out = jnp.einsum(
        "hqk,khd->qhd", tangent_low, value_win, preferred_element_type=jnp.float32
    ) + jnp.einsum("hqk,khd->qhd", prob_low, vtan_win, preferred_element_type=jnp.float32)
    return (result_out.astype(jnp.bfloat16), tangent_out.astype(jnp.bfloat16))


def on_device(
    queries, key_rows, value_rows, query_tangent, key_tangent, value_tangent, partners, cotangent
):
    clip_count = lax.axis_size("clip")
    regrouped = (
        lax.all_to_all(queries, "head", split_axis=1, concat_axis=0, tiled=True),
        lax.all_to_all(key_rows, "head", split_axis=1, concat_axis=0, tiled=True),
        lax.all_to_all(value_rows, "head", split_axis=1, concat_axis=0, tiled=True),
        lax.all_to_all(query_tangent, "head", split_axis=1, concat_axis=0, tiled=True),
        lax.all_to_all(key_tangent, "head", split_axis=1, concat_axis=0, tiled=True),
        lax.all_to_all(value_tangent, "head", split_axis=1, concat_axis=0, tiled=True),
    )
    query_h, key_h, value_h, qtan_h, ktan_h, vtan_h = regrouped
    prev_key, prev_value, prev_ktan, prev_vtan = shifted(
        (key_h, value_h, ktan_h, vtan_h), "clip", 1
    )
    window_key = jnp.concatenate([prev_key, key_h], axis=0)
    window_value = jnp.concatenate([prev_value, value_h], axis=0)
    window_ktan = jnp.concatenate([prev_ktan, ktan_h], axis=0)
    window_vtan = jnp.concatenate([prev_vtan, vtan_h], axis=0)
    group_rows = query_h.shape[0]
    cols_here = query_h.shape[1]
    heads_here = cols_here // HDIM
    clips_here = group_rows // CLIP
    total_clips = clips_here * clip_count
    first_clip = lax.axis_index("clip") * clips_here
    block_rows = min(512, CLIP)

    def one_clip(within):
        partner_row = lax.dynamic_slice_in_dim(partners, first_clip + within, 1, 0)[0]
        slots_here = (partner_row - first_clip + clips_here) % total_clips
        slot_list = [clips_here + within, slots_here[0], slots_here[1]]

        def window(array):
            parts = [lax.dynamic_slice_in_dim(array, slot * CLIP, CLIP, 0) for slot in slot_list]
            return jnp.concatenate(parts, axis=0).reshape(3 * CLIP, heads_here, HDIM)

        key_win = window(window_key)
        value_win = window(window_value)
        ktan_win = window(window_ktan)
        vtan_win = window(window_vtan)
        clip_start = within * CLIP
        query_clip = lax.dynamic_slice_in_dim(query_h, clip_start, CLIP, 0).reshape(
            CLIP, heads_here, HDIM
        )
        qtan_clip = lax.dynamic_slice_in_dim(qtan_h, clip_start, CLIP, 0).reshape(
            CLIP, heads_here, HDIM
        )
        outputs = []
        tangents = []
        for block in range(CLIP // block_rows):
            lower = block * block_rows
            result_out, tangent_out = attend_block(
                query_clip[lower : lower + block_rows],
                qtan_clip[lower : lower + block_rows],
                key_win,
                value_win,
                ktan_win,
                vtan_win,
            )
            outputs.append(result_out.reshape(block_rows, cols_here))
            tangents.append(tangent_out.reshape(block_rows, cols_here))
        return (jnp.concatenate(outputs, axis=0), jnp.concatenate(tangents, axis=0))

    results = lax.map(one_clip, jnp.arange(clips_here, dtype=jnp.int32))
    output_h = results[0].reshape(group_rows, cols_here)
    tangent_h = results[1].reshape(group_rows, cols_here)
    attended, attended_tangent = (
        lax.all_to_all(as_sent(output_h), "head", split_axis=0, concat_axis=1, tiled=True).astype(
            output_h.dtype
        ),
        lax.all_to_all(as_sent(tangent_h), "head", split_axis=0, concat_axis=1, tiled=True).astype(
            tangent_h.dtype
        ),
    )
    partial_term = lax.dot_general(
        cotangent, output_h, (((0,), (0,)), ((), ())), preferred_element_type=jnp.float32
    )
    weight_grad = sum_at_owner(partial_term, "clip", 0)
    return (attended, attended_tangent, weight_grad)


def solution(mesh):
    return jax.shard_map(
        on_device,
        mesh=mesh,
        in_specs=(
            P(("clip", "head"), None),
            P(("clip", "head"), None),
            P(("clip", "head"), None),
            P(("clip", "head"), None),
            P(("clip", "head"), None),
            P(("clip", "head"), None),
            P(),
            P("clip", None),
        ),
        out_specs=(P(("clip", "head"), None), P(("clip", "head"), None), P("clip", "head")),
        check_vma=False,
    )
```

profile of v0, /device:TPU:1, one launch (start us, length us, event | category | flops | bytes accessed | tf_op | source)
XLA Modules:
  0.0 570.2 jit_solution(5212717596973026191)
XLA Ops:
  3.0 9.4 %all-to-all-start.2 = ((bf16[128,16,256]{0,2,1:T(8,128)(2,1)}), bf16[128,16,256]{0,2,1:T(8,128)(2,1)S(1)}, u32[]{:S(2)}, u32[]{:S(2)}) async-start(bf16[128,16,256]{0,2,1:T(8,128)(2,1)} %bitcast.28), calls=%async_computation.2 | async-start | bytes 2097152 | tf_op jit(solution)/shard_map/all_to_all | solution.py:61
  13.7 16.0 %all-to-all-done.2 = bf16[128,16,256]{0,2,1:T(8,128)(2,1)S(1)} async-done(((bf16[128,16,256]{0,2,1:T(8,128)(2,1)}), bf16[128,16,256]{0,2,1:T(8,128)(2,1)S(1)}, u32[]{:S(2)}, u32[]{:S(2)}) %all-to-all-start.2) | async-done | bytes 1048608 | tf_op jit(solution)/shard_map/all_to_all | solution.py:61
  35.3 16.1 %all-to-all-done.4 = bf16[128,16,256]{0,2,1:T(8,128)(2,1)S(1)} async-done(((bf16[128,16,256]{0,2,1:T(8,128)(2,1)}), bf16[128,16,256]{0,2,1:T(8,128)(2,1)S(1)}, u32[]{:S(2)}, u32[]{:S(2)}) %all-to-all-start.4) | async-done | bytes 1048608 | tf_op jit(solution)/shard_map/all_to_all | solution.py:64
  58.0 15.2 %all-to-all-done.5 = bf16[128,16,256]{0,2,1:T(8,128)(2,1)S(1)} async-done(((bf16[128,16,256]{0,2,1:T(8,128)(2,1)}), bf16[128,16,256]{0,2,1:T(8,128)(2,1)S(1)}, u32[]{:S(2)}, u32[]{:S(2)}) %all-to-all-start.5) | async-done | bytes 1048608 | tf_op jit(solution)/shard_map/all_to_all | solution.py:65
  79.6 16.1 %all-to-all-done = bf16[128,16,256]{0,2,1:T(8,128)(2,1)S(1)} async-done(((bf16[128,16,256]{0,2,1:T(8,128)(2,1)}), bf16[128,16,256]{0,2,1:T(8,128)(2,1)S(1)}, u32[]{:S(2)}, u32[]{:S(2)}) %all-to-all-start) | async-done | bytes 1048608 | tf_op jit(solution)/shard_map/all_to_all | solution.py:62
  105.2 12.2 %all-to-all-done.1 = bf16[128,16,256]{0,2,1:T(8,128)(2,1)S(1)} async-done(((bf16[128,16,256]{0,2,1:T(8,128)(2,1)}), bf16[128,16,256]{0,2,1:T(8,128)(2,1)S(1)}, u32[]{:S(2)}, u32[]{:S(2)}) %all-to-all-start.1) | async-done | bytes 1048608 | tf_op jit(solution)/shard_map/all_to_all | solution.py:60
  123.7 20.8 %collective-permute-start.2 = (bf16[2048,256]{1,0:T(8,128)(2,1)}, bf16[2048,256]{1,0:T(8,128)(2,1)}, u32[]{:S(2)}, u32[]{:S(2)}) collective-permute-start(bf16[2048,256]{1,0:T(8,128)(2,1)} %bitcast.196), channel_id=1, source_target_pairs={{0,16},{16,32},{32,48},{48,64},{64,80},{80,96},{96,112},{112,0},{1... | collective-permute-start | bytes 3145736 | tf_op jit(solution)/shard_map/ppermute | solution.py:12
  158.7 18.9 %collective-permute-done.2 = bf16[2048,256]{1,0:T(8,128)(2,1)} collective-permute-done((bf16[2048,256]{1,0:T(8,128)(2,1)}, bf16[2048,256]{1,0:T(8,128)(2,1)}, u32[]{:S(2)}, u32[]{:S(2)}) %collective-permute-start.2) | collective-permute-done | bytes 1048608 | tf_op jit(solution)/shard_map/ppermute | solution.py:12
  181.9 18.1 %collective-permute-done.3 = bf16[2048,256]{1,0:T(8,128)(2,1)} collective-permute-done((bf16[2048,256]{1,0:T(8,128)(2,1)}, bf16[2048,256]{1,0:T(8,128)(2,1)}, u32[]{:S(2)}, u32[]{:S(2)}) %collective-permute-start.3) | collective-permute-done | bytes 1048608 | tf_op jit(solution)/shard_map/ppermute | solution.py:12
  204.7 17.9 %collective-permute-done = bf16[2048,256]{1,0:T(8,128)(2,1)} collective-permute-done((bf16[2048,256]{1,0:T(8,128)(2,1)}, bf16[2048,256]{1,0:T(8,128)(2,1)}, u32[]{:S(2)}, u32[]{:S(2)}) %collective-permute-start) | collective-permute-done | bytes 1048608 | tf_op jit(solution)/shard_map/ppermute | solution.py:12
  227.2 229.5 %while.14 = (s32[]{:T(128)}, bf16[2,1024,256]{2,1,0:T(8,128)(2,1)}, bf16[2,1024,256]{2,1,0:T(8,128)(2,1)}, s32[2]{0:T(128)S(1)}, bf16[4096,256]{0,1:T(8,128)(2,1...) while((s32[]{:T(128)}, bf16[2,1024,256]{2,1,0:T(8,128)(2,1)}, ...), condition=%wide.region_7.8_spmd, body=%wide.region_0.7_spmd.sunk | while | flops 9786101760 | bytes 337176416 | solution.py:119
  236.8 9.5 %fusion.137 = (f32[2,512]{1,0:T(2,128)S(1)}, f32[2,512,3072]{2,1,0:T(8,128)}) fusion(bf16[512,2,128]{0,2,1:T(8,128)(2,1)} %bitcast.178, bf16[3072,2,128]{0,2,1:T(8,128)(2,1)S(1)} %bitcast.161), kind=kOutput, calls=%fused_computation.78.clone.1 | convolution fusion | flops 814746624 | bytes 14422016 | tf_op jit(solution)/shard_map/while/body/eval_jaxpr/sub | solution.py:41
  252.3 9.6 %multiply_reduce_fusion.7 = (f32[2,512]{1,0:T(2,128)S(1)}, f32[2,512,3072]{2,1,0:T(8,128)}) fusion(f32[2,512,3072]{2,1,0:T(8,128)} %get-tuple-element.394, f32[2,512]{1,0:T(2,128)S(1)} %get-tuple-element.395, f32[2,512,3072]{2,1,0:T(8,128)S(1)} %fusion.142, bf16[512,2,128]{0,2,1:T(8,128)(2,1)S(1)} %bitcast.179, bf16[3072,2,128]{0,2,1:T(8,128)(2,1)} %bitcast.169), kind=kOutput, calls=%fused_computation.6.clone.1 | convolution fusion | flops 821033984 | bytes 39591936 | tf_op jit(solution)/shard_map/while/body/eval_jaxpr/qhd,khd->hqk/dot_general | solution.py:38
  262.1 10.3 %fusion.143 = f32[2,128,512]{2,1,0:T(8,128)S(1)} fusion(bf16[3072,2,128]{0,2,1:T(8,128)(2,1)S(1)} %bitcast.165, f32[2,512,3072]{2,1,0:T(8,128)} %get-tuple-element.406, f32[2,512]{1,0:T(2,128)S(1)} %get-tuple-element.407, f32[2,512,3072]{2,1,0:T(8,128)} %get-tuple-element.394, f32[2,512]{1,0:T(2,128)S(1)} %get-tuple-element.395), kind=kOutput, calls=%fused_computation.14.clone.1 | convolution fusion | flops 817889280 | bytes 27271168 | tf_op jit(solution)/shard_map/while/body/eval_jaxpr/hqk,khd->qhd/dot_general | solution.py:49
  272.6 7.4 %fusion.144 = bf16[2,128,512]{2,1,0:T(8,128)(2,1)S(1)} fusion(f32[2,128,512]{2,1,0:T(8,128)S(1)} %fusion.143, bf16[3072,2,128]{0,2,1:T(8,128)(2,1)S(1)} %bitcast.171, f32[2,512,3072]{2,1,0:T(8,128)} %get-tuple-element.394, f32[2,512]{1,0:T(2,128)S(1)} %get-tuple-element.395), kind=kOutput, calls=%fused_computation.39.clone.1 | convolution fusion | flops 811859968 | bytes 14946304 | tf_op jit(solution)/shard_map/while/body/eval_jaxpr/hqk,khd->qhd/dot_general | solution.py:51
  286.8 7.2 %fusion.135 = (f32[2,512]{1,0:T(2,128)S(1)}, f32[2,512,3072]{2,1,0:T(8,128)}) fusion(bf16[512,2,128]{0,2,1:T(8,128)(2,1)S(1)} %bitcast.180, bf16[3072,2,128]{0,2,1:T(8,128)(2,1)S(1)} %bitcast.164), kind=kOutput, calls=%fused_computation.77.clone.1 | convolution fusion | flops 814746624 | bytes 14422016 | tf_op jit(solution)/shard_map/while/body/eval_jaxpr/sub | solution.py:41
  293.9 15.3 %multiply_reduce_fusion.6 = (f32[2,512]{1,0:T(2,128)S(1)}, f32[2,512,3072]{2,1,0:T(8,128)}) fusion(f32[2,512,3072]{2,1,0:T(8,128)} %get-tuple-element.391, f32[2,512]{1,0:T(2,128)S(1)} %get-tuple-element.392, f32[2,512,3072]{2,1,0:T(8,128)} %fusion.139, bf16[512,2,128]{0,2,1:T(8,128)(2,1)S(1)} %bitcast.181, bf16[3072,2,128]{0,2,1:T(8,128)(2,1)} %bitcast.170), kind=kOutput, calls=%fused_computation.3.clone.1 | convolution fusion | flops 821033984 | bytes 39591936 | tf_op jit(solution)/shard_map/while/body/eval_jaxpr/qhd,khd->hqk/dot_general | solution.py:38
  309.3 9.8 %fusion.140 = f32[2,128,512]{2,1,0:T(8,128)S(1)} fusion(bf16[3072,2,128]{0,2,1:T(8,128)(2,1)S(1)} %bitcast.166, f32[2,512,3072]{2,1,0:T(8,128)} %get-tuple-element.400, f32[2,512]{1,0:T(2,128)S(1)} %get-tuple-element.401, f32[2,512,3072]{2,1,0:T(8,128)} %get-tuple-element.391, f32[2,512]{1,0:T(2,128)S(1)} %get-tuple-element.392), kind=kOutput, calls=%fused_computation.15.clone.1 | convolution fusion | flops 817889280 | bytes 27271168 | tf_op jit(solution)/shard_map/while/body/eval_jaxpr/hqk,khd->qhd/dot_general | solution.py:49
  319.1 6.9 %fusion.141 = bf16[2,128,512]{2,1,0:T(8,128)(2,1)S(1)} fusion(f32[2,128,512]{2,1,0:T(8,128)S(1)} %fusion.140, bf16[3072,2,128]{0,2,1:T(8,128)(2,1)S(1)} %bitcast.172, f32[2,512,3072]{2,1,0:T(8,128)} %get-tuple-element.391, f32[2,512]{1,0:T(2,128)S(1)} %get-tuple-element.392), kind=kOutput, calls=%fused_computation.38.clone.1 | convolution fusion | flops 811859968 | bytes 14946304 | tf_op jit(solution)/shard_map/while/body/eval_jaxpr/hqk,khd->qhd/dot_general | solution.py:51
  327.1 6.9 %fusion.138 = bf16[2,128,512]{2,1,0:T(8,128)(2,1)S(1)} fusion(bf16[3072,2,128]{0,2,1:T(8,128)(2,1)S(1)} %bitcast.167, f32[2,512,3072]{2,1,0:T(8,128)} %get-tuple-element.394, f32[2,512]{1,0:T(2,128)S(1)} %get-tuple-element.395), kind=kOutput, calls=%fused_computation.40.clone.1 | convolution fusion | flops 811728896 | bytes 14422016 | tf_op jit(solution)/shard_map/while/body/eval_jaxpr/hqk,khd->qhd/dot_general | solution.py:48
  351.5 9.5 %fusion.137 = (f32[2,512]{1,0:T(2,128)S(1)}, f32[2,512,3072]{2,1,0:T(8,128)}) fusion(bf16[512,2,128]{0,2,1:T(8,128)(2,1)} %bitcast.178, bf16[3072,2,128]{0,2,1:T(8,128)(2,1)S(1)} %bitcast.161), kind=kOutput, calls=%fused_computation.78.clone.1 | convolution fusion | flops 814746624 | bytes 14422016 | tf_op jit(solution)/shard_map/while/body/eval_jaxpr/sub | solution.py:41
  367.0 9.6 %multiply_reduce_fusion.7 = (f32[2,512]{1,0:T(2,128)S(1)}, f32[2,512,3072]{2,1,0:T(8,128)}) fusion(f32[2,512,3072]{2,1,0:T(8,128)} %get-tuple-element.394, f32[2,512]{1,0:T(2,128)S(1)} %get-tuple-element.395, f32[2,512,3072]{2,1,0:T(8,128)S(1)} %fusion.142, bf16[512,2,128]{0,2,1:T(8,128)(2,1)S(1)} %bitcast.179, bf16[3072,2,128]{0,2,1:T(8,128)(2,1)} %bitcast.169), kind=kOutput, calls=%fused_computation.6.clone.1 | convolution fusion | flops 821033984 | bytes 39591936 | tf_op jit(solution)/shard_map/while/body/eval_jaxpr/qhd,khd->hqk/dot_general | solution.py:38
  376.8 10.3 %fusion.143 = f32[2,128,512]{2,1,0:T(8,128)S(1)} fusion(bf16[3072,2,128]{0,2,1:T(8,128)(2,1)S(1)} %bitcast.165, f32[2,512,3072]{2,1,0:T(8,128)} %get-tuple-element.406, f32[2,512]{1,0:T(2,128)S(1)} %get-tuple-element.407, f32[2,512,3072]{2,1,0:T(8,128)} %get-tuple-element.394, f32[2,512]{1,0:T(2,128)S(1)} %get-tuple-element.395), kind=kOutput, calls=%fused_computation.14.clone.1 | convolution fusion | flops 817889280 | bytes 27271168 | tf_op jit(solution)/shard_map/while/body/eval_jaxpr/hqk,khd->qhd/dot_general | solution.py:49
  387.3 7.4 %fusion.144 = bf16[2,128,512]{2,1,0:T(8,128)(2,1)S(1)} fusion(f32[2,128,512]{2,1,0:T(8,128)S(1)} %fusion.143, bf16[3072,2,128]{0,2,1:T(8,128)(2,1)S(1)} %bitcast.171, f32[2,512,3072]{2,1,0:T(8,128)} %get-tuple-element.394, f32[2,512]{1,0:T(2,128)S(1)} %get-tuple-element.395), kind=kOutput, calls=%fused_computation.39.clone.1 | convolution fusion | flops 811859968 | bytes 14946304 | tf_op jit(solution)/shard_map/while/body/eval_jaxpr/hqk,khd->qhd/dot_general | solution.py:51
  401.5 7.2 %fusion.135 = (f32[2,512]{1,0:T(2,128)S(1)}, f32[2,512,3072]{2,1,0:T(8,128)}) fusion(bf16[512,2,128]{0,2,1:T(8,128)(2,1)S(1)} %bitcast.180, bf16[3072,2,128]{0,2,1:T(8,128)(2,1)S(1)} %bitcast.164), kind=kOutput, calls=%fused_computation.77.clone.1 | convolution fusion | flops 814746624 | bytes 14422016 | tf_op jit(solution)/shard_map/while/body/eval_jaxpr/sub | solution.py:41
  408.6 15.3 %multiply_reduce_fusion.6 = (f32[2,512]{1,0:T(2,128)S(1)}, f32[2,512,3072]{2,1,0:T(8,128)}) fusion(f32[2,512,3072]{2,1,0:T(8,128)} %get-tuple-element.391, f32[2,512]{1,0:T(2,128)S(1)} %get-tuple-element.392, f32[2,512,3072]{2,1,0:T(8,128)} %fusion.139, bf16[512,2,128]{0,2,1:T(8,128)(2,1)S(1)} %bitcast.181, bf16[3072,2,128]{0,2,1:T(8,128)(2,1)} %bitcast.170), kind=kOutput, calls=%fused_computation.3.clone.1 | convolution fusion | flops 821033984 | bytes 39591936 | tf_op jit(solution)/shard_map/while/body/eval_jaxpr/qhd,khd->hqk/dot_general | solution.py:38
  424.0 9.8 %fusion.140 = f32[2,128,512]{2,1,0:T(8,128)S(1)} fusion(bf16[3072,2,128]{0,2,1:T(8,128)(2,1)S(1)} %bitcast.166, f32[2,512,3072]{2,1,0:T(8,128)} %get-tuple-element.400, f32[2,512]{1,0:T(2,128)S(1)} %get-tuple-element.401, f32[2,512,3072]{2,1,0:T(8,128)} %get-tuple-element.391, f32[2,512]{1,0:T(2,128)S(1)} %get-tuple-element.392), kind=kOutput, calls=%fused_computation.15.clone.1 | convolution fusion | flops 817889280 | bytes 27271168 | tf_op jit(solution)/shard_map/while/body/eval_jaxpr/hqk,khd->qhd/dot_general | solution.py:49
  433.8 6.9 %fusion.141 = bf16[2,128,512]{2,1,0:T(8,128)(2,1)S(1)} fusion(f32[2,128,512]{2,1,0:T(8,128)S(1)} %fusion.140, bf16[3072,2,128]{0,2,1:T(8,128)(2,1)S(1)} %bitcast.172, f32[2,512,3072]{2,1,0:T(8,128)} %get-tuple-element.391, f32[2,512]{1,0:T(2,128)S(1)} %get-tuple-element.392), kind=kOutput, calls=%fused_computation.38.clone.1 | convolution fusion | flops 811859968 | bytes 14946304 | tf_op jit(solution)/shard_map/while/body/eval_jaxpr/hqk,khd->qhd/dot_general | solution.py:51
  456.6 24.5 %all_to_all.157 = bf16[16,128,256]{2,1,0:T(8,128)(2,1)} all-to-all(bf16[16,128,256]{2,1,0:T(8,128)(2,1)} %bitcast.186), channel_id=1, replica_groups=mesh['clip'=8,'head'=16] {'head'}, dimensions={0} | all-to-all | bytes 2097152 | tf_op jit(solution)/shard_map/all_to_all | solution.py:123
  493.9 9.2 %all-to-all-done.7 = bf16[16,128,256]{2,1,0:T(8,128)(2,1)S(1)} async-done(((bf16[16,128,256]{2,1,0:T(8,128)(2,1)}), bf16[16,128,256]{2,1,0:T(8,128)(2,1)S(1)}, u32[]{:S(2)}, u32[]{:S(2)}) %all-to-all-start.7) | async-done | bytes 1048608 | tf_op jit(solution)/shard_map/all_to_all | solution.py:126
  504.1 20.2 %all-to-all-start.8 = ((f32[8,384,256]{1,2,0:T(8,128)}), f32[8,384,256]{1,2,0:T(8,128)S(1)}, u32[]{:S(2)}, u32[]{:S(2)}) async-start(f32[8,384,256]{1,2,0:T(8,128)} %bitcast.88), calls=%async_computation.8 | async-start | bytes 6291456 | tf_op jit(solution)/shard_map/all_to_all | solution.py:26
  533.3 35.7 %all-to-all-done.8 = f32[8,384,256]{1,2,0:T(8,128)S(1)} async-done(((f32[8,384,256]{1,2,0:T(8,128)}), f32[8,384,256]{1,2,0:T(8,128)S(1)}, u32[]{:S(2)}, u32[]{:S(2)}) %all-to-all-start.8) | async-done | bytes 3145760 | tf_op jit(solution)/shard_map/all_to_all | solution.py:26
  (156 shorter events, 153.2 us)
Async XLA Ops:
  0.6 11.8 %copy-start.17 = (bf16[128,4096]{1,0:T(8,128)(2,1)S(1)}, bf16[128,4096]{1,0:T(8,128)(2,1)}, u32[]{:S(2)}) copy-start(bf16[128,4096]{1,0:T(8,128)(2,1)} %param.14) | copy-start | bytes 3145732
  3.0 31.0 %copy-start.18 = (bf16[128,4096]{1,0:T(8,128)(2,1)S(1)}, bf16[128,4096]{1,0:T(8,128)(2,1)}, u32[]{:S(2)}) copy-start(bf16[128,4096]{1,0:T(8,128)(2,1)} %param.15) | copy-start | bytes 3145732
  3.0 26.8 %all-to-all-start.2 = ((bf16[128,16,256]{0,2,1:T(8,128)(2,1)}), bf16[128,16,256]{0,2,1:T(8,128)(2,1)S(1)}, u32[]{:S(2)}, u32[]{:S(2)}) async-start(bf16[128,16,256]{0,2,1:T(8,128)(2,1)} %bitcast.28), calls=%async_computation.2 | async-start | bytes 2097152 | tf_op jit(solution)/shard_map/all_to_all | solution.py:61
  29.8 21.6 %copy-start.14 = (bf16[128,16,256]{0,2,1:T(8,128)(2,1)}, bf16[128,16,256]{0,2,1:T(8,128)(2,1)S(1)}, u32[]{:S(2)}) copy-start(bf16[128,16,256]{0,2,1:T(8,128)(2,1)S(1)} %all-to-all-done.2) | copy-start | bytes 3145732
  29.8 21.6 %all-to-all-start.4 = ((bf16[128,16,256]{0,2,1:T(8,128)(2,1)}), bf16[128,16,256]{0,2,1:T(8,128)(2,1)S(1)}, u32[]{:S(2)}, u32[]{:S(2)}) async-start(bf16[128,16,256]{0,2,1:T(8,128)(2,1)} %bitcast.34), calls=%async_computation.4 | async-start | bytes 2097152 | tf_op jit(solution)/shard_map/all_to_all | solution.py:64
  51.4 26.9 %copy-start.19 = (bf16[128,4096]{1,0:T(8,128)(2,1)S(1)}, bf16[128,4096]{1,0:T(8,128)(2,1)}, u32[]{:S(2)}) copy-start(bf16[128,4096]{1,0:T(8,128)(2,1)} %param.10) | copy-start | bytes 3145732
  51.4 21.7 %all-to-all-start.5 = ((bf16[128,16,256]{0,2,1:T(8,128)(2,1)}), bf16[128,16,256]{0,2,1:T(8,128)(2,1)S(1)}, u32[]{:S(2)}, u32[]{:S(2)}) async-start(bf16[128,16,256]{0,2,1:T(8,128)(2,1)} %bitcast.37), calls=%async_computation.5 | async-start | bytes 2097152 | tf_op jit(solution)/shard_map/all_to_all | solution.py:65
  74.2 21.6 %all-to-all-start = ((bf16[128,16,256]{0,2,1:T(8,128)(2,1)}), bf16[128,16,256]{0,2,1:T(8,128)(2,1)S(1)}, u32[]{:S(2)}, u32[]{:S(2)}) async-start(bf16[128,16,256]{0,2,1:T(8,128)(2,1)} %bitcast.22), calls=%async_computation | async-start | bytes 2097152 | tf_op jit(solution)/shard_map/all_to_all | solution.py:62
  95.8 21.6 %all-to-all-start.1 = ((bf16[128,16,256]{0,2,1:T(8,128)(2,1)}), bf16[128,16,256]{0,2,1:T(8,128)(2,1)S(1)}, u32[]{:S(2)}, u32[]{:S(2)}) async-start(bf16[128,16,256]{0,2,1:T(8,128)(2,1)} %bitcast.191), calls=%async_computation.1 | async-start | bytes 2097152 | tf_op jit(solution)/shard_map/all_to_all | solution.py:60
  102.2 51.9 %collective-permute-start.1 = (bf16[2048,256]{1,0:T(8,128)(2,1)}, bf16[2048,256]{1,0:T(8,128)(2,1)}, u32[]{:S(2)}, u32[]{:S(2)}) collective-permute-start(bf16[2048,256]{1,0:T(8,128)(2,1)} %bitcast.194), channel_id=1, source_target_pairs={{0,16},{16,32},{32,48},{48,64},{64,80},{80,96},{96,112},{112,0},{1... | collective-permute-start | bytes 3145736 | tf_op jit(solution)/shard_map/ppermute | solution.py:12
  117.4 29.3 %copy-start.20 = (s32[16,2]{0,1:T(2,128)S(1)}, s32[16,2]{0,1:T(2,128)}, u32[]{:S(2)}) copy-start(s32[16,2]{0,1:T(2,128)} %param.16) | copy-start | bytes 388
  117.4 34.5 %all-to-all-start.3 = ((bf16[128,16,256]{0,2,1:T(8,128)(2,1)}), bf16[128,16,256]{0,2,1:T(8,128)(2,1)}, u32[]{:S(2)}, u32[]{:S(2)}) async-start(bf16[128,16,256]{0,2,1:T(8,128)(2,1)} %bitcast.188), calls=%async_computation.3 | async-start | bytes 2097152 | tf_op jit(solution)/shard_map/all_to_all | solution.py:63
  123.7 53.9 %collective-permute-start.2 = (bf16[2048,256]{1,0:T(8,128)(2,1)}, bf16[2048,256]{1,0:T(8,128)(2,1)}, u32[]{:S(2)}, u32[]{:S(2)}) collective-permute-start(bf16[2048,256]{1,0:T(8,128)(2,1)} %bitcast.196), channel_id=1, source_target_pairs={{0,16},{16,32},{32,48},{48,64},{64,80},{80,96},{96,112},{112,0},{1... | collective-permute-start | bytes 3145736 | tf_op jit(solution)/shard_map/ppermute | solution.py:12
  146.7 53.4 %collective-permute-start.3 = (bf16[2048,256]{1,0:T(8,128)(2,1)}, bf16[2048,256]{1,0:T(8,128)(2,1)}, u32[]{:S(2)}, u32[]{:S(2)}) collective-permute-start(bf16[2048,256]{1,0:T(8,128)(2,1)} %bitcast.39), channel_id=1, source_target_pairs={{0,16},{16,32},{32,48},{48,64},{64,80},{80,96},{96,112},{112,0},{1... | collective-permute-start | bytes 3145736 | tf_op jit(solution)/shard_map/ppermute | solution.py:12
  148.1 74.4 %collective-permute-start = (bf16[2048,256]{1,0:T(8,128)(2,1)}, bf16[2048,256]{1,0:T(8,128)(2,1)}, u32[]{:S(2)}, u32[]{:S(2)}) collective-permute-start(bf16[2048,256]{1,0:T(8,128)(2,1)} %bitcast.24), channel_id=1, source_target_pairs={{0,16},{16,32},{32,48},{48,64},{64,80},{80,96},{96,112},{112,0},{1... | collective-permute-start | bytes 3145736 | tf_op jit(solution)/shard_map/ppermute | solution.py:12
  155.8 21.8 %copy-start.16 = (bf16[128,16,256]{2,0,1:T(8,128)(2,1)S(1)}, bf16[128,16,256]{2,0,1:T(8,128)(2,1)}, u32[]{:S(2)}) copy-start(bf16[128,16,256]{2,0,1:T(8,128)(2,1)} %copy.116) | copy-start | bytes 3145732
  262.0 10.3 %copy-start.5 = (bf16[3072,256]{0,1:T(8,128)(2,1)}, bf16[3072,256]{0,1:T(8,128)(2,1)S(1)}, u32[]{:S(2)}) copy-start(bf16[3072,256]{0,1:T(8,128)(2,1)S(1)} %pad_maximum_fusion.12) | copy-start | bytes 4718596 | tf_op jit(solution)/shard_map/while
  262.1 10.3 %copy-start = (bf16[1024,256]{0,1:T(8,128)(2,1)S(1)}, bf16[1024,256]{0,1:T(8,128)(2,1)}, u32[]{:S(2)}) copy-start(bf16[1024,256]{0,1:T(8,128)(2,1)} %get-tuple-element.404) | copy-start | bytes 1572868 | tf_op jit(solution)/shard_map/while
  262.1 10.3 %copy-start.1 = (bf16[1024,256]{0,1:T(8,128)(2,1)S(1)}, bf16[1024,256]{0,1:T(8,128)(2,1)}, u32[]{:S(2)}) copy-start(bf16[1024,256]{0,1:T(8,128)(2,1)} %get-tuple-element.402) | copy-start | bytes 1572868 | tf_op jit(solution)/shard_map/while
  262.1 10.3 %copy-start.2 = (bf16[1024,256]{0,1:T(8,128)(2,1)S(1)}, bf16[1024,256]{0,1:T(8,128)(2,1)}, u32[]{:S(2)}) copy-start(bf16[1024,256]{0,1:T(8,128)(2,1)} %get-tuple-element.403) | copy-start | bytes 1572868 | tf_op jit(solution)/shard_map/while
  272.5 7.5 %copy-start.7 = (bf16[3072,256]{0,1:T(8,128)(2,1)}, bf16[3072,256]{0,1:T(8,128)(2,1)S(1)}, u32[]{:S(2)}) copy-start(bf16[3072,256]{0,1:T(8,128)(2,1)S(1)} %pad_maximum_fusion.15) | copy-start | bytes 4718596 | tf_op jit(solution)/shard_map/while
  293.9 15.3 %copy-start.6 = (bf16[3072,256]{0,1:T(8,128)(2,1)S(1)}, bf16[3072,256]{0,1:T(8,128)(2,1)}, u32[]{:S(2)}) copy-start(bf16[3072,256]{0,1:T(8,128)(2,1)} %copy-done.5) | copy-start | bytes 4718596 | tf_op jit(solution)/shard_map/while
  309.3 9.8 %copy-start.8 = (bf16[3072,256]{0,1:T(8,128)(2,1)S(1)}, bf16[3072,256]{0,1:T(8,128)(2,1)}, u32[]{:S(2)}) copy-start(bf16[3072,256]{0,1:T(8,128)(2,1)} %copy-done.7) | copy-start | bytes 4718596 | tf_op jit(solution)/shard_map/while
  376.8 10.3 %copy-start.5 = (bf16[3072,256]{0,1:T(8,128)(2,1)}, bf16[3072,256]{0,1:T(8,128)(2,1)S(1)}, u32[]{:S(2)}) copy-start(bf16[3072,256]{0,1:T(8,128)(2,1)S(1)} %pad_maximum_fusion.12) | copy-start | bytes 4718596 | tf_op jit(solution)/shard_map/while
  376.8 10.3 %copy-start = (bf16[1024,256]{0,1:T(8,128)(2,1)S(1)}, bf16[1024,256]{0,1:T(8,128)(2,1)}, u32[]{:S(2)}) copy-start(bf16[1024,256]{0,1:T(8,128)(2,1)} %get-tuple-element.404) | copy-start | bytes 1572868 | tf_op jit(solution)/shard_map/while
  376.8 10.3 %copy-start.1 = (bf16[1024,256]{0,1:T(8,128)(2,1)S(1)}, bf16[1024,256]{0,1:T(8,128)(2,1)}, u32[]{:S(2)}) copy-start(bf16[1024,256]{0,1:T(8,128)(2,1)} %get-tuple-element.402) | copy-start | bytes 1572868 | tf_op jit(solution)/shard_map/while
  376.8 10.3 %copy-start.2 = (bf16[1024,256]{0,1:T(8,128)(2,1)S(1)}, bf16[1024,256]{0,1:T(8,128)(2,1)}, u32[]{:S(2)}) copy-start(bf16[1024,256]{0,1:T(8,128)(2,1)} %get-tuple-element.403) | copy-start | bytes 1572868 | tf_op jit(solution)/shard_map/while
  408.6 15.3 %copy-start.6 = (bf16[3072,256]{0,1:T(8,128)(2,1)S(1)}, bf16[3072,256]{0,1:T(8,128)(2,1)}, u32[]{:S(2)}) copy-start(bf16[3072,256]{0,1:T(8,128)(2,1)} %copy-done.5) | copy-start | bytes 4718596 | tf_op jit(solution)/shard_map/while
  424.0 9.8 %copy-start.8 = (bf16[3072,256]{0,1:T(8,128)(2,1)S(1)}, bf16[3072,256]{0,1:T(8,128)(2,1)}, u32[]{:S(2)}) copy-start(bf16[3072,256]{0,1:T(8,128)(2,1)} %copy-done.7) | copy-start | bytes 4718596 | tf_op jit(solution)/shard_map/while
  456.6 29.0 %copy-start.12 = (bf16[2,1024,256]{2,1,0:T(8,128)(2,1)S(1)}, bf16[2,1024,256]{2,1,0:T(8,128)(2,1)}, u32[]{:S(2)}) copy-start(bf16[2,1024,256]{2,1,0:T(8,128)(2,1)} %get-tuple-element.154) | copy-start | bytes 3145732
  481.1 22.0 %all-to-all-start.7 = ((bf16[16,128,256]{2,1,0:T(8,128)(2,1)}), bf16[16,128,256]{2,1,0:T(8,128)(2,1)S(1)}, u32[]{:S(2)}, u32[]{:S(2)}) async-start(bf16[16,128,256]{2,1,0:T(8,128)(2,1)} %bitcast.198), calls=%async_computation.7 | async-start | bytes 2097152 | tf_op jit(solution)/shard_map/all_to_all | solution.py:126
  504.1 65.0 %all-to-all-start.8 = ((f32[8,384,256]{1,2,0:T(8,128)}), f32[8,384,256]{1,2,0:T(8,128)S(1)}, u32[]{:S(2)}, u32[]{:S(2)}) async-start(f32[8,384,256]{1,2,0:T(8,128)} %bitcast.88), calls=%async_computation.8 | async-start | bytes 6291456 | tf_op jit(solution)/shard_map/all_to_all | solution.py:26
  (13 other events, 48.0 us)
where the time goes:
time: 572 us; the launch traced here: 570 us
  matrix products  203 us (35%)
  waiting for transfers between devices  175 us (31%)
  starting transfers between devices  79.8 us (14%)
  local copies, waits for them, and re-layouts  70.2 us (12%)
  blocking collectives  24.5 us (4%)
  other arithmetic  10 us (2%)
  loops' own time  6.95 us (1%)
    ppermute x4, waiting for transfers between devices, shifted(): lax.ppermute(shard, axis, [(i, (i + by) % length) for i in range(length)])  54.9 us
    dot_general x4, matrix products, attend_block(): jnp.einsum('qhd,khd->hqk', query_block, ktan_win, preferred_element_type=...  49.9 us
    dot_general x4, matrix products, attend_block(): jnp.einsum('hqk,khd->qhd', tangent_low, value_win, preferred_element_type...  40.2 us
    all_to_all x1, waiting for transfers between devices, sum_at_owner(): lax.all_to_all(cut_along(shard, dim, length), axis, 0, 0, tiled=True)  35.7 us
    sub x4, matrix products, attend_block(): raw_weights = jnp.exp(scores - row_max)  33.4 us
    dot_general x4, matrix products, attend_block(): jnp.einsum('hqk,khd->qhd', prob_low, vtan_win, preferred_element_type=jnp...  28.6 us
    dot_general x4, matrix products, attend_block(): jnp.einsum('hqk,khd->qhd', prob_low, value_win, preferred_element_type=jn...  27.4 us
    all_to_all x1, blocking collectives, on_device(): lax.all_to_all(as_sent(output_h), 'head', split_axis=0, concat_axis=1, ti...  24.5 us
  transfers between devices with their start and end apart: 12, of which 10 were waited for; matrix products, arithmetic and copies ran while one was open for 9% of the time, Pallas kernels for 0%

commit v1 on v0

v1 whole, which is shorter than its diff:
```python
import functools

import jax
import jax.numpy as jnp
import numpy as np
from jax import lax
from jax.experimental import pallas as pl
from jax.experimental.pallas import tpu as pltpu
from jax.sharding import Mesh
from jax.sharding import PartitionSpec as P

HDIM = 128
CLIP = 1024
BLOCK = 256
LOG2E = 1.4426950408889634
PLANE = ("zl", "zh", "y", "c")
GROUP = ("zh", "y", "c")
CLIPS = ("x", "zl")
EVERY = ("x", "zl", "zh", "y", "c")


def attend_kernel(slots_ref, q_ref, own_ref, *rest, loads):
    halo_ref = rest[0] if len(rest) == 7 else None
    out_ref, tan_ref, kv, scores, tangents, sem = rest[-6:]
    scale = HDIM**-0.5
    clip, block = pl.program_id(0), pl.program_id(1)

    @pl.when((clip == 0) & (block == 0))
    def _():
        copies = [
            pltpu.make_async_copy(
                (halo_ref if from_halo else own_ref).at[pl.ds(source, count)],
                kv.at[pl.ds(target, count)],
                sem.at[n],
            )
            for n, (from_halo, source, target, count) in enumerate(loads)
        ]
        for copy in copies:
            copy.start()
        for copy in copies:
            copy.wait()

    both = q_ref[0]
    query = both[:, HDIM:]
    top = jnp.full((BLOCK, HDIM), -jnp.inf, jnp.float32)
    picks = [slots_ref[clip, n] for n in range(3)]
    nt = (((1,), (1,)), ((), ()))
    for n, pick in enumerate(picks):
        part = lax.dot_general(query, kv[pick, :, :HDIM], nt, preferred_element_type=jnp.float32)
        scores[:, n * CLIP : (n + 1) * CLIP] = part
        for lane in range(0, CLIP, HDIM):
            top = jnp.maximum(top, part[:, lane : lane + HDIM])
        tangents[:, n * CLIP : (n + 1) * CLIP] = lax.dot_general(
            both, kv[pick, :, : 2 * HDIM], nt, preferred_element_type=jnp.float32
        )
    top = jnp.max(top, axis=1, keepdims=True)
    total = jnp.zeros((BLOCK, HDIM), jnp.float32)
    mean = jnp.zeros((BLOCK, HDIM), jnp.float32)
    for lane in range(0, 3 * CLIP, HDIM):
        part = jnp.exp2((scores[:, lane : lane + HDIM] - top) * (scale * LOG2E))
        total += part
        mean += part * tangents[:, lane : lane + HDIM]
        scores[:, lane : lane + HDIM] = part
    inverse = 1.0 / jnp.sum(total, axis=1, keepdims=True)
    mean = jnp.sum(mean, axis=1, keepdims=True) * inverse
    out = jnp.zeros((BLOCK, 2 * HDIM), jnp.float32)
    tan = jnp.zeros((BLOCK, HDIM), jnp.float32)
    for n, pick in enumerate(picks):
        weight = scores[:, n * CLIP : (n + 1) * CLIP]
        weight_tan = weight * (tangents[:, n * CLIP : (n + 1) * CLIP] - mean)
        out += jnp.dot(
            weight.astype(jnp.bfloat16),
            kv[pick, :, 2 * HDIM :],
            preferred_element_type=jnp.float32,
        )
        tan += jnp.dot(
            weight_tan.astype(jnp.bfloat16),
            kv[pick, :, 2 * HDIM : 3 * HDIM],
            preferred_element_type=jnp.float32,
        )
    out_ref[0] = (out[:, :HDIM] * inverse).astype(jnp.bfloat16)
    tan_ref[0] = ((tan * scale + out[:, HDIM:]) * inverse).astype(jnp.bfloat16)


def attend(slots, queries, own, halo, first, loads):
    kept = [q for q in (own, halo) if q is not None]
    spec = pl.BlockSpec((1, BLOCK, HDIM), lambda i, j, s: (i, j, 0))
    shape = jax.ShapeDtypeStruct((2, CLIP, HDIM), jnp.bfloat16)
    return pl.pallas_call(
        functools.partial(attend_kernel, loads=loads),
        out_shape=(shape, shape),
        grid_spec=pltpu.PrefetchScalarGridSpec(
            num_scalar_prefetch=1,
            grid=(2, CLIP // BLOCK),
            in_specs=[pl.BlockSpec((1, BLOCK, 2 * HDIM), lambda i, j, s: (first + i, j, 0))]
            + [pl.BlockSpec(memory_space=pl.ANY)] * len(kept),
            out_specs=(spec, spec),
            scratch_shapes=[
                pltpu.VMEM((4, CLIP, 4 * HDIM), jnp.bfloat16),
                pltpu.VMEM((BLOCK, 3 * CLIP), jnp.float32),
                pltpu.VMEM((BLOCK, 3 * CLIP), jnp.float32),
                pltpu.SemaphoreType.DMA((len(loads),)),
            ],
        ),
        compiler_params=pltpu.CompilerParams(
            dimension_semantics=("arbitrary", "arbitrary"), vmem_limit_bytes=40 << 20
        ),
        cost_estimate=pl.CostEstimate(
            flops=2 * 2 * CLIP * 3 * CLIP * HDIM * 8,
            transcendentals=2 * CLIP * 3 * CLIP,
            bytes_accessed=8 << 20,
        ),
    )(slots, queries, *kept)


def to_heads(*arrays):
    rows = arrays[0].shape[0]
    cut = [a.reshape(rows, 16, 2, HDIM) for a in arrays]
    sent = jnp.concatenate(cut, axis=3).transpose(2, 1, 0, 3)
    got = lax.all_to_all(
        sent.reshape(32, rows, -1), PLANE, split_axis=0, concat_axis=0, tiled=True
    )
    return got.reshape(4, CLIP, -1)


def on_device(
    queries, key_rows, value_rows, query_tangent, key_tangent, value_tangent, partners, cotangent
):
    own = to_heads(key_rows, key_tangent, value_rows, value_tangent)
    halo = lax.ppermute(own[2:], "x", [(i, (i + 1) % 4) for i in range(4)])
    query = to_heads(query_tangent, queries)

    plane = lax.axis_index("x") * 4
    mine = lax.dynamic_slice_in_dim(partners, plane, 4, 0)
    near = (mine - plane + 2) % 16
    slots = jnp.concatenate([jnp.arange(2, 6, dtype=jnp.int32)[:, None], near], axis=1)
    late, late_tan = attend(slots[2:] - 2, query, own, None, 2, ((False, 0, 0, 4),))
    early, early_tan = attend(
        slots[:2], query, own, halo, 0, ((True, 0, 0, 2), (False, 0, 2, 2))
    )
    pair = lax.all_to_all(
        jnp.stack([early, late]).reshape(2, 2 * CLIP, HDIM), "zl", 0, 0, tiled=True
    )
    term = lax.dot_general(
        cotangent,
        pair.transpose(1, 0, 2).reshape(2 * CLIP, 2 * HDIM),
        (((0,), (0,)), ((), ())),
        preferred_element_type=jnp.float32,
    )
    term = term.astype(jnp.bfloat16).reshape(8, -1, 2 * HDIM)
    pieces = lax.all_to_all(term, CLIPS, 0, 0, tiled=True)
    weight_grad = jnp.sum(pieces.astype(jnp.float32), axis=0)

    def to_tokens(a, axes):
        got = lax.all_to_all(a, axes, 0, 0, tiled=True)
        return got

    rows = queries.shape[0]
    att = jnp.stack(
        [early.reshape(16, rows, HDIM), late.reshape(16, rows, HDIM)]
    ).reshape(32, rows, HDIM)
    tan = jnp.stack(
        [early_tan.reshape(16, rows, HDIM), late_tan.reshape(16, rows, HDIM)]
    ).reshape(32, rows, HDIM)
    back = to_tokens(jnp.stack([att, tan], axis=1), PLANE)
    back = back.reshape(2, 16, 2, rows, HDIM).transpose(2, 3, 1, 0, 4).reshape(2, rows, 32 * HDIM)
    return back[0], back[1], weight_grad


def solution(mesh):
    shape = (4, 2, 2, 4, 2)
    fine = Mesh(np.asarray(mesh.devices).reshape(shape), EVERY)
    rows = P(EVERY, None)
    return jax.shard_map(
        on_device,
        mesh=fine,
        in_specs=(rows, rows, rows, rows, rows, rows, P(), P(CLIPS, None)),
        out_specs=(rows, rows, P(CLIPS, GROUP)),
        check_vma=False,
    )
```

time: 572 us -> 265 us (0.46)
  matrix products: 203 us -> 7.98 us
  waiting for transfers between devices: 175 us -> 116 us
  starting transfers between devices: 79.8 us -> 29.3 us
  Pallas kernels: 0 us -> 49.6 us
  local copies, waits for them, and re-layouts: 70.2 us -> 31 us
  blocking collectives: 24.5 us -> 15 us
  loops' own time: 6.95 us -> 0 us
    dot_general x21 -> x1, matrix products: 169 us -> 7.98 us  [on_device(): lax.dot_general(cotangent, pair.transpose(1, 0, 2).reshape(2 * CLIP, 2 *...]
    ppermute x4 -> x1, waiting for transfers between devices: 54.9 us -> 0.01 us  [on_device(): halo = lax.ppermute(own[2:], 'x', [(i, (i + 1) % 4) for i in range(4)])]
    pallas_call x0 -> x2, Pallas kernels: none -> 49.6 us  [attend(): pl.pallas_call(functools.partial(attend_kernel, loads=loads), out_shape=(...]
    sub x4 -> x0, matrix products: 33.4 us -> none  [attend_block(): raw_weights = jnp.exp(scores - row_max)]
    all_to_all x8 -> x4, starting transfers between devices: 55.9 us -> 28.1 us  [the longest x2 15.7 us: to_heads(): lax.all_to_all(sent.reshape(32, rows, -1), PLANE, split_axis=0, concat_ax...]
    ppermute x4 -> x1, starting transfers between devices: 23.9 us -> 1.21 us  [on_device(): halo = lax.ppermute(own[2:], 'x', [(i, (i + 1) % 4) for i in range(4)])]
    while x61 -> x0, local copies, waits for them, and re-layouts: 17 us -> none  [the longest x5 11.8 us: on_device(): results = lax.map(one_clip, jnp.arange(clips_here, dtype=jnp.int32))]
    all_to_all x8 -> x0, local copies, waits for them, and re-layouts: 15.3 us -> none  [the longest x1 2.28 us: on_device(): lax.all_to_all(key_rows, 'head', split_axis=1, concat_axis=0, tiled=True)]
  transfers between devices with their start and end apart: 12 -> 5, of which waited for: 10 -> 4; matrix products, arithmetic and copies ran while one was open for 9% -> 6% of each run, Pallas kernels for 0% -> 9%
where the time goes in v1:
time: 265 us; the launch traced here: 264 us
  waiting for transfers between devices  116 us (44%)
  Pallas kernels  49.6 us (19%)
  local copies, waits for them, and re-layouts  31 us (12%)
  starting transfers between devices  29.3 us (11%)
  other arithmetic  15.1 us (6%)
  blocking collectives  15 us (6%)
  matrix products  7.98 us (3%)
    all_to_all x2, waiting for transfers between devices, to_heads(): lax.all_to_all(sent.reshape(32, rows, -1), PLANE, split_axis=0, concat_ax...  69.3 us
    pallas_call x2, Pallas kernels, attend(): pl.pallas_call(functools.partial(attend_kernel, loads=loads), out_shape=(...  49.6 us
    all_to_all x1, waiting for transfers between devices, to_tokens(): got = lax.all_to_all(a, axes, 0, 0, tiled=True)  26.6 us
    all_to_all x1, waiting for transfers between devices, on_device(): pieces = lax.all_to_all(term, CLIPS, 0, 0, tiled=True)  19.7 us
    all_to_all x2, starting transfers between devices, to_heads(): lax.all_to_all(sent.reshape(32, rows, -1), PLANE, split_axis=0, concat_ax...  15.7 us
    all_to_all x1, blocking collectives, on_device(): lax.all_to_all(jnp.stack([early, late]).reshape(2, 2 * CLIP, HDIM), 'zl',...  15 us
    transpose x2, other arithmetic, to_heads(): sent = jnp.concatenate(cut, axis=3).transpose(2, 1, 0, 3)  10.5 us
    reshape x6, local copies, waits for them, and re-layouts, to_heads(): cut = [a.reshape(rows, 16, 2, HDIM) for a in arrays]  9.48 us
  transfers between devices with their start and end apart: 5, of which 4 were waited for; matrix products, arithmetic and copies ran while one was open for 6% of the time, Pallas kernels for 9%

profile of v1, /device:TPU:1, one launch (start us, length us, event | category | flops | bytes accessed | tf_op | source)
XLA Modules:
  0.0 264.4 jit_solution(17342486425229695056)
XLA Ops:
  0.6 1.8 reshape.67
  2.4 1.8 reshape.68
  4.2 1.8 reshape.69
  6.0 2.6 reshape.70
  8.6 7.7 %maximum_bitcast_fusion = bf16[2,16,128,512]{3,0,1,2:T(2,128)(2,1)S(1)} fusion(bf16[128,16,2,128]{3,2,1,0:T(2,128)(2,1)} %reshape.70, bf16[128,16,2,128]{3,2,1,0:T(2,128)(2,1)S(1)} %reshape.69, bf16[128,16,2,128]{3,2,1,0:T(2,128)(2,1)S(1)} %reshape.68, bf16[128,16,2,128]{3,2,1,0:T(2,128)(2,1)S(1)} %reshape.67), kind=kLoop, calls=%fused_computation | loop fusion | flops 16777216 | bytes 8388608 | tf_op jit(solution)/shard_map/transpose | solution.py:119
  16.3 4.4 %copy.30 = bf16[2,16,128,512]{3,2,1,0:T(8,128)(2,1)} copy(bf16[2,16,128,512]{3,0,1,2:T(2,128)(2,1)S(1)} %maximum_bitcast_fusion) | data formatting | bytes 8388608 | tf_op jit(solution)/shard_map/transpose | solution.py:119
  20.7 9.8 %all-to-all-start.1 = ((bf16[32,128,512]{2,1,0:T(8,128)(2,1)}), bf16[32,128,512]{2,1,0:T(8,128)(2,1)}, u32[]{:S(2)}, u32[]{:S(2)}) async-start(bf16[32,128,512]{2,1,0:T(8,128)(2,1)} %bitcast.40), calls=%async_computation.1 | async-start | bytes 8388608 | tf_op jit(solution)/shard_map/all_to_all | solution.py:120
  32.0 2.8 %maximum_bitcast_fusion.1 = bf16[2,16,128,256]{3,0,1,2:T(2,128)(2,1)S(1)} fusion(bf16[128,16,2,128]{3,2,1,0:T(2,128)(2,1)S(1)} %reshape.64, bf16[128,16,2,128]{3,2,1,0:T(2,128)(2,1)S(1)} %reshape.63), kind=kLoop, calls=%fused_computation.3 | loop fusion | flops 4194304 | bytes 4194304 | tf_op jit(solution)/shard_map/transpose | solution.py:119
  34.9 2.6 copy.29
  37.4 44.7 %all-to-all-done.1 = bf16[32,128,512]{2,1,0:T(8,128)(2,1)} async-done(((bf16[32,128,512]{2,1,0:T(8,128)(2,1)}), bf16[32,128,512]{2,1,0:T(8,128)(2,1)}, u32[]{:S(2)}, u32[]{:S(2)}) %all-to-all-start.1) | async-done | bytes 4194336 | tf_op jit(solution)/shard_map/all_to_all | solution.py:120
  82.2 5.9 %all-to-all-start = ((bf16[32,128,256]{2,1,0:T(8,128)(2,1)}), bf16[32,128,256]{2,1,0:T(8,128)(2,1)S(1)}, u32[]{:S(2)}, u32[]{:S(2)}) async-start(bf16[32,128,256]{2,1,0:T(8,128)(2,1)} %bitcast.41), calls=%async_computation | async-start | bytes 4194304 | tf_op jit(solution)/shard_map/all_to_all | solution.py:120
  88.0 3.1 %slice.26 = bf16[16,128,512]{2,1,0:T(8,128)(2,1)} slice(bf16[32,128,512]{2,1,0:T(8,128)(2,1)} %all-to-all-done.1), slice={[16:32], [0:128], [0:512]} | slice | bytes 4194304 | tf_op jit(solution)/shard_map/slice | solution.py:130
  91.2 1.2 collective-permute-start
  92.7 24.6 %all-to-all-done = bf16[32,128,256]{2,1,0:T(8,128)(2,1)S(1)} async-done(((bf16[32,128,256]{2,1,0:T(8,128)(2,1)}), bf16[32,128,256]{2,1,0:T(8,128)(2,1)S(1)}, u32[]{:S(2)}, u32[]{:S(2)}) %all-to-all-start) | async-done | bytes 2097184 | tf_op jit(solution)/shard_map/all_to_all | solution.py:120
  117.2 24.8 %shard_map.104 = (bf16[2,1024,128]{2,1,0:T(8,128)(2,1)S(1)}, bf16[2,1024,128]{2,1,0:T(8,128)(2,1)S(1)}) custom-call(s32[2,3]{1,0:T(2,128)S(1)} %get-tuple-element.20.slots_ref, bf16[4,1024,256]{2,1,0:T(8,128)(2,1)S(1)} %bitcast.32, bf16[4,1024,512]{2,1,0:T(8,128)(2,1)} %bitcast.5.own_ref), custom_call_target="tpu_custom_call" | custom-call | flops 12884901888 | bytes 8388608 | tf_op jit(solution)/shard_map/pallas_call | solution.py:89
  142.8 1.1 copy.34
  143.9 24.8 %shard_map.103 = (bf16[2,1024,128]{2,1,0:T(8,128)(2,1)S(1)}, bf16[2,1024,128]{2,1,0:T(8,128)(2,1)S(1)}) custom-call(s32[2,3]{1,0:T(2,128)S(1)} %get-tuple-element.19.slots_ref, bf16[4,1024,256]{2,1,0:T(8,128)(2,1)S(1)} %bitcast.33, bf16[4,1024,512]{2,1,0:T(8,128)(2,1)} %bitcast.5.own_ref, bf16[2,1024,512]{2,1,0:T(8,128)(2,1)} %collective-permute-done.rest_0_), custom_call_target="tpu_custom_call" | custom-call | flops 12884901888 | bytes 8388608 | tf_op jit(solution)/shard_map/pallas_call | solution.py:89
  169.8 1.1 pad_maximum_fusion.3
  170.9 15.0 %all_to_all.25 = bf16[2,2048,128]{1,2,0:T(8,128)(2,1)S(1)} all-to-all(bf16[2,2048,128]{1,2,0:T(8,128)(2,1)S(1)} %pad_maximum_fusion.3), channel_id=1, replica_groups=mesh['x'=4,'zl'=2,'zh'=2,'y'=4,'c'=2] {'zl'}, dimensions={0} | all-to-all | bytes 2097152 | tf_op jit(solution)/shard_map/all_to_all | solution.py:141
  185.9 8.0 %convolution_convert_fusion = bf16[256,3072]{1,0:T(8,128)(2,1)S(1)} fusion(bf16[2048,256]{0,1:T(8,128)(2,1)S(1)} %bitcast.49, bf16[2048,3072]{1,0:T(8,128)(2,1)} %param.15), kind=kOutput, calls=%fused_computation.1 | convolution fusion | flops 3222011904 | bytes 15204352 | tf_op jit(solution)/shard_map/dot_general | solution.py:144
  194.0 1.3 copy.44
  195.3 4.3 %all-to-all-start.4 = ((bf16[8,384,256]{1,2,0:T(8,128)(2,1)}), bf16[8,384,256]{1,2,0:T(8,128)(2,1)}, u32[]{:S(2)}, u32[]{:S(2)}) async-start(bf16[8,384,256]{1,2,0:T(8,128)(2,1)} %bitcast.43), calls=%async_computation.4 | async-start | bytes 3145728 | tf_op jit(solution)/shard_map/all_to_all | solution.py:151
  199.8 1.5 pad_maximum_fusion
  201.4 19.7 %all-to-all-done.4 = bf16[8,384,256]{1,2,0:T(8,128)(2,1)} async-done(((bf16[8,384,256]{1,2,0:T(8,128)(2,1)}), bf16[8,384,256]{1,2,0:T(8,128)(2,1)}, u32[]{:S(2)}, u32[]{:S(2)}) %all-to-all-start.4) | async-done | bytes 1572896 | tf_op jit(solution)/shard_map/all_to_all | solution.py:151
  221.1 8.1 %all-to-all-start.2 = ((bf16[32,2,128,128]{3,2,1,0:T(8,128)(2,1)}), bf16[32,2,128,128]{3,2,1,0:T(8,128)(2,1)S(1)}, u32[]{:S(2)}, u32[]{:S(2)}) async-start(bf16[32,2,128,128]{3,2,1,0:T(8,128)(2,1)} %pad_maximum_fusion), calls=%async_computation.2 | async-start | bytes 4194304 | tf_op jit(solution)/shard_map/all_to_all | solution.py:155
  229.2 1.7 convert_reduce_fusion
  230.9 0.9 copy.39
  231.8 26.6 %all-to-all-done.2 = bf16[32,2,128,128]{3,2,1,0:T(8,128)(2,1)S(1)} async-done(((bf16[32,2,128,128]{3,2,1,0:T(8,128)(2,1)}), bf16[32,2,128,128]{3,2,1,0:T(8,128)(2,1)S(1)}, u32[]{:S(2)}, u32[]{:S(2)}) %all-to-all-start.2) | async-done | bytes 2097184 | tf_op jit(solution)/shard_map/all_to_all | solution.py:155
  258.3 1.2 fusion.1
  259.5 1.6 copy.31
  261.1 1.3 copy.37
  263.1 1.3 copy.38
  (29 shorter events, 4.5 us)
Async XLA Ops:
  0.6 91.8 %copy-start = (s32[16,2]{0,1:T(2,128)S(1)}, s32[16,2]{0,1:T(2,128)}, u32[]{:S(2)}) copy-start(s32[16,2]{0,1:T(2,128)} %param.14) | copy-start | bytes 388
  20.7 9.8 %copy-start.6 = (bf16[128,4096]{1,0:T(8,128)(2,1)S(1)}, bf16[128,4096]{1,0:T(8,128)(2,1)}, u32[]{:S(2)}) copy-start(bf16[128,4096]{1,0:T(8,128)(2,1)} %param.11) | copy-start | bytes 3145732
  20.7 10.6 %copy-start.7 = (bf16[128,4096]{1,0:T(8,128)(2,1)S(1)}, bf16[128,4096]{1,0:T(8,128)(2,1)}, u32[]{:S(2)}) copy-start(bf16[128,4096]{1,0:T(8,128)(2,1)} %param.8) | copy-start | bytes 3145732
  20.7 61.5 %all-to-all-start.1 = ((bf16[32,128,512]{2,1,0:T(8,128)(2,1)}), bf16[32,128,512]{2,1,0:T(8,128)(2,1)}, u32[]{:S(2)}, u32[]{:S(2)}) async-start(bf16[32,128,512]{2,1,0:T(8,128)(2,1)} %bitcast.40), calls=%async_computation.1 | async-start | bytes 8388608 | tf_op jit(solution)/shard_map/all_to_all | solution.py:120
  82.2 35.1 %all-to-all-start = ((bf16[32,128,256]{2,1,0:T(8,128)(2,1)}), bf16[32,128,256]{2,1,0:T(8,128)(2,1)S(1)}, u32[]{:S(2)}, u32[]{:S(2)}) async-start(bf16[32,128,256]{2,1,0:T(8,128)(2,1)} %bitcast.41), calls=%async_computation | async-start | bytes 4194304 | tf_op jit(solution)/shard_map/all_to_all | solution.py:120
  91.2 52.7 %collective-permute-start = (bf16[2,1024,512]{2,1,0:T(8,128)(2,1)}, bf16[2,1024,512]{2,1,0:T(8,128)(2,1)}, u32[]{:S(2)}, u32[]{:S(2)}) collective-permute-start(bf16[2,1024,512]{2,1,0:T(8,128)(2,1)} %bitcast.6), channel_id=1, source_target_pairs={{0,32},{32,64},{64,96},{96,0},{1,33},{33,65},{65,97},{97,1},{2,34}... | collective-permute-start | bytes 6291464 | tf_op jit(solution)/shard_map/ppermute | solution.py:130
  142.0 0.8 copy-start.2
  168.7 0.8 copy-start.4
  193.9 5.8 %copy-start.3 = (bf16[2,1024,128]{2,1,0:T(8,128)(2,1)S(1)}, bf16[2,1024,128]{2,1,0:T(8,128)(2,1)}, u32[]{:S(2)}) copy-start(bf16[2,1024,128]{2,1,0:T(8,128)(2,1)} %copy-done.2) | copy-start | bytes 1572868
  193.9 5.8 %copy-start.5 = (bf16[2,1024,128]{2,1,0:T(8,128)(2,1)S(1)}, bf16[2,1024,128]{2,1,0:T(8,128)(2,1)}, u32[]{:S(2)}) copy-start(bf16[2,1024,128]{2,1,0:T(8,128)(2,1)} %copy-done.4) | copy-start | bytes 1572868
  195.3 25.8 %all-to-all-start.4 = ((bf16[8,384,256]{1,2,0:T(8,128)(2,1)}), bf16[8,384,256]{1,2,0:T(8,128)(2,1)}, u32[]{:S(2)}, u32[]{:S(2)}) async-start(bf16[8,384,256]{1,2,0:T(8,128)(2,1)} %bitcast.43), calls=%async_computation.4 | async-start | bytes 3145728 | tf_op jit(solution)/shard_map/all_to_all | solution.py:151
  221.1 37.3 %all-to-all-start.2 = ((bf16[32,2,128,128]{3,2,1,0:T(8,128)(2,1)}), bf16[32,2,128,128]{3,2,1,0:T(8,128)(2,1)S(1)}, u32[]{:S(2)}, u32[]{:S(2)}) async-start(bf16[32,2,128,128]{3,2,1,0:T(8,128)(2,1)} %pad_maximum_fusion), calls=%async_computation.2 | async-start | bytes 4194304 | tf_op jit(solution)/shard_map/all_to_all | solution.py:155
  259.5 4.9 %copy-start.1 = (s32[16,2]{0,1:T(2,128)S(1)}, s32[16,2]{0,1:T(2,128)}, u32[]{:S(2)}) copy-start(s32[16,2]{0,1:T(2,128)} %param.14) | copy-start | bytes 388

commit v2 on v1

v2 whole, which is shorter than its diff:
```python
import functools

import jax
import jax.numpy as jnp
import numpy as np
from jax import lax
from jax.experimental import pallas as pl
from jax.experimental.pallas import tpu as pltpu
from jax.sharding import Mesh
from jax.sharding import PartitionSpec as P

HDIM = 128
CLIP = 1024
HEADS = 32
HALF = 64
SENDERS = 8
BLOCK = SENDERS * HALF
TILE = 256
LOG2E = 1.4426950408889634
PLANE = ("zl", "zh", "y", "c")
GROUP = ("zh", "y", "c")
CLIPS = ("x", "zl")
EVERY = ("x", "zl", "zh", "y", "c")
NT = (((1,), (1,)), ((), ()))
bf16, f32 = jnp.bfloat16, jnp.float32


def pack_kernel(*refs):
    *ins, out = refs
    for n, ref in enumerate(ins):
        for head in range(4):
            out[head % 2, head // 2, :, n * HDIM : (n + 1) * HDIM] = ref[
                :, head * HDIM : (head + 1) * HDIM
            ]


def to_heads(*arrays):
    rows, width = arrays[0].shape[0], len(arrays) * HDIM
    sent = pl.pallas_call(
        pack_kernel,
        out_shape=jax.ShapeDtypeStruct((2, 16, rows, width), bf16),
        grid=(8,),
        in_specs=[pl.BlockSpec((rows, 4 * HDIM), lambda j: (0, j))] * len(arrays),
        compiler_params=pltpu.CompilerParams(vmem_limit_bytes=60 << 20),
        out_specs=pl.BlockSpec((2, 2, rows, width), lambda j: (0, j, 0, 0)),
        cost_estimate=pl.CostEstimate(
            flops=0, transcendentals=0, bytes_accessed=4 * rows * HEADS * width
        ),
    )(*arrays)
    return lax.all_to_all(sent.reshape(32, rows, width), PLANE, 0, 0, tiled=True)


def unpack_kernel(first_ref, second_ref, out_ref, tan_ref):
    for half, ref in enumerate((first_ref, second_ref)):
        rows = slice(half * HALF, (half + 1) * HALF)
        for head in range(4):
            lanes = slice(head * HDIM, (head + 1) * HDIM)
            out_ref[rows, lanes] = ref[head % 2, head // 2, :, :HDIM]
            tan_ref[rows, lanes] = ref[head % 2, head // 2, :, HDIM:]


def unpack(first, second):
    shape = jax.ShapeDtypeStruct((2 * HALF, HEADS * HDIM), bf16)
    spec = pl.BlockSpec((2 * HALF, 4 * HDIM), lambda j: (0, j))
    return pl.pallas_call(
        unpack_kernel,
        out_shape=(shape, shape),
        grid=(8,),
        in_specs=[pl.BlockSpec((2, 2, HALF, 2 * HDIM), lambda j: (0, j, 0, 0))] * 2,
        out_specs=(spec, spec),
        cost_estimate=pl.CostEstimate(flops=0, transcendentals=0, bytes_accessed=4 << 20),
    )(first.reshape(2, 16, HALF, 2 * HDIM), second.reshape(2, 16, HALF, 2 * HDIM))


def attend_kernel(slots_ref, q_ref, *rest, loads, sources, halves, first_half):
    kept, rest = rest[:sources], rest[sources:]
    *outs, kv, scores, tangents, sem = rest
    outs = outs if halves == 2 else outs[-2:]
    scale = HDIM**-0.5
    half, clip = pl.program_id(0), pl.program_id(1)
    start = (half == 0) & (clip == 0)
    split = 2 * HDIM

    def copies(part):
        lanes = pl.ds(part * split, split)
        return [
            pltpu.make_async_copy(
                kept[which].at[pl.ds(source * SENDERS, count * SENDERS), :, lanes],
                kv.at[pl.ds(target * SENDERS, count * SENDERS), :, lanes],
                sem.at[part, n],
            )
            for n, (which, source, target, count) in enumerate(loads)
        ]

    @pl.when(start)
    def _():
        for copy in copies(0) + copies(1):
            copy.start()
        for copy in copies(0):
            copy.wait()

    both = q_ref[...].reshape(BLOCK, 2 * HDIM)
    query = both[:, HDIM:]
    picks = [slots_ref[clip, n] * SENDERS for n in range(3)]
    tiles = [(n, k) for n in range(3) for k in range(0, CLIP, TILE)]

    def window(n, k, lanes):
        rows = pl.ds(picks[n] + k // 128, TILE // 128)
        return kv[rows, :, lanes].reshape(TILE, -1)

    top = None
    for n, k in tiles:
        part = lax.dot_general(query, window(n, k, slice(0, HDIM)), NT, preferred_element_type=f32)
        at = n * CLIP + k
        scores[:, at : at + TILE] = part
        for lane in range(0, TILE, HDIM):
            piece = part[:, lane : lane + HDIM]
            top = piece if top is None else jnp.maximum(top, piece)
    top = jnp.broadcast_to(jnp.max(top, axis=1, keepdims=True), (BLOCK, HDIM))
    total = jnp.zeros((BLOCK, HDIM), f32)
    mean = jnp.zeros((BLOCK, HDIM), f32)
    for n, k in tiles:
        tangent = lax.dot_general(
            both, window(n, k, slice(0, 2 * HDIM)), NT, preferred_element_type=f32
        )
        for lane in range(0, TILE, HDIM):
            at = n * CLIP + k + lane
            part = jnp.exp2((scores[:, at : at + HDIM] - top) * (scale * LOG2E))
            moved = part * tangent[:, lane : lane + HDIM]
            total += part
            mean += moved
            scores[:, at : at + HDIM] = part
            tangents[:, at : at + HDIM] = moved
    inverse = 1.0 / jnp.sum(total, axis=1, keepdims=True)
    mean = jnp.broadcast_to(jnp.sum(mean, axis=1, keepdims=True) * inverse, (BLOCK, HDIM))

    @pl.when(start)
    def _():
        for copy in copies(1):
            copy.wait()

    out = jnp.zeros((BLOCK, 2 * HDIM), f32)
    tan = jnp.zeros((BLOCK, HDIM), f32)
    for n, k in tiles:
        weights, weights_tan = [], []
        for lane in range(0, TILE, HDIM):
            at = n * CLIP + k + lane
            part = scores[:, at : at + HDIM]
            weights.append(part.astype(bf16))
            weights_tan.append((tangents[:, at : at + HDIM] - part * mean).astype(bf16))
        out += jnp.dot(
            jnp.concatenate(weights, axis=1),
            window(n, k, slice(2 * HDIM, 4 * HDIM)),
            preferred_element_type=f32,
        )
        tan += jnp.dot(
            jnp.concatenate(weights_tan, axis=1),
            window(n, k, slice(2 * HDIM, 3 * HDIM)),
            preferred_element_type=f32,
        )
    result = (out[:, :HDIM] * inverse).astype(bf16).reshape(SENDERS, HALF, HDIM)
    result_tan = ((tan * scale + out[:, HDIM:]) * inverse).astype(bf16)
    result_tan = result_tan.reshape(SENDERS, HALF, HDIM)

    def store(pair_ref, sent_ref):
        pair_ref[...] = result
        sent_ref[:, :, :HDIM] = result
        sent_ref[:, :, HDIM:] = result_tan

    if halves == 1:
        store(*outs)
    else:
        pl.when(half == 0)(lambda: store(outs[0], outs[1]))
        pl.when(half == 1)(lambda: store(outs[2], outs[3]))


def attend(slots, queries, kept, loads, late, first_half, halves, filled=None):
    first = 2 if late else 0
    pair_shape = jax.ShapeDtypeStruct((16, HALF, HDIM), bf16)
    sent_shape = jax.ShapeDtypeStruct((32, HALF, 2 * HDIM), bf16)
    in_specs = [
        pl.BlockSpec((SENDERS, HALF, 2 * HDIM), lambda h, c, s: (first + c, first_half + h, 0))
    ] + [pl.BlockSpec(memory_space=pl.ANY)] * (len(kept) + (filled is not None))
    out_shape, out_specs = [], []
    for n in range(halves):

        def place(h, c, n=n):
            return c if halves == 1 else jnp.where(h == n, c, 1 - n)

        out_shape += [pair_shape, sent_shape]
        out_specs += [
            pl.BlockSpec((SENDERS, HALF, HDIM), lambda h, c, s, p=place: (p(h, c), 0, 0)),
            pl.BlockSpec(
                (SENDERS, HALF, 2 * HDIM), lambda h, c, s, p=place: (first + p(h, c), 0, 0)
            ),
        ]
    operands = (slots, queries, *kept) + (() if filled is None else (filled,))
    return pl.pallas_call(
        functools.partial(
            attend_kernel,
            loads=loads,
            sources=len(kept) + (filled is not None),
            halves=halves,
            first_half=first_half,
        ),
        out_shape=out_shape,
        grid_spec=pltpu.PrefetchScalarGridSpec(
            num_scalar_prefetch=1,
            grid=(halves, 2),
            in_specs=in_specs,
            out_specs=out_specs,
            scratch_shapes=[
                pltpu.VMEM((4 * SENDERS, 128, 4 * HDIM), bf16),
                pltpu.VMEM((BLOCK, 3 * CLIP), f32),
                pltpu.VMEM((BLOCK, 3 * CLIP), f32),
                pltpu.SemaphoreType.DMA((2, len(loads))),
            ],
        ),
        input_output_aliases={} if filled is None else {len(operands) - 1: 1},
        compiler_params=pltpu.CompilerParams(
            dimension_semantics=("arbitrary", "arbitrary"), vmem_limit_bytes=60 << 20
        ),
        cost_estimate=pl.CostEstimate(
            flops=2 * 2 * halves * BLOCK * 3 * CLIP * HDIM * 8,
            transcendentals=2 * halves * BLOCK * 3 * CLIP,
            bytes_accessed=8 << 20,
        ),
    )(*operands)


def grad_kernel(side_ref, own_a, own_b, got_a, got_b, late_a, late_b, cot_ref, out_ref, pair, turned, sem):
    @pl.when(pl.program_id(0) == 0)
    def _():
        def load(left, right):
            copies = []
            for column, halves in enumerate((left, right)):
                for half, ref in enumerate(halves):
                    copies.append(
                        pltpu.make_async_copy(
                            ref,
                            pair.at[:, pl.ds(half * HALF, HALF), pl.ds(column * HDIM, HDIM)],
                            sem.at[2 * column + half],
                        )
                    )
            for copy in copies:
                copy.start()
            for copy in copies:
                copy.wait()

        early = (own_a, own_b)
        far = (got_a, got_b)
        late = (late_a, late_b)
        pl.when(side_ref[0] == 0)(lambda: load(early, far))
        pl.when(side_ref[0] == 1)(lambda: load(far, late))
        turned[...] = pair[...].reshape(2 * CLIP, 2 * HDIM).T

    part = jnp.dot(turned[...], cot_ref[...], preferred_element_type=f32)
    out_ref[0] = part.T.astype(bf16)


def grad_term(side, early, got, late, cotangent):
    rows, columns = cotangent.shape
    width = columns // 8
    return pl.pallas_call(
        grad_kernel,
        out_shape=jax.ShapeDtypeStruct((8, width, 2 * HDIM), bf16),
        grid_spec=pltpu.PrefetchScalarGridSpec(
            num_scalar_prefetch=1,
            grid=(8,),
            in_specs=[pl.BlockSpec(memory_space=pl.ANY)] * 6
            + [pl.BlockSpec((rows, width), lambda j, s: (0, j))],
            out_specs=pl.BlockSpec((1, width, 2 * HDIM), lambda j, s: (j, 0, 0)),
            scratch_shapes=[
                pltpu.VMEM((16, 2 * HALF, 2 * HDIM), bf16),
                pltpu.VMEM((2 * HDIM, rows), bf16),
                pltpu.SemaphoreType.DMA((4,)),
            ],
        ),
        compiler_params=pltpu.CompilerParams(vmem_limit_bytes=60 << 20),
        cost_estimate=pl.CostEstimate(
            flops=2 * rows * columns * 2 * HDIM, transcendentals=0, bytes_accessed=15 << 20
        ),
    )(side, *early, *got, *late, cotangent)


def on_device(
    queries, key_rows, value_rows, query_tangent, key_tangent, value_tangent, partners, cotangent
):
    own = to_heads(key_rows, key_tangent, value_rows, value_tangent)
    halo = lax.ppermute(own[16:], "x", [(i, (i + 1) % 4) for i in range(4)])
    query = to_heads(query_tangent, queries)

    plane = lax.axis_index("x") * 4
    mine = lax.dynamic_slice_in_dim(partners, plane, 4, 0)
    near = (mine - plane + 2) % 16
    slots = jnp.concatenate([jnp.arange(2, 6, dtype=jnp.int32)[:, None], near], axis=1)
    late1, sent1, late2, sent2 = attend(
        slots[2:] - 2, query, (own,), ((0, 0, 0, 4),), True, 0, 2
    )
    window = ((1, 0, 0, 2), (0, 0, 2, 2))
    early1, sent1 = attend(slots[:2], query, (own, halo), window, False, 0, 1, sent1)
    early2, sent2 = attend(slots[:2], query, (own, halo), window, False, 1, 1, sent2)

    side = lax.axis_index("zl")

    def swap(late, early):
        return lax.ppermute(jnp.where(side == 0, late, early), "zl", [(0, 1), (1, 0)])

    got1, got2 = swap(late1, early1), swap(late2, early2)
    term = grad_term(side[None], (early1, early2), (got1, got2), (late1, late2), cotangent)
    back1 = lax.all_to_all(sent1, PLANE, 0, 0, tiled=True)
    sent2, _ = lax.optimization_barrier((sent2, got2))
    back2 = lax.all_to_all(sent2, PLANE, 0, 0, tiled=True)
    pieces = lax.all_to_all(term, CLIPS, 0, 0, tiled=True)
    weight_grad = jnp.sum(pieces.astype(f32), axis=0)
    attended, attended_tangent = unpack(back1, back2)
    return attended, attended_tangent, weight_grad


def solution(mesh):
    fine = Mesh(np.asarray(mesh.devices).reshape(4, 2, 2, 4, 2), EVERY)
    rows = P(EVERY, None)
    return jax.shard_map(
        on_device,
        mesh=fine,
        in_specs=(rows, rows, rows, rows, rows, rows, P(), P(CLIPS, None)),
        out_specs=(rows, rows, P(CLIPS, GROUP)),
        check_vma=False,
    )
```

time: 265 us -> 241 us (0.909)
  Pallas kernels: 49.6 us -> 80.7 us
  local copies, waits for them, and re-layouts: 31 us -> 6.42 us
  blocking collectives: 15 us -> 0 us
  other arithmetic: 15.1 us -> 1.72 us
  starting transfers between devices: 29.3 us -> 38.2 us
  matrix products: 7.98 us -> 0 us
  waiting for transfers between devices: 116 us -> 111 us
    pallas_call x2 -> x7, Pallas kernels: 49.6 us -> 80.7 us  [the longest x3 49.5 us: attend(): pl.pallas_call(functools.partial(attend_kernel, loads=loads, sources=len(...]
    all_to_all x3 -> x4, waiting for transfers between devices: 95.9 us -> 69.8 us  [the longest x2 69.8 us: to_heads(): lax.all_to_all(sent.reshape(32, rows, width), PLANE, 0, 0, tiled=True)]
    ppermute x1 -> x3, waiting for transfers between devices: 0.01 us -> 24 us  [the longest x2 24 us: swap(): lax.ppermute(jnp.where(side == 0, late, early), 'zl', [(0, 1), (1, 0)])]
    all_to_all x1 -> x0, blocking collectives: 15 us -> none  [on_device(): lax.all_to_all(jnp.stack([early, late]).reshape(2, 2 * CLIP, HDIM), 'zl',...]
    reshape x7 -> x0, local copies, waits for them, and re-layouts: 10.8 us -> none  [the longest x6 9.48 us: to_heads(): cut = [a.reshape(rows, 16, 2, HDIM) for a in arrays]]
    transpose x2 -> x0, other arithmetic: 10.5 us -> none  [to_heads(): sent = jnp.concatenate(cut, axis=3).transpose(2, 1, 0, 3)]
    dot_general x1 -> x0, matrix products: 7.98 us -> none  [on_device(): lax.dot_general(cotangent, pair.transpose(1, 0, 2).reshape(2 * CLIP, 2 *...]
    transpose x2 -> x0, local copies, waits for them, and re-layouts: 6.95 us -> none  [to_heads(): sent = jnp.concatenate(cut, axis=3).transpose(2, 1, 0, 3)]
  transfers between devices with their start and end apart: 5 -> 8, of which waited for: 4 -> 5; matrix products, arithmetic and copies ran while one was open for 6% -> 2% of each run, Pallas kernels for 9% -> 25%
where the time goes in v2:
time: 241 us; the launch traced here: 239 us
  waiting for transfers between devices  111 us (46%)
  Pallas kernels  80.7 us (33%)
  starting transfers between devices  38.2 us (16%)
  local copies, waits for them, and re-layouts  6.42 us (3%)
    all_to_all x2, waiting for transfers between devices, to_heads(): lax.all_to_all(sent.reshape(32, rows, width), PLANE, 0, 0, tiled=True)  69.8 us
    pallas_call x3, Pallas kernels, attend(): pl.pallas_call(functools.partial(attend_kernel, loads=loads, sources=len(...  49.5 us
    ppermute x2, waiting for transfers between devices, swap(): lax.ppermute(jnp.where(side == 0, late, early), 'zl', [(0, 1), (1, 0)])  24 us
    all_to_all x1, waiting for transfers between devices, on_device(): pieces = lax.all_to_all(term, CLIPS, 0, 0, tiled=True)  17.2 us
    all_to_all x2, starting transfers between devices, to_heads(): lax.all_to_all(sent.reshape(32, rows, width), PLANE, 0, 0, tiled=True)  15.5 us
    pallas_call x2, Pallas kernels, to_heads(): pl.pallas_call(pack_kernel, out_shape=jax.ShapeDtypeStruct((2, 16, rows,...  12.8 us
    pallas_call x1, Pallas kernels, grad_term(): pl.pallas_call(grad_kernel, out_shape=jax.ShapeDtypeStruct((8, width, 2 *...  12.5 us
    all_to_all x1, starting transfers between devices, on_device(): back2 = lax.all_to_all(sent2, PLANE, 0, 0, tiled=True)  7.73 us
  transfers between devices with their start and end apart: 8, of which 5 were waited for; matrix products, arithmetic and copies ran while one was open for 2% of the time, Pallas kernels for 25%

profile of v2, /device:TPU:1, one launch (start us, length us, event | category | flops | bytes accessed | tf_op | source)
XLA Modules:
  0.0 238.9 jit_solution(7170657021180137082)
XLA Ops:
  0.6 0.0 copy-start
  0.6 7.0 %shard_map.104 = bf16[2,16,128,512]{3,2,1,0:T(8,128)(2,1)} custom-call(bf16[128,4096]{1,0:T(8,128)(2,1)} %refs_0_.3, bf16[128,4096]{1,0:T(8,128)(2,1)} %refs_1_.3, bf16[128,4096]{1,0:T(8,128)(2,1)} %refs_2_.1, bf16[128,4096]{1,0:T(8,128)(2,1)} %refs_3_.1), custom_call_target="tpu_custom_call" | custom-call | bytes 8388608 | tf_op jit(solution)/shard_map/pallas_call | solution.py:39
  7.6 9.7 %all-to-all-start.1 = ((bf16[32,128,512]{2,1,0:T(8,128)(2,1)}), bf16[32,128,512]{2,1,0:T(8,128)(2,1)}, u32[]{:S(2)}, u32[]{:S(2)}) async-start(bf16[32,128,512]{2,1,0:T(8,128)(2,1)} %bitcast.5), calls=%async_computation.1 | async-start | bytes 8388608 | tf_op jit(solution)/shard_map/all_to_all | solution.py:50
  17.3 5.9 %shard_map.103 = bf16[2,16,128,256]{3,2,1,0:T(8,128)(2,1)} custom-call(bf16[128,4096]{1,0:T(8,128)(2,1)} %refs_0_.2, bf16[128,4096]{1,0:T(8,128)(2,1)} %refs_1_.2), custom_call_target="tpu_custom_call" | custom-call | bytes 4194304 | tf_op jit(solution)/shard_map/pallas_call | solution.py:39
  23.1 45.8 %all-to-all-done.1.rest_0_ = bf16[32,128,512]{2,1,0:T(8,128)(2,1)} async-done(((bf16[32,128,512]{2,1,0:T(8,128)(2,1)}), bf16[32,128,512]{2,1,0:T(8,128)(2,1)}, u32[]{:S(2)}, u32[]{:S(2)}) %all-to-all-start.1) | async-done | bytes 4194336 | tf_op jit(solution)/shard_map/all_to_all | solution.py:50
  69.0 5.9 %all-to-all-start = ((bf16[32,128,256]{2,1,0:T(8,128)(2,1)}), bf16[32,128,256]{2,1,0:T(8,128)(2,1)S(1)}, u32[]{:S(2)}, u32[]{:S(2)}) async-start(bf16[32,128,256]{2,1,0:T(8,128)(2,1)} %bitcast.6), calls=%async_computation | async-start | bytes 4194304 | tf_op jit(solution)/shard_map/all_to_all | solution.py:50
  74.8 3.2 %slice.13 = bf16[16,128,512]{2,1,0:T(8,128)(2,1)} slice(bf16[32,128,512]{2,1,0:T(8,128)(2,1)} %all-to-all-done.1.rest_0_), slice={[16:32], [0:128], [0:512]} | slice | bytes 4194304 | tf_op jit(solution)/shard_map/slice | solution.py:290
  78.0 1.2 collective-permute-start
  79.2 0.1 constant_dynamic-slice_fusion
  79.3 0.1 copy.14
  79.4 0.1 pad_add_fusion
  79.5 0.6 slice_add_fusion
  80.1 24.0 %all-to-all-done.q_ref = bf16[32,128,256]{2,1,0:T(8,128)(2,1)S(1)} async-done(((bf16[32,128,256]{2,1,0:T(8,128)(2,1)}), bf16[32,128,256]{2,1,0:T(8,128)(2,1)S(1)}, u32[]{:S(2)}, u32[]{:S(2)}) %all-to-all-start) | async-done | bytes 2097184 | tf_op jit(solution)/shard_map/all_to_all | solution.py:50
  104.0 1.4 copy-done.3
  105.4 23.0 %shard_map.105 = (bf16[16,64,128]{2,1,0:T(8,128)(2,1)}, bf16[32,64,256]{2,1,0:T(8,128)(2,1)}, bf16[16,64,128]{2,1,0:T(8,128)(2,1)}, bf16[32,64,256]{2,1,0:T(8,128)(2,1)}) custom-call(s32[2,3]{1,0:T(2,128)} %get-tuple-element.25.slots_ref, bf16[32,128,256]{2,1,0:T(8,128)(2,1)} %copy-done.3, bf16[32,128,512]{2,1,0:T(8,128)(2,1)} %all-to-all-done.1.rest_0_), custom_call_target="tpu_custom_call" | custom-call | flops 12884901888 | bytes 8388608 | tf_op jit(solution)/shard_map/pallas_call | solution.py:198
  128.4 0.0 collective-permute-done.rest_1_
  128.4 13.2 %shard_map.106 = (bf16[16,64,128]{2,1,0:T(8,128)(2,1)}, bf16[32,64,256]{2,1,0:T(8,128)(2,1)}) custom-call(s32[2,3]{1,0:T(2,128)} %get-tuple-element.26.slots_ref, bf16[32,128,256]{2,1,0:T(8,128)(2,1)} %copy-done.3, bf16[32,128,512]{2,1,0:T(8,128)(2,1)} %all-to-all-done.1.rest_0_, ...), custom_call_target="tpu_custom_call", output_to_operand_aliasing={{1}: (4, {})} | custom-call | flops 6442450944 | bytes 8388608 | tf_op jit(solution)/shard_map/pallas_call | solution.py:198
  141.6 6.3 %all-to-all-start.2 = ((bf16[32,64,256]{2,1,0:T(8,128)(2,1)}), bf16[32,64,256]{2,1,0:T(8,128)(2,1)S(1)}, u32[]{:S(2)}, u32[]{:S(2)}) async-start(bf16[32,64,256]{2,1,0:T(8,128)(2,1)} %get-tuple-element.15), calls=%async_computation.2 | async-start | bytes 2097152 | tf_op jit(solution)/shard_map/all_to_all | solution.py:311
  147.9 13.3 %shard_map.107 = (bf16[16,64,128]{2,1,0:T(8,128)(2,1)}, bf16[32,64,256]{2,1,0:T(8,128)(2,1)}) custom-call(s32[2,3]{1,0:T(2,128)} %get-tuple-element.26.slots_ref, bf16[32,128,256]{2,1,0:T(8,128)(2,1)} %copy-done.3, bf16[32,128,512]{2,1,0:T(8,128)(2,1)} %all-to-all-done.1.rest_0_, ...), custom_call_target="tpu_custom_call", output_to_operand_aliasing={{1}: (4, {})} | custom-call | flops 6442450944 | bytes 8388608 | tf_op jit(solution)/shard_map/pallas_call | solution.py:198
  161.2 0.0 copy-start.4
  161.3 2.5 %collective-permute-start.1 = (bf16[16,64,128]{2,1,0:T(8,128)(2,1)S(1)}, bf16[16,64,128]{2,1,0:T(8,128)(2,1)S(1)}, u32[]{:S(2)}, u32[]{:S(2)}) collective-permute-start(bf16[16,64,128]{2,1,0:T(8,128)(2,1)S(1)} %broadcast_select_fusion.1), channel_id=1, source_target_pairs={{0,16},{16,0},{1,17},{17,1},{2,18},{18,2},{3,19},{19,3},{4,20},{20... | collective-permute-start | bytes 786440 | tf_op jit(solution)/shard_map/ppermute | solution.py:307
  163.8 6.4 %collective-permute-done.1.got_b = bf16[16,64,128]{2,1,0:T(8,128)(2,1)S(1)} collective-permute-done((bf16[16,64,128]{2,1,0:T(8,128)(2,1)S(1)}, bf16[16,64,128]{2,1,0:T(8,128)(2,1)S(1)}, u32[]{:S(2)}, u32[]{:S(2)}) %collective-permute-start.1) | collective-permute-done | bytes 262176 | tf_op jit(solution)/shard_map/ppermute | solution.py:307
  170.2 7.7 %all-to-all-start.3 = ((bf16[32,64,256]{2,1,0:T(8,128)(2,1)}), bf16[32,64,256]{2,1,0:T(8,128)(2,1)S(1)}, u32[]{:S(2)}, u32[]{:S(2)}) async-start(bf16[32,64,256]{2,1,0:T(8,128)(2,1)} %get-tuple-element.20), calls=%async_computation.3 | async-start | bytes 2097152 | tf_op jit(solution)/shard_map/all_to_all | solution.py:313
  178.0 1.5 collective-permute-start.2
  179.5 17.6 %collective-permute-done.2.got_a = bf16[16,64,128]{2,1,0:T(8,128)(2,1)S(1)} collective-permute-done((bf16[16,64,128]{2,1,0:T(8,128)(2,1)S(1)}, bf16[16,64,128]{2,1,0:T(8,128)(2,1)S(1)}, u32[]{:S(2)}, u32[]{:S(2)}) %collective-permute-start.2) | collective-permute-done | bytes 262176 | tf_op jit(solution)/shard_map/ppermute | solution.py:307
  197.0 0.7 copy-done.8
  197.7 12.5 %shard_map.109 = bf16[8,384,256]{2,1,0:T(8,128)(2,1)} custom-call(s32[1]{0:T(128)} %bitcast.4.side_ref, bf16[16,64,128]{2,1,0:T(8,128)(2,1)} %get-tuple-element.23.own_a, bf16[16,64,128]{2,1,0:T(8,128)(2,1)} %get-tuple-element.19.own_b, bf16[16,64,128]{2,1,0:T(8,128)(2,1)} %copy-done.8, bf16[16,64,128]{2,1,0:T(8,128)(2,1)} %copy-done.7, ...), custom_call_target="tpu_custom_call" | custom-call | flops 3221225472 | bytes 15728640 | tf_op jit(solution)/shard_map/pallas_call | solution.py:264
  210.3 1.0 copy-done.2
  211.3 3.6 %all-to-all-start.4 = ((bf16[8,384,256]{2,1,0:T(8,128)(2,1)}), bf16[8,384,256]{2,1,0:T(8,128)(2,1)S(1)}, u32[]{:S(2)}, u32[]{:S(2)}) async-start(bf16[8,384,256]{2,1,0:T(8,128)(2,1)} %shard_map.109), calls=%async_computation.4 | async-start | bytes 3145728 | tf_op jit(solution)/shard_map/all_to_all | solution.py:314
  214.9 5.9 %shard_map.108 = (bf16[128,4096]{1,0:T(8,128)(2,1)}, bf16[128,4096]{1,0:T(8,128)(2,1)}) custom-call(bf16[2,16,64,256]{3,2,1,0:T(8,128)(2,1)} %bitcast.7, bf16[2,16,64,256]{3,2,1,0:T(8,128)(2,1)} %bitcast.8), custom_call_target="tpu_custom_call" | custom-call | bytes 4194304 | tf_op jit(solution)/shard_map/pallas_call | solution.py:65
  220.7 17.2 %all-to-all-done.4 = bf16[8,384,256]{2,1,0:T(8,128)(2,1)S(1)} async-done(((bf16[8,384,256]{2,1,0:T(8,128)(2,1)}), bf16[8,384,256]{2,1,0:T(8,128)(2,1)S(1)}, u32[]{:S(2)}, u32[]{:S(2)}) %all-to-all-start.4) | async-done | bytes 1572896 | tf_op jit(solution)/shard_map/all_to_all | solution.py:314
  237.9 1.0 convert_reduce_fusion
  (19 shorter events, 0.1 us)
Async XLA Ops:
  0.6 78.6 %copy-start = (s32[16,2]{0,1:T(2,128)S(1)}, s32[16,2]{0,1:T(2,128)}, u32[]{:S(2)}) copy-start(s32[16,2]{0,1:T(2,128)} %param.14) | copy-start | bytes 388
  7.6 61.4 %all-to-all-start.1 = ((bf16[32,128,512]{2,1,0:T(8,128)(2,1)}), bf16[32,128,512]{2,1,0:T(8,128)(2,1)}, u32[]{:S(2)}, u32[]{:S(2)}) async-start(bf16[32,128,512]{2,1,0:T(8,128)(2,1)} %bitcast.5), calls=%async_computation.1 | async-start | bytes 8388608 | tf_op jit(solution)/shard_map/all_to_all | solution.py:50
  69.0 35.1 %all-to-all-start = ((bf16[32,128,256]{2,1,0:T(8,128)(2,1)}), bf16[32,128,256]{2,1,0:T(8,128)(2,1)S(1)}, u32[]{:S(2)}, u32[]{:S(2)}) async-start(bf16[32,128,256]{2,1,0:T(8,128)(2,1)} %bitcast.6), calls=%async_computation | async-start | bytes 4194304 | tf_op jit(solution)/shard_map/all_to_all | solution.py:50
  78.0 50.4 %collective-permute-start = (bf16[16,128,512]{2,1,0:T(8,128)(2,1)}, bf16[16,128,512]{2,1,0:T(8,128)(2,1)}, u32[]{:S(2)}, u32[]{:S(2)}) collective-permute-start(bf16[16,128,512]{2,1,0:T(8,128)(2,1)} %slice.13), channel_id=1, source_target_pairs={{0,32},{32,64},{64,96},{96,0},{1,33},{33,65},{65,97},{97,1},{2,34}... | collective-permute-start | bytes 6291464 | tf_op jit(solution)/shard_map/ppermute | solution.py:290
  104.0 1.4 copy-start.3
  141.6 28.6 %all-to-all-start.2 = ((bf16[32,64,256]{2,1,0:T(8,128)(2,1)}), bf16[32,64,256]{2,1,0:T(8,128)(2,1)S(1)}, u32[]{:S(2)}, u32[]{:S(2)}) async-start(bf16[32,64,256]{2,1,0:T(8,128)(2,1)} %get-tuple-element.15), calls=%async_computation.2 | async-start | bytes 2097152 | tf_op jit(solution)/shard_map/all_to_all | solution.py:311
  147.9 13.4 %copy-start.5 = (bf16[16,64,128]{2,1,0:T(8,128)(2,1)S(1)}, bf16[16,64,128]{2,1,0:T(8,128)(2,1)}, u32[]{:S(2)}) copy-start(bf16[16,64,128]{2,1,0:T(8,128)(2,1)} %get-tuple-element.18.late_b) | copy-start | bytes 786436
  161.2 16.7 %copy-start.4 = (bf16[16,64,128]{2,1,0:T(8,128)(2,1)S(1)}, bf16[16,64,128]{2,1,0:T(8,128)(2,1)}, u32[]{:S(2)}) copy-start(bf16[16,64,128]{2,1,0:T(8,128)(2,1)} %get-tuple-element.24.late_a) | copy-start | bytes 786436
  161.2 16.7 %copy-start.6 = (bf16[16,64,128]{2,1,0:T(8,128)(2,1)S(1)}, bf16[16,64,128]{2,1,0:T(8,128)(2,1)}, u32[]{:S(2)}) copy-start(bf16[16,64,128]{2,1,0:T(8,128)(2,1)} %get-tuple-element.23.own_a) | copy-start | bytes 786436
  161.3 8.9 %collective-permute-start.1 = (bf16[16,64,128]{2,1,0:T(8,128)(2,1)S(1)}, bf16[16,64,128]{2,1,0:T(8,128)(2,1)S(1)}, u32[]{:S(2)}, u32[]{:S(2)}) collective-permute-start(bf16[16,64,128]{2,1,0:T(8,128)(2,1)S(1)} %broadcast_select_fusion.1), channel_id=1, source_target_pairs={{0,16},{16,0},{1,17},{17,1},{2,18},{18,2},{3,19},{19,3},{4,20},{20... | collective-permute-start | bytes 786440 | tf_op jit(solution)/shard_map/ppermute | solution.py:307
  170.2 26.9 %copy-start.7 = (bf16[16,64,128]{2,1,0:T(8,128)(2,1)}, bf16[16,64,128]{2,1,0:T(8,128)(2,1)S(1)}, u32[]{:S(2)}) copy-start(bf16[16,64,128]{2,1,0:T(8,128)(2,1)S(1)} %collective-permute-done.1.got_b) | copy-start | bytes 786436
  170.2 40.1 %copy-start.1 = (bf16[32,64,256]{2,1,0:T(8,128)(2,1)}, bf16[32,64,256]{2,1,0:T(8,128)(2,1)S(1)}, u32[]{:S(2)}) copy-start(bf16[32,64,256]{2,1,0:T(8,128)(2,1)S(1)} %all-to-all-done.2) | copy-start | bytes 3145732
  170.2 40.1 %all-to-all-start.3 = ((bf16[32,64,256]{2,1,0:T(8,128)(2,1)}), bf16[32,64,256]{2,1,0:T(8,128)(2,1)S(1)}, u32[]{:S(2)}, u32[]{:S(2)}) async-start(bf16[32,64,256]{2,1,0:T(8,128)(2,1)} %get-tuple-element.20), calls=%async_computation.3 | async-start | bytes 2097152 | tf_op jit(solution)/shard_map/all_to_all | solution.py:313
  178.0 19.1 %collective-permute-start.2 = (bf16[16,64,128]{2,1,0:T(8,128)(2,1)S(1)}, bf16[16,64,128]{2,1,0:T(8,128)(2,1)S(1)}, u32[]{:S(2)}, u32[]{:S(2)}) collective-permute-start(bf16[16,64,128]{2,1,0:T(8,128)(2,1)S(1)} %broadcast_select_fusion), channel_id=1, source_target_pairs={{0,16},{16,0},{1,17},{17,1},{2,18},{18,2},{3,19},{19,3},{4,20},{20... | collective-permute-start | bytes 786440 | tf_op jit(solution)/shard_map/ppermute | solution.py:307
  197.0 0.7 copy-start.8
  210.3 1.0 copy-start.2
  211.3 26.7 %all-to-all-start.4 = ((bf16[8,384,256]{2,1,0:T(8,128)(2,1)}), bf16[8,384,256]{2,1,0:T(8,128)(2,1)S(1)}, u32[]{:S(2)}, u32[]{:S(2)}) async-start(bf16[8,384,256]{2,1,0:T(8,128)(2,1)} %shard_map.109), calls=%async_computation.4 | async-start | bytes 3145728 | tf_op jit(solution)/shard_map/all_to_all | solution.py:314

commit v3 on v2

--- a/solution.py
+++ b/solution.py
@@ -26,23 +26,57 @@
 
 
 def pack_kernel(*refs):
-    *ins, out = refs
-    for n, ref in enumerate(ins):
-        for head in range(4):
-            out[head % 2, head // 2, :, n * HDIM : (n + 1) * HDIM] = ref[
-                :, head * HDIM : (head + 1) * HDIM
-            ]
+    count = len(refs) - 5
+    ins, (out, rows, cut, arrived, left) = refs[:count], refs[count:]
+    steps = arrived.shape[0]
+    heads = HEADS // steps
+    width = heads * HDIM
+    reads = [
+        [
+            pltpu.make_async_copy(
+                ref.at[:, pl.ds(step * width, width)],
+                rows.at[n, :, pl.ds(step * width, width)],
+                arrived.at[step, n],
+            )
+            for n, ref in enumerate(ins)
+        ]
+        for step in range(steps)
+    ]
+    for copies in reads:
+        for copy in copies:
+            copy.start()
+    writes = []
+    for step, copies in enumerate(reads):
+        for n, copy in enumerate(copies):
+            copy.wait()
+            for head in range(step * heads, (step + 1) * heads):
+                cut[head % 2, head // 2, :, n * HDIM : (n + 1) * HDIM] = rows[
+                    n, :, head * HDIM : (head + 1) * HDIM
+                ]
+        part = pl.ds(step * heads // 2, heads // 2)
+        writes.append(pltpu.make_async_copy(cut.at[:, part], out.at[:, part], left.at[step]))
+        writes[-1].start()
+    for copy in writes:
+        copy.wait()
 
 
 def to_heads(*arrays):
-    rows, width = arrays[0].shape[0], len(arrays) * HDIM
+    count = len(arrays)
+    rows, width = arrays[0].shape[0], count * HDIM
+    steps = 4
+    anywhere = pl.BlockSpec(memory_space=pl.ANY)
     sent = pl.pallas_call(
         pack_kernel,
         out_shape=jax.ShapeDtypeStruct((2, 16, rows, width), bf16),
-        grid=(8,),
-        in_specs=[pl.BlockSpec((rows, 4 * HDIM), lambda j: (0, j))] * len(arrays),
+        in_specs=[anywhere] * count,
+        out_specs=anywhere,
+        scratch_shapes=[
+            pltpu.VMEM((count, rows, HEADS * HDIM), bf16),
+            pltpu.VMEM((2, 16, rows, width), bf16),
+            pltpu.SemaphoreType.DMA((steps, count)),
+            pltpu.SemaphoreType.DMA((steps,)),
+        ],
         compiler_params=pltpu.CompilerParams(vmem_limit_bytes=60 << 20),
-        out_specs=pl.BlockSpec((2, 2, rows, width), lambda j: (0, j, 0, 0)),
         cost_estimate=pl.CostEstimate(
             flops=0, transcendentals=0, bytes_accessed=4 * rows * HEADS * width
         ),
@@ -72,14 +106,24 @@
     )(first.reshape(2, 16, HALF, 2 * HDIM), second.reshape(2, 16, HALF, 2 * HDIM))
 
 
-def attend_kernel(slots_ref, q_ref, *rest, loads, sources, halves, first_half):
+def attend_kernel(slots_ref, q_ref, *rest, loads, sources, halves, first, first_half):
     kept, rest = rest[:sources], rest[sources:]
-    *outs, kv, scores, tangents, sem = rest
-    outs = outs if halves == 2 else outs[-2:]
+    *outs, queries, kv, scores, tangents, sem, query_sem = rest
     scale = HDIM**-0.5
     half, clip = pl.program_id(0), pl.program_id(1)
     start = (half == 0) & (clip == 0)
     split = 2 * HDIM
+    blocks = [(h, c) for h in range(halves) for c in range(2)]
+
+    def fetch(step, at):
+        return pltpu.make_async_copy(
+            q_ref.at[
+                pl.ds((first + at[1]) * SENDERS, SENDERS),
+                pl.ds((first_half + at[0]) * HALF, HALF),
+            ],
+            queries.at[step],
+            query_sem.at[step],
+        )
 
     def copies(part):
         lanes = pl.ds(part * split, split)
@@ -94,12 +138,13 @@
 
     @pl.when(start)
     def _():
-        for copy in copies(0) + copies(1):
+        fetches = [fetch(step, at) for step, at in enumerate(blocks)]
+        for copy in copies(0) + fetches + copies(1):
             copy.start()
-        for copy in copies(0):
+        for copy in copies(0) + fetches:
             copy.wait()
 
-    both = q_ref[...].reshape(BLOCK, 2 * HDIM)
+    both = queries[2 * half + clip].reshape(BLOCK, 2 * HDIM)
     query = both[:, HDIM:]
     picks = [slots_ref[clip, n] * SENDERS for n in range(3)]
     tiles = [(n, k) for n in range(3) for k in range(0, CLIP, TILE)]
@@ -178,9 +223,7 @@
     first = 2 if late else 0
     pair_shape = jax.ShapeDtypeStruct((16, HALF, HDIM), bf16)
     sent_shape = jax.ShapeDtypeStruct((32, HALF, 2 * HDIM), bf16)
-    in_specs = [
-        pl.BlockSpec((SENDERS, HALF, 2 * HDIM), lambda h, c, s: (first + c, first_half + h, 0))
-    ] + [pl.BlockSpec(memory_space=pl.ANY)] * (len(kept) + (filled is not None))
+    in_specs = [pl.BlockSpec(memory_space=pl.ANY)] * (1 + len(kept) + (filled is not None))
     out_shape, out_specs = [], []
     for n in range(halves):
 
@@ -201,6 +244,7 @@
             loads=loads,
             sources=len(kept) + (filled is not None),
             halves=halves,
+            first=first,
             first_half=first_half,
         ),
         out_shape=out_shape,
@@ -210,10 +254,12 @@
             in_specs=in_specs,
             out_specs=out_specs,
             scratch_shapes=[
+                pltpu.VMEM((2 * halves, SENDERS, HALF, 2 * HDIM), bf16),
                 pltpu.VMEM((4 * SENDERS, 128, 4 * HDIM), bf16),
                 pltpu.VMEM((BLOCK, 3 * CLIP), f32),
                 pltpu.VMEM((BLOCK, 3 * CLIP), f32),
                 pltpu.SemaphoreType.DMA((2, len(loads))),
+                pltpu.SemaphoreType.DMA((2 * halves,)),
             ],
         ),
         input_output_aliases={} if filled is None else {len(operands) - 1: 1},
@@ -228,7 +274,7 @@
     )(*operands)
 
 
-def grad_kernel(side_ref, own_a, own_b, got_a, got_b, late_a, late_b, cot_ref, out_ref, pair, turned, sem):
+def grad_kernel(side_ref, own_a, own_b, got_a, got_b, late_a, late_b, cot_ref, out_ref, pair, sem):
     @pl.when(pl.program_id(0) == 0)
     def _():
         def load(left, right):
@@ -252,10 +298,14 @@
         late = (late_a, late_b)
         pl.when(side_ref[0] == 0)(lambda: load(early, far))
         pl.when(side_ref[0] == 1)(lambda: load(far, late))
-        turned[...] = pair[...].reshape(2 * CLIP, 2 * HDIM).T
-
-    part = jnp.dot(turned[...], cot_ref[...], preferred_element_type=f32)
-    out_ref[0] = part.T.astype(bf16)
+
+    part = lax.dot_general(
+        cot_ref[...],
+        pair[...].reshape(2 * CLIP, 2 * HDIM),
+        (((0,), (0,)), ((), ())),
+        preferred_element_type=f32,
+    )
+    out_ref[...] = part.astype(bf16).reshape(out_ref.shape)
 
 
 def grad_term(side, early, got, late, cotangent):
@@ -266,13 +316,12 @@
         out_shape=jax.ShapeDtypeStruct((8, width, 2 * HDIM), bf16),
         grid_spec=pltpu.PrefetchScalarGridSpec(
             num_scalar_prefetch=1,
-            grid=(8,),
+            grid=(2,),
             in_specs=[pl.BlockSpec(memory_space=pl.ANY)] * 6
-            + [pl.BlockSpec((rows, width), lambda j, s: (0, j))],
-            out_specs=pl.BlockSpec((1, width, 2 * HDIM), lambda j, s: (j, 0, 0)),
+            + [pl.BlockSpec((rows, 4 * width), lambda j, s: (0, j))],
+            out_specs=pl.BlockSpec((4, width, 2 * HDIM), lambda j, s: (j, 0, 0)),
             scratch_shapes=[
                 pltpu.VMEM((16, 2 * HALF, 2 * HDIM), bf16),
-                pltpu.VMEM((2 * HDIM, rows), bf16),
                 pltpu.SemaphoreType.DMA((4,)),
             ],
         ),
@@ -303,10 +352,14 @@
 
     side = lax.axis_index("zl")
 
-    def swap(late, early):
-        return lax.ppermute(jnp.where(side == 0, late, early), "zl", [(0, 1), (1, 0)])
-
-    got1, got2 = swap(late1, early1), swap(late2, early2)
+    def swap(late, early, after=None):
+        sent = jnp.where(side == 0, late, early)
+        if after is not None:
+            sent, _ = lax.optimization_barrier((sent, after))
+        return lax.ppermute(sent, "zl", [(0, 1), (1, 0)])
+
+    got1 = swap(late1, early1)
+    got2 = swap(late2, early2, got1)
     term = grad_term(side[None], (early1, early2), (got1, got2), (late1, late2), cotangent)
     back1 = lax.all_to_all(sent1, PLANE, 0, 0, tiled=True)
     sent2, _ = lax.optimization_barrier((sent2, got2))

time: 241 us -> 226 us (0.938)
  Pallas kernels: 80.7 us -> 69.8 us
    ppermute x2, waiting for transfers between devices: 24 us -> 11.3 us  [swap(): return lax.ppermute(sent, 'zl', [(0, 1), (1, 0)])]
    all_to_all x1, waiting for transfers between devices: 0.01 us -> 7.54 us  [on_device(): back2 = lax.all_to_all(sent2, PLANE, 0, 0, tiled=True)]
    pallas_call x2, Pallas kernels: 12.8 us -> 5.99 us  [to_heads(): pl.pallas_call(pack_kernel, out_shape=jax.ShapeDtypeStruct((2, 16, rows,...]
    all_to_all x2, waiting for transfers between devices: 69.8 us -> 73.1 us  [to_heads(): lax.all_to_all(sent.reshape(32, rows, width), PLANE, 0, 0, tiled=True)]
    pallas_call x1, Pallas kernels: 12.5 us -> 9.67 us  [grad_term(): pl.pallas_call(grad_kernel, out_shape=jax.ShapeDtypeStruct((8, width, 2 *...]
  transfers between devices with their start and end apart: 8 -> 8, of which waited for: 5 -> 6; matrix products, arithmetic and copies ran while one was open for 2% -> 2% of each run, Pallas kernels for 25% -> 24%
where the time goes in v3:
time: 226 us
  waiting for transfers between devices  110 us (49%)
  Pallas kernels  69.8 us (31%)
  starting transfers between devices  37.4 us (17%)
  local copies, waits for them, and re-layouts  5.73 us (3%)
    all_to_all x2, waiting for transfers between devices, to_heads(): lax.all_to_all(sent.reshape(32, rows, width), PLANE, 0, 0, tiled=True)  73.1 us
    pallas_call x3, Pallas kernels, attend(): pl.pallas_call(functools.partial(attend_kernel, loads=loads, sources=len(...  48.3 us
    all_to_all x1, waiting for transfers between devices, on_device(): pieces = lax.all_to_all(term, CLIPS, 0, 0, tiled=True)  18.1 us
    all_to_all x2, starting transfers between devices, to_heads(): lax.all_to_all(sent.reshape(32, rows, width), PLANE, 0, 0, tiled=True)  15.5 us
    ppermute x2, waiting for transfers between devices, swap(): return lax.ppermute(sent, 'zl', [(0, 1), (1, 0)])  11.3 us
    pallas_call x1, Pallas kernels, grad_term(): pl.pallas_call(grad_kernel, out_shape=jax.ShapeDtypeStruct((8, width, 2 *...  9.67 us
    all_to_all x1, starting transfers between devices, on_device(): back2 = lax.all_to_all(sent2, PLANE, 0, 0, tiled=True)  8.42 us
    all_to_all x1, waiting for transfers between devices, on_device(): back2 = lax.all_to_all(sent2, PLANE, 0, 0, tiled=True)  7.54 us
  transfers between devices with their start and end apart: 8, of which 6 were waited for; matrix products, arithmetic and copies ran while one was open for 2% of the time, Pallas kernels for 24%

profile of v3, /device:TPU:1, one launch (start us, length us, event | category | flops | bytes accessed | tf_op | source)
XLA Modules:
  0.0 225.6 jit_solution(9650778497110444698)
XLA Ops:
  0.6 0.0 copy-start
  0.6 3.5 %shard_map.104 = bf16[2,16,128,512]{3,2,1,0:T(8,128)(2,1)} custom-call(bf16[128,4096]{1,0:T(8,128)(2,1)} %refs_0_.3, bf16[128,4096]{1,0:T(8,128)(2,1)} %refs_1_.3, bf16[128,4096]{1,0:T(8,128)(2,1)} %refs_2_.1, bf16[128,4096]{1,0:T(8,128)(2,1)} %refs_3_.1), custom_call_target="tpu_custom_call" | custom-call | bytes 8388608 | tf_op jit(solution)/shard_map/pallas_call | solution.py:68
  4.1 9.7 %all-to-all-start.1 = ((bf16[32,128,512]{2,1,0:T(8,128)(2,1)}), bf16[32,128,512]{2,1,0:T(8,128)(2,1)}, u32[]{:S(2)}, u32[]{:S(2)}) async-start(bf16[32,128,512]{2,1,0:T(8,128)(2,1)} %bitcast.5), calls=%async_computation.1 | async-start | bytes 8388608 | tf_op jit(solution)/shard_map/all_to_all | solution.py:84
  13.8 2.5 %shard_map.103 = bf16[2,16,128,256]{3,2,1,0:T(8,128)(2,1)} custom-call(bf16[128,4096]{1,0:T(8,128)(2,1)} %refs_0_.2, bf16[128,4096]{1,0:T(8,128)(2,1)} %refs_1_.2), custom_call_target="tpu_custom_call" | custom-call | bytes 4194304 | tf_op jit(solution)/shard_map/pallas_call | solution.py:68
  16.3 49.2 %all-to-all-done.1.rest_0_ = bf16[32,128,512]{2,1,0:T(8,128)(2,1)} async-done(((bf16[32,128,512]{2,1,0:T(8,128)(2,1)}), bf16[32,128,512]{2,1,0:T(8,128)(2,1)}, u32[]{:S(2)}, u32[]{:S(2)}) %all-to-all-start.1) | async-done | bytes 4194336 | tf_op jit(solution)/shard_map/all_to_all | solution.py:84
  65.5 5.9 %all-to-all-start = ((bf16[32,128,256]{2,1,0:T(8,128)(2,1)}), bf16[32,128,256]{2,1,0:T(8,128)(2,1)S(1)}, u32[]{:S(2)}, u32[]{:S(2)}) async-start(bf16[32,128,256]{2,1,0:T(8,128)(2,1)} %bitcast.6), calls=%async_computation | async-start | bytes 4194304 | tf_op jit(solution)/shard_map/all_to_all | solution.py:84
  71.4 3.2 %slice.13 = bf16[16,128,512]{2,1,0:T(8,128)(2,1)} slice(bf16[32,128,512]{2,1,0:T(8,128)(2,1)} %all-to-all-done.1.rest_0_), slice={[16:32], [0:128], [0:512]} | slice | bytes 4194304 | tf_op jit(solution)/shard_map/slice | solution.py:339
  74.5 1.2 collective-permute-start
  75.7 0.1 constant_dynamic-slice_fusion
  75.8 0.1 copy.14
  75.9 0.1 pad_add_fusion
  76.0 0.6 slice_add_fusion
  76.6 24.0 %all-to-all-done.q_ref = bf16[32,128,256]{2,1,0:T(8,128)(2,1)S(1)} async-done(((bf16[32,128,256]{2,1,0:T(8,128)(2,1)}), bf16[32,128,256]{2,1,0:T(8,128)(2,1)S(1)}, u32[]{:S(2)}, u32[]{:S(2)}) %all-to-all-start) | async-done | bytes 2097184 | tf_op jit(solution)/shard_map/all_to_all | solution.py:84
  100.6 1.4 copy-done.3
  101.9 22.5 %shard_map.105 = (bf16[16,64,128]{2,1,0:T(8,128)(2,1)}, bf16[32,64,256]{2,1,0:T(8,128)(2,1)}, bf16[16,64,128]{2,1,0:T(8,128)(2,1)}, bf16[32,64,256]{2,1,0:T(8,128)(2,1)}) custom-call(s32[2,3]{1,0:T(2,128)} %get-tuple-element.27.slots_ref, bf16[32,128,256]{2,1,0:T(8,128)(2,1)} %copy-done.3, bf16[32,128,512]{2,1,0:T(8,128)(2,1)} %all-to-all-done.1.rest_0_), custom_call_target="tpu_custom_call" | custom-call | flops 12884901888 | bytes 8388608 | tf_op jit(solution)/shard_map/pallas_call | solution.py:241
  124.5 0.0 collective-permute-done.rest_1_
  124.5 12.8 %shard_map.106 = (bf16[16,64,128]{2,1,0:T(8,128)(2,1)}, bf16[32,64,256]{2,1,0:T(8,128)(2,1)}) custom-call(s32[2,3]{1,0:T(2,128)} %get-tuple-element.28.slots_ref, bf16[32,128,256]{2,1,0:T(8,128)(2,1)} %copy-done.3, bf16[32,128,512]{2,1,0:T(8,128)(2,1)} %all-to-all-done.1.rest_0_, ...), custom_call_target="tpu_custom_call", output_to_operand_aliasing={{1}: (4, {})} | custom-call | flops 6442450944 | bytes 8388608 | tf_op jit(solution)/shard_map/pallas_call | solution.py:241
  137.3 0.0 copy-start.4
  137.3 7.0 %all-to-all-start.2 = ((bf16[32,64,256]{2,1,0:T(8,128)(2,1)}), bf16[32,64,256]{2,1,0:T(8,128)(2,1)S(1)}, u32[]{:S(2)}, u32[]{:S(2)}) async-start(bf16[32,64,256]{2,1,0:T(8,128)(2,1)} %get-tuple-element.16), calls=%async_computation.2 | async-start | bytes 2097152 | tf_op jit(solution)/shard_map/all_to_all | solution.py:364
  144.4 1.5 collective-permute-start.1
  145.9 12.9 %shard_map.107 = (bf16[16,64,128]{2,1,0:T(8,128)(2,1)}, bf16[32,64,256]{2,1,0:T(8,128)(2,1)}) custom-call(s32[2,3]{1,0:T(2,128)} %get-tuple-element.28.slots_ref, bf16[32,128,256]{2,1,0:T(8,128)(2,1)} %copy-done.3, bf16[32,128,512]{2,1,0:T(8,128)(2,1)} %all-to-all-done.1.rest_0_, ...), custom_call_target="tpu_custom_call", output_to_operand_aliasing={{1}: (4, {})} | custom-call | flops 6442450944 | bytes 8388608 | tf_op jit(solution)/shard_map/pallas_call | solution.py:241
  158.9 4.6 %collective-permute-done.1.got_a = bf16[16,64,128]{2,1,0:T(8,128)(2,1)S(1)} collective-permute-done((bf16[16,64,128]{2,1,0:T(8,128)(2,1)S(1)}, bf16[16,64,128]{2,1,0:T(8,128)(2,1)S(1)}, u32[]{:S(2)}, u32[]{:S(2)}) %collective-permute-start.1) | collective-permute-done | bytes 262176 | tf_op jit(solution)/shard_map/ppermute | solution.py:359
  163.5 0.2 collective-permute-start.2
  163.7 6.8 %collective-permute-done.2.got_b = bf16[16,64,128]{2,1,0:T(8,128)(2,1)S(1)} collective-permute-done((bf16[16,64,128]{2,1,0:T(8,128)(2,1)S(1)}, bf16[16,64,128]{2,1,0:T(8,128)(2,1)S(1)}, u32[]{:S(2)}, u32[]{:S(2)}) %collective-permute-start.2) | collective-permute-done | bytes 262176 | tf_op jit(solution)/shard_map/ppermute | solution.py:359
  170.4 8.4 %all-to-all-start.3 = ((bf16[32,64,256]{2,1,0:T(8,128)(2,1)}), bf16[32,64,256]{2,1,0:T(8,128)(2,1)S(1)}, u32[]{:S(2)}, u32[]{:S(2)}) async-start(bf16[32,64,256]{2,1,0:T(8,128)(2,1)} %get-tuple-element.24), calls=%async_computation.3 | async-start | bytes 2097152 | tf_op jit(solution)/shard_map/all_to_all | solution.py:366
  178.9 9.7 %shard_map.109 = bf16[8,384,256]{2,1,0:T(8,128)(2,1)} custom-call(s32[1]{0:T(128)} %bitcast.4.side_ref, bf16[16,64,128]{2,1,0:T(8,128)(2,1)} %get-tuple-element.22.own_a, bf16[16,64,128]{2,1,0:T(8,128)(2,1)} %get-tuple-element.20.own_b, bf16[16,64,128]{2,1,0:T(8,128)(2,1)} %copy-done.7, bf16[16,64,128]{2,1,0:T(8,128)(2,1)} %copy-done.8, ...), custom_call_target="tpu_custom_call" | custom-call | flops 3221225472 | bytes 15728640 | tf_op jit(solution)/shard_map/pallas_call | solution.py:314
  188.6 7.5 %all-to-all-done.3 = bf16[32,64,256]{2,1,0:T(8,128)(2,1)S(1)} async-done(((bf16[32,64,256]{2,1,0:T(8,128)(2,1)}), bf16[32,64,256]{2,1,0:T(8,128)(2,1)S(1)}, u32[]{:S(2)}, u32[]{:S(2)}) %all-to-all-start.3) | async-done | bytes 1048608 | tf_op jit(solution)/shard_map/all_to_all | solution.py:366
  196.1 1.0 copy-done.2
  197.1 3.6 %all-to-all-start.4 = ((bf16[8,384,256]{2,1,0:T(8,128)(2,1)}), bf16[8,384,256]{2,1,0:T(8,128)(2,1)S(1)}, u32[]{:S(2)}, u32[]{:S(2)}) async-start(bf16[8,384,256]{2,1,0:T(8,128)(2,1)} %shard_map.109), calls=%async_computation.4 | async-start | bytes 3145728 | tf_op jit(solution)/shard_map/all_to_all | solution.py:367
  200.7 5.9 %shard_map.108 = (bf16[128,4096]{1,0:T(8,128)(2,1)}, bf16[128,4096]{1,0:T(8,128)(2,1)}) custom-call(bf16[2,16,64,256]{3,2,1,0:T(8,128)(2,1)} %bitcast.7, bf16[2,16,64,256]{3,2,1,0:T(8,128)(2,1)} %bitcast.8), custom_call_target="tpu_custom_call" | custom-call | bytes 4194304 | tf_op jit(solution)/shard_map/pallas_call | solution.py:99
  206.5 18.1 %all-to-all-done.4 = bf16[8,384,256]{2,1,0:T(8,128)(2,1)S(1)} async-done(((bf16[8,384,256]{2,1,0:T(8,128)(2,1)}), bf16[8,384,256]{2,1,0:T(8,128)(2,1)S(1)}, u32[]{:S(2)}, u32[]{:S(2)}) %all-to-all-start.4) | async-done | bytes 1572896 | tf_op jit(solution)/shard_map/all_to_all | solution.py:367
  224.6 1.0 convert_reduce_fusion
  (19 shorter events, 0.1 us)
Async XLA Ops:
  0.6 75.1 %copy-start = (s32[16,2]{0,1:T(2,128)S(1)}, s32[16,2]{0,1:T(2,128)}, u32[]{:S(2)}) copy-start(s32[16,2]{0,1:T(2,128)} %param.14) | copy-start | bytes 388
  4.1 61.4 %all-to-all-start.1 = ((bf16[32,128,512]{2,1,0:T(8,128)(2,1)}), bf16[32,128,512]{2,1,0:T(8,128)(2,1)}, u32[]{:S(2)}, u32[]{:S(2)}) async-start(bf16[32,128,512]{2,1,0:T(8,128)(2,1)} %bitcast.5), calls=%async_computation.1 | async-start | bytes 8388608 | tf_op jit(solution)/shard_map/all_to_all | solution.py:84
  65.5 35.1 %all-to-all-start = ((bf16[32,128,256]{2,1,0:T(8,128)(2,1)}), bf16[32,128,256]{2,1,0:T(8,128)(2,1)S(1)}, u32[]{:S(2)}, u32[]{:S(2)}) async-start(bf16[32,128,256]{2,1,0:T(8,128)(2,1)} %bitcast.6), calls=%async_computation | async-start | bytes 4194304 | tf_op jit(solution)/shard_map/all_to_all | solution.py:84
  74.5 49.9 %collective-permute-start = (bf16[16,128,512]{2,1,0:T(8,128)(2,1)}, bf16[16,128,512]{2,1,0:T(8,128)(2,1)}, u32[]{:S(2)}, u32[]{:S(2)}) collective-permute-start(bf16[16,128,512]{2,1,0:T(8,128)(2,1)} %slice.13), channel_id=1, source_target_pairs={{0,32},{32,64},{64,96},{96,0},{1,33},{33,65},{65,97},{97,1},{2,34}... | collective-permute-start | bytes 6291464 | tf_op jit(solution)/shard_map/ppermute | solution.py:339
  100.6 1.4 copy-start.3
  137.3 7.0 %copy-start.4 = (bf16[16,64,128]{2,1,0:T(8,128)(2,1)S(1)}, bf16[16,64,128]{2,1,0:T(8,128)(2,1)}, u32[]{:S(2)}) copy-start(bf16[16,64,128]{2,1,0:T(8,128)(2,1)} %get-tuple-element.21.late_a) | copy-start | bytes 786436
  137.3 7.0 %copy-start.6 = (bf16[16,64,128]{2,1,0:T(8,128)(2,1)S(1)}, bf16[16,64,128]{2,1,0:T(8,128)(2,1)}, u32[]{:S(2)}) copy-start(bf16[16,64,128]{2,1,0:T(8,128)(2,1)} %get-tuple-element.22.own_a) | copy-start | bytes 786436
  137.3 33.1 %all-to-all-start.2 = ((bf16[32,64,256]{2,1,0:T(8,128)(2,1)}), bf16[32,64,256]{2,1,0:T(8,128)(2,1)S(1)}, u32[]{:S(2)}, u32[]{:S(2)}) async-start(bf16[32,64,256]{2,1,0:T(8,128)(2,1)} %get-tuple-element.16), calls=%async_computation.2 | async-start | bytes 2097152 | tf_op jit(solution)/shard_map/all_to_all | solution.py:364
  144.4 19.1 %collective-permute-start.1 = (bf16[16,64,128]{2,1,0:T(8,128)(2,1)S(1)}, bf16[16,64,128]{2,1,0:T(8,128)(2,1)S(1)}, u32[]{:S(2)}, u32[]{:S(2)}) collective-permute-start(bf16[16,64,128]{2,1,0:T(8,128)(2,1)S(1)} %broadcast_select_fusion), channel_id=1, source_target_pairs={{0,16},{16,0},{1,17},{17,1},{2,18},{18,2},{3,19},{19,3},{4,20},{20... | collective-permute-start | bytes 786440 | tf_op jit(solution)/shard_map/ppermute | solution.py:359
  145.9 12.9 %copy-start.5 = (bf16[16,64,128]{2,1,0:T(8,128)(2,1)S(1)}, bf16[16,64,128]{2,1,0:T(8,128)(2,1)}, u32[]{:S(2)}) copy-start(bf16[16,64,128]{2,1,0:T(8,128)(2,1)} %get-tuple-element.19.late_b) | copy-start | bytes 786436
  163.5 15.4 %copy-start.7 = (bf16[16,64,128]{2,1,0:T(8,128)(2,1)}, bf16[16,64,128]{2,1,0:T(8,128)(2,1)S(1)}, u32[]{:S(2)}) copy-start(bf16[16,64,128]{2,1,0:T(8,128)(2,1)S(1)} %collective-permute-done.1.got_a) | copy-start | bytes 786436
  163.5 7.0 %collective-permute-start.2 = (bf16[16,64,128]{2,1,0:T(8,128)(2,1)S(1)}, bf16[16,64,128]{2,1,0:T(8,128)(2,1)S(1)}, u32[]{:S(2)}, u32[]{:S(2)}) collective-permute-start(bf16[16,64,128]{2,1,0:T(8,128)(2,1)S(1)} %broadcast_select_fusion.1), channel_id=1, source_target_pairs={{0,16},{16,0},{1,17},{17,1},{2,18},{18,2},{3,19},{19,3},{4,20},{20... | collective-permute-start | bytes 786440 | tf_op jit(solution)/shard_map/ppermute | solution.py:359
  170.4 8.4 %copy-start.8 = (bf16[16,64,128]{2,1,0:T(8,128)(2,1)}, bf16[16,64,128]{2,1,0:T(8,128)(2,1)S(1)}, u32[]{:S(2)}) copy-start(bf16[16,64,128]{2,1,0:T(8,128)(2,1)S(1)} %collective-permute-done.2.got_b) | copy-start | bytes 786436
  170.4 18.1 %copy-start.1 = (bf16[32,64,256]{2,1,0:T(8,128)(2,1)}, bf16[32,64,256]{2,1,0:T(8,128)(2,1)S(1)}, u32[]{:S(2)}) copy-start(bf16[32,64,256]{2,1,0:T(8,128)(2,1)S(1)} %all-to-all-done.2) | copy-start | bytes 3145732
  170.4 25.7 %all-to-all-start.3 = ((bf16[32,64,256]{2,1,0:T(8,128)(2,1)}), bf16[32,64,256]{2,1,0:T(8,128)(2,1)S(1)}, u32[]{:S(2)}, u32[]{:S(2)}) async-start(bf16[32,64,256]{2,1,0:T(8,128)(2,1)} %get-tuple-element.24), calls=%async_computation.3 | async-start | bytes 2097152 | tf_op jit(solution)/shard_map/all_to_all | solution.py:366
  196.1 1.0 copy-start.2
  197.1 27.5 %all-to-all-start.4 = ((bf16[8,384,256]{2,1,0:T(8,128)(2,1)}), bf16[8,384,256]{2,1,0:T(8,128)(2,1)S(1)}, u32[]{:S(2)}, u32[]{:S(2)}) async-start(bf16[8,384,256]{2,1,0:T(8,128)(2,1)} %shard_map.109), calls=%async_computation.4 | async-start | bytes 3145728 | tf_op jit(solution)/shard_map/all_to_all | solution.py:367

commit v4 on v3

--- a/solution.py
+++ b/solution.py
@@ -16,6 +16,7 @@
 SENDERS = 8
 BLOCK = SENDERS * HALF
 TILE = 256
+HOPS = (2, 1, 3, 0)
 LOG2E = 1.4426950408889634
 PLANE = ("zl", "zh", "y", "c")
 GROUP = ("zh", "y", "c")
@@ -60,12 +61,12 @@
         copy.wait()
 
 
-def to_heads(*arrays):
+def packed(*arrays):
     count = len(arrays)
     rows, width = arrays[0].shape[0], count * HDIM
     steps = 4
     anywhere = pl.BlockSpec(memory_space=pl.ANY)
-    sent = pl.pallas_call(
+    return pl.pallas_call(
         pack_kernel,
         out_shape=jax.ShapeDtypeStruct((2, 16, rows, width), bf16),
         in_specs=[anywhere] * count,
@@ -80,30 +81,32 @@
         cost_estimate=pl.CostEstimate(
             flops=0, transcendentals=0, bytes_accessed=4 * rows * HEADS * width
         ),
-    )(*arrays)
-    return lax.all_to_all(sent.reshape(32, rows, width), PLANE, 0, 0, tiled=True)
-
-
-def unpack_kernel(first_ref, second_ref, out_ref, tan_ref):
-    for half, ref in enumerate((first_ref, second_ref)):
-        rows = slice(half * HALF, (half + 1) * HALF)
-        for head in range(4):
-            lanes = slice(head * HDIM, (head + 1) * HDIM)
-            out_ref[rows, lanes] = ref[head % 2, head // 2, :, :HDIM]
-            tan_ref[rows, lanes] = ref[head % 2, head // 2, :, HDIM:]
-
-
-def unpack(first, second):
-    shape = jax.ShapeDtypeStruct((2 * HALF, HEADS * HDIM), bf16)
-    spec = pl.BlockSpec((2 * HALF, 4 * HDIM), lambda j: (0, j))
+    )(*arrays).reshape(32, rows, width)
+
+
+def to_heads(sent):
+    return lax.all_to_all(sent, PLANE, 0, 0, tiled=True)
+
+
+def unpack_kernel(ref, out_ref, tan_ref):
+    for head in range(8):
+        lanes = slice(head * HDIM, (head + 1) * HDIM)
+        out_ref[:, lanes] = ref[head % 2, head // 2, :, :HDIM]
+        tan_ref[:, lanes] = ref[head % 2, head // 2, :, HDIM:]
+
+
+def unpack(back):
+    rows = back.shape[1]
+    shape = jax.ShapeDtypeStruct((rows, HEADS * HDIM), bf16)
+    spec = pl.BlockSpec((rows, 8 * HDIM), lambda j: (0, j))
     return pl.pallas_call(
         unpack_kernel,
         out_shape=(shape, shape),
-        grid=(8,),
-        in_specs=[pl.BlockSpec((2, 2, HALF, 2 * HDIM), lambda j: (0, j, 0, 0))] * 2,
+        grid=(4,),
+        in_specs=[pl.BlockSpec((2, 4, rows, 2 * HDIM), lambda j: (0, j, 0, 0))],
         out_specs=(spec, spec),
         cost_estimate=pl.CostEstimate(flops=0, transcendentals=0, bytes_accessed=4 << 20),
-    )(first.reshape(2, 16, HALF, 2 * HDIM), second.reshape(2, 16, HALF, 2 * HDIM))
+    )(back.reshape(2, 16, rows, 2 * HDIM))
 
 
 def attend_kernel(slots_ref, q_ref, *rest, loads, sources, halves, first, first_half):
@@ -207,36 +210,25 @@
     result_tan = ((tan * scale + out[:, HDIM:]) * inverse).astype(bf16)
     result_tan = result_tan.reshape(SENDERS, HALF, HDIM)
 
-    def store(pair_ref, sent_ref):
-        pair_ref[...] = result
-        sent_ref[:, :, :HDIM] = result
-        sent_ref[:, :, HDIM:] = result_tan
-
-    if halves == 1:
-        store(*outs)
-    else:
-        pl.when(half == 0)(lambda: store(outs[0], outs[1]))
-        pl.when(half == 1)(lambda: store(outs[2], outs[3]))
+    pair_ref, sent_ref = outs
+    pair_ref[0] = result
+    sent_ref[:, :, :HDIM] = result
+    sent_ref[:, :, HDIM:] = result_tan
 
 
 def attend(slots, queries, kept, loads, late, first_half, halves, filled=None):
     first = 2 if late else 0
-    pair_shape = jax.ShapeDtypeStruct((16, HALF, HDIM), bf16)
-    sent_shape = jax.ShapeDtypeStruct((32, HALF, 2 * HDIM), bf16)
     in_specs = [pl.BlockSpec(memory_space=pl.ANY)] * (1 + len(kept) + (filled is not None))
-    out_shape, out_specs = [], []
-    for n in range(halves):
-
-        def place(h, c, n=n):
-            return c if halves == 1 else jnp.where(h == n, c, 1 - n)
-
-        out_shape += [pair_shape, sent_shape]
-        out_specs += [
-            pl.BlockSpec((SENDERS, HALF, HDIM), lambda h, c, s, p=place: (p(h, c), 0, 0)),
-            pl.BlockSpec(
-                (SENDERS, HALF, 2 * HDIM), lambda h, c, s, p=place: (first + p(h, c), 0, 0)
-            ),
-        ]
+    out_shape = (
+        jax.ShapeDtypeStruct((halves, 16, HALF, HDIM), bf16),
+        jax.ShapeDtypeStruct((32, 2 * HALF, 2 * HDIM), bf16),
+    )
+    out_specs = (
+        pl.BlockSpec((1, SENDERS, HALF, HDIM), lambda h, c, s: (h, c, 0, 0)),
+        pl.BlockSpec(
+            (SENDERS, HALF, 2 * HDIM), lambda h, c, s: (first + c, first_half + h, 0)
+        ),
+    )
     operands = (slots, queries, *kept) + (() if filled is None else (filled,))
     return pl.pallas_call(
         functools.partial(
@@ -274,99 +266,139 @@
     )(*operands)
 
 
-def grad_kernel(side_ref, own_a, own_b, got_a, got_b, late_a, late_b, cot_ref, out_ref, pair, sem):
-    @pl.when(pl.program_id(0) == 0)
-    def _():
-        def load(left, right):
-            copies = []
-            for column, halves in enumerate((left, right)):
-                for half, ref in enumerate(halves):
-                    copies.append(
-                        pltpu.make_async_copy(
-                            ref,
-                            pair.at[:, pl.ds(half * HALF, HALF), pl.ds(column * HDIM, HDIM)],
-                            sem.at[2 * column + half],
-                        )
+def turn_kernel(ref, out_ref):
+    out_ref[...] = ref[...].T
+
+
+def turned(cotangent):
+    rows, columns = cotangent.shape
+    return pl.pallas_call(
+        turn_kernel,
+        out_shape=jax.ShapeDtypeStruct((columns, rows), bf16),
+        grid=(8,),
+        in_specs=[pl.BlockSpec((rows, columns // 8), lambda j: (0, j))],
+        out_specs=pl.BlockSpec((columns // 8, rows), lambda j: (j, 0)),
+        compiler_params=pltpu.CompilerParams(vmem_limit_bytes=32 << 20),
+        cost_estimate=pl.CostEstimate(flops=0, transcendentals=0, bytes_accessed=24 << 20),
+    )(cotangent)
+
+
+def grad_kernel(place_ref, early_a, early_b, got_a, got_b, late, got_late, cot_ref, *rest):
+    outs, (pair, rows, parts, cut, sem, arrived, left) = rest[:8], rest[8:]
+    plane, side = place_ref[0], place_ref[1]
+    height = 2 * parts.shape[2]
+    reads = [
+        pltpu.make_async_copy(
+            cot_ref.at[pl.ds(pl.multiple_of((plane + dx) % 4 * height, height), height)],
+            rows.at[step],
+            arrived.at[step],
+        )
+        for step, dx in enumerate(HOPS)
+    ]
+
+    def load(left_halves, right_halves):
+        copies = []
+        for column, halves in enumerate((left_halves, right_halves)):
+            for half, ref in enumerate(halves):
+                copies.append(
+                    pltpu.make_async_copy(
+                        ref,
+                        pair.at[:, pl.ds(half * HALF, HALF), pl.ds(column * HDIM, HDIM)],
+                        sem.at[2 * column + half],
                     )
-            for copy in copies:
-                copy.start()
-            for copy in copies:
-                copy.wait()
-
-        early = (own_a, own_b)
-        far = (got_a, got_b)
-        late = (late_a, late_b)
-        pl.when(side_ref[0] == 0)(lambda: load(early, far))
-        pl.when(side_ref[0] == 1)(lambda: load(far, late))
-
-    part = lax.dot_general(
-        cot_ref[...],
-        pair[...].reshape(2 * CLIP, 2 * HDIM),
-        (((0,), (0,)), ((), ())),
-        preferred_element_type=f32,
-    )
-    out_ref[...] = part.astype(bf16).reshape(out_ref.shape)
-
-
-def grad_term(side, early, got, late, cotangent):
-    rows, columns = cotangent.shape
+                )
+        for copy in copies:
+            copy.start()
+        for copy in copies:
+            copy.wait()
+
+    for copy in reads:
+        copy.start()
+    halves = lambda ref: (ref.at[0], ref.at[1])
+    own = (early_a.at[0], early_b.at[0])
+    far = (got_a.at[0], got_b.at[0])
+    pl.when(side == 0)(lambda: load(own, far))
+    pl.when(side == 1)(lambda: load(halves(got_late), halves(late)))
+    writes = []
+    for step, copy in enumerate(reads):
+        copy.wait()
+        part = jnp.dot(
+            rows[step], pair[...].reshape(2 * CLIP, 2 * HDIM), preferred_element_type=f32
+        )
+        parts[step] = part.astype(bf16).reshape(2, height // 2, 2 * HDIM)
+        for dz in range(2):
+            n = 2 * step + dz
+            cut[n] = parts[step, side ^ dz]
+            writes.append(pltpu.make_async_copy(cut.at[n], outs[n], left.at[n]))
+            writes[-1].start()
+    for copy in writes:
+        copy.wait()
+
+
+def grad_terms(place, attended, cotangent):
+    columns, rows = cotangent.shape
     width = columns // 8
+    anywhere = pl.BlockSpec(memory_space=pl.ANY)
     return pl.pallas_call(
         grad_kernel,
-        out_shape=jax.ShapeDtypeStruct((8, width, 2 * HDIM), bf16),
+        out_shape=[jax.ShapeDtypeStruct((width, 2 * HDIM), bf16)] * 8,
         grid_spec=pltpu.PrefetchScalarGridSpec(
             num_scalar_prefetch=1,
-            grid=(2,),
-            in_specs=[pl.BlockSpec(memory_space=pl.ANY)] * 6
-            + [pl.BlockSpec((rows, 4 * width), lambda j, s: (0, j))],
-            out_specs=pl.BlockSpec((4, width, 2 * HDIM), lambda j, s: (j, 0, 0)),
+            grid=(),
+            in_specs=[anywhere] * 7,
+            out_specs=[anywhere] * 8,
             scratch_shapes=[
                 pltpu.VMEM((16, 2 * HALF, 2 * HDIM), bf16),
+                pltpu.VMEM((4, 2 * width, rows), bf16),
+                pltpu.VMEM((4, 2, width, 2 * HDIM), bf16),
+                pltpu.VMEM((8, width, 2 * HDIM), bf16),
                 pltpu.SemaphoreType.DMA((4,)),
+                pltpu.SemaphoreType.DMA((4,)),
+                pltpu.SemaphoreType.DMA((8,)),
             ],
         ),
         compiler_params=pltpu.CompilerParams(vmem_limit_bytes=60 << 20),
         cost_estimate=pl.CostEstimate(
             flops=2 * rows * columns * 2 * HDIM, transcendentals=0, bytes_accessed=15 << 20
         ),
-    )(side, *early, *got, *late, cotangent)
+    )(place, *attended, cotangent)
 
 
 def on_device(
     queries, key_rows, value_rows, query_tangent, key_tangent, value_tangent, partners, cotangent
 ):
-    own = to_heads(key_rows, key_tangent, value_rows, value_tangent)
+    own = to_heads(packed(key_rows, key_tangent, value_rows, value_tangent))
     halo = lax.ppermute(own[16:], "x", [(i, (i + 1) % 4) for i in range(4)])
-    query = to_heads(query_tangent, queries)
+    query, columns = lax.optimization_barrier((packed(query_tangent, queries), turned(cotangent)))
+    query = to_heads(query)
 
     plane = lax.axis_index("x") * 4
     mine = lax.dynamic_slice_in_dim(partners, plane, 4, 0)
     near = (mine - plane + 2) % 16
     slots = jnp.concatenate([jnp.arange(2, 6, dtype=jnp.int32)[:, None], near], axis=1)
-    late1, sent1, late2, sent2 = attend(
-        slots[2:] - 2, query, (own,), ((0, 0, 0, 4),), True, 0, 2
+    late, sent = attend(slots[2:] - 2, query, (own,), ((0, 0, 0, 4),), True, 0, 2)
+    window = ((1, 0, 0, 2), (0, 0, 2, 2))
+    early1, sent = attend(slots[:2], query, (own, halo), window, False, 0, 1, sent)
+    early2, sent = attend(slots[:2], query, (own, halo), window, False, 1, 1, sent)
+
+    got_late = lax.ppermute(late, "zl", [(0, 1)])
+    got1 = lax.ppermute(early1, "zl", [(1, 0)])
+    last, *_ = lax.optimization_barrier((early2, got_late, got1))
+    got2 = lax.ppermute(last, "zl", [(1, 0)])
+    sent, _ = lax.optimization_barrier((sent, got2))
+    back = lax.all_to_all(sent, PLANE, 0, 0, tiled=True)
+    place = jnp.stack([lax.axis_index("x"), lax.axis_index("zl")]).astype(jnp.int32)
+    terms = grad_terms(
+        place, (early1, early2, got1, got2, late, got_late), columns
     )
-    window = ((1, 0, 0, 2), (0, 0, 2, 2))
-    early1, sent1 = attend(slots[:2], query, (own, halo), window, False, 0, 1, sent1)
-    early2, sent2 = attend(slots[:2], query, (own, halo), window, False, 1, 1, sent2)
-
-    side = lax.axis_index("zl")
-
-    def swap(late, early, after=None):
-        sent = jnp.where(side == 0, late, early)
-        if after is not None:
-            sent, _ = lax.optimization_barrier((sent, after))
-        return lax.ppermute(sent, "zl", [(0, 1), (1, 0)])
-
-    got1 = swap(late1, early1)
-    got2 = swap(late2, early2, got1)
-    term = grad_term(side[None], (early1, early2), (got1, got2), (late1, late2), cotangent)
-    back1 = lax.all_to_all(sent1, PLANE, 0, 0, tiled=True)
-    sent2, _ = lax.optimization_barrier((sent2, got2))
-    back2 = lax.all_to_all(sent2, PLANE, 0, 0, tiled=True)
-    pieces = lax.all_to_all(term, CLIPS, 0, 0, tiled=True)
-    weight_grad = jnp.sum(pieces.astype(f32), axis=0)
-    attended, attended_tangent = unpack(back1, back2)
+    weight_grad = 0.0
+    for n, term in enumerate(terms):
+        dx, dz = HOPS[n // 2], n % 2
+        if (dx, dz) != (0, 0):
+            ring = [(2 * x + z, 2 * ((x + dx) % 4) + (z ^ dz)) for x in range(4) for z in range(2)]
+            term = lax.ppermute(term, CLIPS, ring)
+        weight_grad += term.astype(f32)
+    attended, attended_tangent = unpack(back)
     return attended, attended_tangent, weight_grad
 
 

time: 226 us -> 220 us (0.973)
  waiting for transfers between devices: 110 us -> 85.8 us
  Pallas kernels: 69.8 us -> 79.7 us
  local copies, waits for them, and re-layouts: 5.73 us -> 11.2 us
    all_to_all x5 -> x3, waiting for transfers between devices: 98.8 us -> 60.2 us  [the longest x2 60.2 us: to_heads(): return lax.all_to_all(sent, PLANE, 0, 0, tiled=True)]
    ppermute x2 -> x10, starting transfers between devices: 1.67 us -> 16.9 us  [the longest x7 11.7 us: on_device(): term = lax.ppermute(term, CLIPS, ring)]
    ppermute x2 -> x10, waiting for transfers between devices: 11.3 us -> 25.6 us  [the longest x7 17.5 us: on_device(): term = lax.ppermute(term, CLIPS, ring)]
    all_to_all x5 -> x3, starting transfers between devices: 34.6 us -> 20.9 us  [the longest x2 15.5 us: to_heads(): return lax.all_to_all(sent, PLANE, 0, 0, tiled=True)]
    pallas_call x4 -> x5, Pallas kernels: 21.5 us -> 32 us  [the longest x1 13.6 us: grad_terms(): pl.pallas_call(grad_kernel, out_shape=[jax.ShapeDtypeStruct((width, 2 * H...]
    unnamed x19 -> x15, local copies, waits for them, and re-layouts: 2.49 us -> 7.96 us
  transfers between devices with their start and end apart: 8 -> 14, of which waited for: 6 -> 8; matrix products, arithmetic and copies ran while one was open for 2% -> 3% of each run, Pallas kernels for 24% -> 33%
where the time goes in v4:
time: 220 us
  waiting for transfers between devices  85.8 us (39%)
  Pallas kernels  79.7 us (36%)
  starting transfers between devices  39 us (18%)
  local copies, waits for them, and re-layouts  11.2 us (5%)
  other arithmetic  3.2 us (1%)
    all_to_all x2, waiting for transfers between devices, to_heads(): return lax.all_to_all(sent, PLANE, 0, 0, tiled=True)  60.2 us
    pallas_call x3, Pallas kernels, attend(): pl.pallas_call(functools.partial(attend_kernel, loads=loads, sources=len(...  47.7 us
    ppermute x7, waiting for transfers between devices, on_device(): term = lax.ppermute(term, CLIPS, ring)  17.5 us
    all_to_all x2, starting transfers between devices, to_heads(): return lax.all_to_all(sent, PLANE, 0, 0, tiled=True)  15.5 us
    pallas_call x1, Pallas kernels, grad_terms(): pl.pallas_call(grad_kernel, out_shape=[jax.ShapeDtypeStruct((width, 2 * H...  13.6 us
    ppermute x7, starting transfers between devices, on_device(): term = lax.ppermute(term, CLIPS, ring)  11.7 us
    pallas_call x1, Pallas kernels, turned(): pl.pallas_call(turn_kernel, out_shape=jax.ShapeDtypeStruct((columns, rows...  8.43 us
    ppermute x1, waiting for transfers between devices, on_device(): got2 = lax.ppermute(last, 'zl', [(1, 0)])  8.07 us
  transfers between devices with their start and end apart: 14, of which 8 were waited for; matrix products, arithmetic and copies ran while one was open for 3% of the time, Pallas kernels for 33%

profile of v4, /device:TPU:1, one launch (start us, length us, event | category | flops | bytes accessed | tf_op | source)
XLA Modules:
  0.0 219.7 jit_solution(15141568888666177665)
XLA Ops:
  0.6 3.4 %shard_map.105 = bf16[2,16,128,512]{3,2,1,0:T(8,128)(2,1)} custom-call(bf16[128,4096]{1,0:T(8,128)(2,1)} %refs_0_.3, bf16[128,4096]{1,0:T(8,128)(2,1)} %refs_1_.3, bf16[128,4096]{1,0:T(8,128)(2,1)} %refs_2_.1, bf16[128,4096]{1,0:T(8,128)(2,1)} %refs_3_.1), custom_call_target="tpu_custom_call" | custom-call | bytes 8388608 | tf_op jit(solution)/shard_map/pallas_call | solution.py:69
  4.1 9.7 %all-to-all-start.1 = ((bf16[32,128,512]{2,1,0:T(8,128)(2,1)}), bf16[32,128,512]{2,1,0:T(8,128)(2,1)}, u32[]{:S(2)}, u32[]{:S(2)}) async-start(bf16[32,128,512]{2,1,0:T(8,128)(2,1)} %bitcast.5), calls=%async_computation.1 | async-start | bytes 8388608 | tf_op jit(solution)/shard_map/all_to_all | solution.py:88
  13.7 8.4 %shard_map.104.cot_ref = bf16[3072,2048]{1,0:T(8,128)(2,1)S(1)} custom-call(bf16[2048,3072]{1,0:T(8,128)(2,1)} %ref.1), custom_call_target="tpu_custom_call" | custom-call | bytes 25165824 | tf_op jit(solution)/shard_map/pallas_call | solution.py:275
  22.2 4.5 %copy-done.1 = bf16[3072,2048]{1,0:T(8,128)(2,1)} copy-done((bf16[3072,2048]{1,0:T(8,128)(2,1)}, bf16[3072,2048]{1,0:T(8,128)(2,1)S(1)}, u32[]{:S(2)}) %copy-start.1) | copy-done | bytes 12582936
  26.7 2.5 %shard_map.103 = bf16[2,16,128,256]{3,2,1,0:T(8,128)(2,1)} custom-call(bf16[128,4096]{1,0:T(8,128)(2,1)} %refs_0_.2, bf16[128,4096]{1,0:T(8,128)(2,1)} %refs_1_.2), custom_call_target="tpu_custom_call" | custom-call | bytes 4194304 | tf_op jit(solution)/shard_map/pallas_call | solution.py:69
  29.2 36.2 %all-to-all-done.1.rest_0_ = bf16[32,128,512]{2,1,0:T(8,128)(2,1)} async-done(((bf16[32,128,512]{2,1,0:T(8,128)(2,1)}), bf16[32,128,512]{2,1,0:T(8,128)(2,1)}, u32[]{:S(2)}, u32[]{:S(2)}) %all-to-all-start.1) | async-done | bytes 4194336 | tf_op jit(solution)/shard_map/all_to_all | solution.py:88
  65.4 5.9 %all-to-all-start = ((bf16[32,128,256]{2,1,0:T(8,128)(2,1)}), bf16[32,128,256]{2,1,0:T(8,128)(2,1)S(1)}, u32[]{:S(2)}, u32[]{:S(2)}) async-start(bf16[32,128,256]{2,1,0:T(8,128)(2,1)} %bitcast.7), calls=%async_computation | async-start | bytes 4194304 | tf_op jit(solution)/shard_map/all_to_all | solution.py:88
  71.3 3.1 %slice.13 = bf16[16,128,512]{2,1,0:T(8,128)(2,1)} slice(bf16[32,128,512]{2,1,0:T(8,128)(2,1)} %all-to-all-done.1.rest_0_), slice={[16:32], [0:128], [0:512]} | slice | bytes 4194304 | tf_op jit(solution)/shard_map/slice | solution.py:371
  74.4 1.2 collective-permute-start
  76.5 24.0 %all-to-all-done.q_ref = bf16[32,128,256]{2,1,0:T(8,128)(2,1)S(1)} async-done(((bf16[32,128,256]{2,1,0:T(8,128)(2,1)}), bf16[32,128,256]{2,1,0:T(8,128)(2,1)S(1)}, u32[]{:S(2)}, u32[]{:S(2)}) %all-to-all-start) | async-done | bytes 2097184 | tf_op jit(solution)/shard_map/all_to_all | solution.py:88
  100.5 1.3 copy-done.3
  101.8 22.1 %shard_map.106 = (bf16[2,16,64,128]{3,2,1,0:T(8,128)(2,1)}, bf16[32,128,256]{2,1,0:T(8,128)(2,1)}) custom-call(s32[2,3]{1,0:T(2,128)} %get-tuple-element.43.slots_ref, bf16[32,128,256]{2,1,0:T(8,128)(2,1)} %copy-done.3, bf16[32,128,512]{2,1,0:T(8,128)(2,1)} %all-to-all-done.1.rest_0_), custom_call_target="tpu_custom_call" | custom-call | flops 12884901888 | bytes 8388608 | tf_op jit(solution)/shard_map/pallas_call | solution.py:233
  123.9 2.6 %collective-permute-start.1 = (bf16[2,16,64,128]{3,2,1,0:T(8,128)(2,1)}, bf16[2,16,64,128]{3,2,1,0:T(8,128)(2,1)S(1)}, u32[]{:S(2)}, u32[]{:S(2)}) collective-permute-start(bf16[2,16,64,128]{3,2,1,0:T(8,128)(2,1)} %get-tuple-element.28.late), channel_id=1, source_target_pairs={{0,16},{1,17},{2,18},{3,19},{4,20},{5,21},{6,22},{7,23},{8,24},{9,... | collective-permute-start | bytes 1572872 | tf_op jit(solution)/shard_map/ppermute | solution.py:384
  126.5 12.8 %shard_map.107 = (bf16[1,16,64,128]{3,2,1,0:T(8,128)(2,1)}, bf16[32,128,256]{2,1,0:T(8,128)(2,1)}) custom-call(s32[2,3]{1,0:T(2,128)} %get-tuple-element.44.slots_ref, bf16[32,128,256]{2,1,0:T(8,128)(2,1)} %copy-done.3, bf16[32,128,512]{2,1,0:T(8,128)(2,1)} %all-to-all-done.1.rest_0_, ...), custom_call_target="tpu_custom_call", output_to_operand_aliasing={{1}: (4, {})} | custom-call | flops 6442450944 | bytes 8388608 | tf_op jit(solution)/shard_map/pallas_call | solution.py:233
  139.3 1.3 collective-permute-start.2
  140.6 12.8 %shard_map.108 = (bf16[1,16,64,128]{3,2,1,0:T(8,128)(2,1)}, bf16[32,128,256]{2,1,0:T(8,128)(2,1)}) custom-call(s32[2,3]{1,0:T(2,128)} %get-tuple-element.44.slots_ref, bf16[32,128,256]{2,1,0:T(8,128)(2,1)} %copy-done.3, bf16[32,128,512]{2,1,0:T(8,128)(2,1)} %all-to-all-done.1.rest_0_, ...), custom_call_target="tpu_custom_call", output_to_operand_aliasing={{1}: (4, {})} | custom-call | flops 6442450944 | bytes 8388608 | tf_op jit(solution)/shard_map/pallas_call | solution.py:233
  153.5 1.3 collective-permute-start.3
  154.8 8.1 %collective-permute-done.3.got_b = bf16[1,16,64,128]{3,2,1,0:T(8,128)(2,1)S(1)} collective-permute-done((bf16[1,16,64,128]{3,2,1,0:T(8,128)(2,1)}, bf16[1,16,64,128]{3,2,1,0:T(8,128)(2,1)S(1)}, u32[]{:S(2)}, u32[]{:S(2)}) %collective-permute-start.3) | collective-permute-done | bytes 262176 | tf_op jit(solution)/shard_map/ppermute | solution.py:387
  163.6 5.4 %all-to-all-start.2 = ((bf16[32,128,256]{2,1,0:T(8,128)(2,1)}), bf16[32,128,256]{2,1,0:T(8,128)(2,1)S(1)}, u32[]{:S(2)}, u32[]{:S(2)}) async-start(bf16[32,128,256]{2,1,0:T(8,128)(2,1)} %get-tuple-element.31), calls=%async_computation.2 | async-start | bytes 4194304 | tf_op jit(solution)/shard_map/all_to_all | solution.py:389
  169.7 13.6 %shard_map.110 = (bf16[384,256]{1,0:T(8,128)(2,1)}, bf16[384,256]{1,0:T(8,128)(2,1)}, bf16[384,256]{1,0:T(8,128)(2,1)}, bf16[384,256]{1,0:T(8,128)(2,1)}, bf16[3...) custom-call(s32[2]{0:T(128)} %pad_add_fusion.1.place_ref, ...), custom_call_target="tpu_custom_call" | custom-call | flops 3221225472 | bytes 15728640 | tf_op jit(solution)/shard_map/pallas_call | solution.py:342
  183.3 2.8 %collective-permute-start.4 = (bf16[384,256]{1,0:T(8,128)(2,1)}, bf16[384,256]{1,0:T(8,128)(2,1)S(1)}, u32[]{:S(2)}, u32[]{:S(2)}) collective-permute-start(bf16[384,256]{1,0:T(8,128)(2,1)} %get-tuple-element.35), channel_id=1, source_target_pairs={{0,64},{16,80},{32,96},{48,112},{64,0},{80,16},{96,32},{112,48},{1... | collective-permute-start | bytes 589832 | tf_op jit(solution)/shard_map/ppermute | solution.py:399
  186.1 1.3 collective-permute-start.5
  187.4 1.2 collective-permute-start.6
  189.6 1.5 collective-permute-start.8
  191.1 3.7 %collective-permute-start.9 = (bf16[384,256]{1,0:T(8,128)(2,1)}, bf16[384,256]{1,0:T(8,128)(2,1)S(1)}, u32[]{:S(2)}, u32[]{:S(2)}) collective-permute-start(bf16[384,256]{1,0:T(8,128)(2,1)} %get-tuple-element.40), channel_id=1, source_target_pairs={{0,112},{16,96},{32,16},{48,0},{64,48},{80,32},{96,80},{112,64},{1... | collective-permute-start | bytes 589832 | tf_op jit(solution)/shard_map/ppermute | solution.py:399
  194.8 2.9 %collective-permute-done.5 = bf16[384,256]{1,0:T(8,128)(2,1)S(1)} collective-permute-done((bf16[384,256]{1,0:T(8,128)(2,1)}, bf16[384,256]{1,0:T(8,128)(2,1)S(1)}, u32[]{:S(2)}, u32[]{:S(2)}) %collective-permute-start.5) | collective-permute-done | bytes 196640 | tf_op jit(solution)/shard_map/ppermute | solution.py:399
  197.8 2.5 %collective-permute-done.6 = bf16[384,256]{1,0:T(8,128)(2,1)S(1)} collective-permute-done((bf16[384,256]{1,0:T(8,128)(2,1)}, bf16[384,256]{1,0:T(8,128)(2,1)S(1)}, u32[]{:S(2)}, u32[]{:S(2)}) %collective-permute-start.6) | collective-permute-done | bytes 196640 | tf_op jit(solution)/shard_map/ppermute | solution.py:399
  200.3 7.8 %collective-permute-done.7 = bf16[384,256]{1,0:T(8,128)(2,1)S(1)} collective-permute-done((bf16[384,256]{1,0:T(8,128)(2,1)}, bf16[384,256]{1,0:T(8,128)(2,1)S(1)}, u32[]{:S(2)}, u32[]{:S(2)}) %collective-permute-start.7) | collective-permute-done | bytes 196640 | tf_op jit(solution)/shard_map/ppermute | solution.py:399
  208.6 3.9 %collective-permute-done.10 = bf16[384,256]{1,0:T(8,128)(2,1)S(1)} collective-permute-done((bf16[384,256]{1,0:T(8,128)(2,1)}, bf16[384,256]{1,0:T(8,128)(2,1)S(1)}, u32[]{:S(2)}, u32[]{:S(2)}) %collective-permute-start.10) | collective-permute-done | bytes 196640 | tf_op jit(solution)/shard_map/ppermute | solution.py:399
  212.5 1.9 convert_add_fusion
  214.3 1.3 copy-done.2
  215.7 4.0 %shard_map.109 = (bf16[128,4096]{1,0:T(8,128)(2,1)}, bf16[128,4096]{1,0:T(8,128)(2,1)}) custom-call(bf16[2,16,128,256]{3,2,1,0:T(8,128)(2,1)} %bitcast.6), custom_call_target="tpu_custom_call" | custom-call | bytes 4194304 | tf_op jit(solution)/shard_map/pallas_call | solution.py:102
  (27 shorter events, 3.9 us)
Async XLA Ops:
  0.6 75.0 %copy-start = (s32[16,2]{0,1:T(2,128)S(1)}, s32[16,2]{0,1:T(2,128)}, u32[]{:S(2)}) copy-start(s32[16,2]{0,1:T(2,128)} %param.14) | copy-start | bytes 388
  4.1 61.4 %all-to-all-start.1 = ((bf16[32,128,512]{2,1,0:T(8,128)(2,1)}), bf16[32,128,512]{2,1,0:T(8,128)(2,1)}, u32[]{:S(2)}, u32[]{:S(2)}) async-start(bf16[32,128,512]{2,1,0:T(8,128)(2,1)} %bitcast.5), calls=%async_computation.1 | async-start | bytes 8388608 | tf_op jit(solution)/shard_map/all_to_all | solution.py:88
  22.2 4.5 %copy-start.1 = (bf16[3072,2048]{1,0:T(8,128)(2,1)}, bf16[3072,2048]{1,0:T(8,128)(2,1)S(1)}, u32[]{:S(2)}) copy-start(bf16[3072,2048]{1,0:T(8,128)(2,1)S(1)} %shard_map.104.cot_ref) | copy-start | bytes 37748740
  65.4 35.1 %all-to-all-start = ((bf16[32,128,256]{2,1,0:T(8,128)(2,1)}), bf16[32,128,256]{2,1,0:T(8,128)(2,1)S(1)}, u32[]{:S(2)}, u32[]{:S(2)}) async-start(bf16[32,128,256]{2,1,0:T(8,128)(2,1)} %bitcast.7), calls=%async_computation | async-start | bytes 4194304 | tf_op jit(solution)/shard_map/all_to_all | solution.py:88
  74.4 52.1 %collective-permute-start = (bf16[16,128,512]{2,1,0:T(8,128)(2,1)}, bf16[16,128,512]{2,1,0:T(8,128)(2,1)}, u32[]{:S(2)}, u32[]{:S(2)}) collective-permute-start(bf16[16,128,512]{2,1,0:T(8,128)(2,1)} %slice.13), channel_id=1, source_target_pairs={{0,32},{32,64},{64,96},{96,0},{1,33},{33,65},{65,97},{97,1},{2,34}... | collective-permute-start | bytes 6291464 | tf_op jit(solution)/shard_map/ppermute | solution.py:371
  100.5 1.3 copy-start.3
  123.9 29.6 %collective-permute-start.1 = (bf16[2,16,64,128]{3,2,1,0:T(8,128)(2,1)}, bf16[2,16,64,128]{3,2,1,0:T(8,128)(2,1)S(1)}, u32[]{:S(2)}, u32[]{:S(2)}) collective-permute-start(bf16[2,16,64,128]{3,2,1,0:T(8,128)(2,1)} %get-tuple-element.28.late), channel_id=1, source_target_pairs={{0,16},{1,17},{2,18},{3,19},{4,20},{5,21},{6,22},{7,23},{8,24},{9,... | collective-permute-start | bytes 1572872 | tf_op jit(solution)/shard_map/ppermute | solution.py:384
  139.3 14.1 %collective-permute-start.2 = (bf16[1,16,64,128]{3,2,1,0:T(8,128)(2,1)}, bf16[1,16,64,128]{3,2,1,0:T(8,128)(2,1)S(1)}, u32[]{:S(2)}, u32[]{:S(2)}) collective-permute-start(bf16[1,16,64,128]{3,2,1,0:T(8,128)(2,1)} %get-tuple-element.29.early_a), channel_id=1, source_target_pairs={{16,0},{17,1},{18,2},{19,3},{20,4},{21,5},{22,6},{23,7},{24,8},{25... | collective-permute-start | bytes 786440 | tf_op jit(solution)/shard_map/ppermute | solution.py:385
  153.5 9.4 %copy-start.4 = (bf16[2,16,64,128]{3,2,1,0:T(8,128)(2,1)}, bf16[2,16,64,128]{3,2,1,0:T(8,128)(2,1)S(1)}, u32[]{:S(2)}) copy-start(bf16[2,16,64,128]{3,2,1,0:T(8,128)(2,1)S(1)} %collective-permute-done.1.got_late) | copy-start | bytes 1572868
  153.5 9.4 %copy-start.5 = (bf16[1,16,64,128]{3,2,1,0:T(8,128)(2,1)}, bf16[1,16,64,128]{3,2,1,0:T(8,128)(2,1)S(1)}, u32[]{:S(2)}) copy-start(bf16[1,16,64,128]{3,2,1,0:T(8,128)(2,1)S(1)} %collective-permute-done.2.got_a) | copy-start | bytes 786436
  153.5 9.4 %collective-permute-start.3 = (bf16[1,16,64,128]{3,2,1,0:T(8,128)(2,1)}, bf16[1,16,64,128]{3,2,1,0:T(8,128)(2,1)S(1)}, u32[]{:S(2)}, u32[]{:S(2)}) collective-permute-start(bf16[1,16,64,128]{3,2,1,0:T(8,128)(2,1)} %get-tuple-element.30.early_b), channel_id=1, source_target_pairs={{16,0},{17,1},{18,2},{19,3},{20,4},{21,5},{22,6},{23,7},{24,8},{25... | collective-permute-start | bytes 786440 | tf_op jit(solution)/shard_map/ppermute | solution.py:387
  162.9 0.7 copy-start.6
  163.6 50.7 %all-to-all-start.2 = ((bf16[32,128,256]{2,1,0:T(8,128)(2,1)}), bf16[32,128,256]{2,1,0:T(8,128)(2,1)S(1)}, u32[]{:S(2)}, u32[]{:S(2)}) async-start(bf16[32,128,256]{2,1,0:T(8,128)(2,1)} %get-tuple-element.31), calls=%async_computation.2 | async-start | bytes 4194304 | tf_op jit(solution)/shard_map/all_to_all | solution.py:389
  183.3 7.8 %collective-permute-start.4 = (bf16[384,256]{1,0:T(8,128)(2,1)}, bf16[384,256]{1,0:T(8,128)(2,1)S(1)}, u32[]{:S(2)}, u32[]{:S(2)}) collective-permute-start(bf16[384,256]{1,0:T(8,128)(2,1)} %get-tuple-element.35), channel_id=1, source_target_pairs={{0,64},{16,80},{32,96},{48,112},{64,0},{80,16},{96,32},{112,48},{1... | collective-permute-start | bytes 589832 | tf_op jit(solution)/shard_map/ppermute | solution.py:399
  186.1 11.6 %collective-permute-start.5 = (bf16[384,256]{1,0:T(8,128)(2,1)}, bf16[384,256]{1,0:T(8,128)(2,1)S(1)}, u32[]{:S(2)}, u32[]{:S(2)}) collective-permute-start(bf16[384,256]{1,0:T(8,128)(2,1)} %get-tuple-element.36), channel_id=1, source_target_pairs={{0,80},{16,64},{32,112},{48,96},{64,16},{80,0},{96,48},{112,32},{1... | collective-permute-start | bytes 589832 | tf_op jit(solution)/shard_map/ppermute | solution.py:399
  187.4 12.9 %collective-permute-start.6 = (bf16[384,256]{1,0:T(8,128)(2,1)}, bf16[384,256]{1,0:T(8,128)(2,1)S(1)}, u32[]{:S(2)}, u32[]{:S(2)}) collective-permute-start(bf16[384,256]{1,0:T(8,128)(2,1)} %get-tuple-element.37), channel_id=1, source_target_pairs={{0,32},{16,48},{32,64},{48,80},{64,96},{80,112},{96,0},{112,16},{1... | collective-permute-start | bytes 589832 | tf_op jit(solution)/shard_map/ppermute | solution.py:399
  188.6 19.4 %collective-permute-start.7 = (bf16[384,256]{1,0:T(8,128)(2,1)}, bf16[384,256]{1,0:T(8,128)(2,1)S(1)}, u32[]{:S(2)}, u32[]{:S(2)}) collective-permute-start(bf16[384,256]{1,0:T(8,128)(2,1)} %get-tuple-element.38), channel_id=1, source_target_pairs={{0,48},{16,32},{32,80},{48,64},{64,112},{80,96},{96,16},{112,0},{1... | collective-permute-start | bytes 589832 | tf_op jit(solution)/shard_map/ppermute | solution.py:399
  189.6 18.5 %collective-permute-start.8 = (bf16[384,256]{1,0:T(8,128)(2,1)}, bf16[384,256]{1,0:T(8,128)(2,1)S(1)}, u32[]{:S(2)}, u32[]{:S(2)}) collective-permute-start(bf16[384,256]{1,0:T(8,128)(2,1)} %get-tuple-element.39), channel_id=1, source_target_pairs={{0,96},{16,112},{32,0},{48,16},{64,32},{80,48},{96,64},{112,80},{1... | collective-permute-start | bytes 589832 | tf_op jit(solution)/shard_map/ppermute | solution.py:399
  191.1 17.5 %collective-permute-start.9 = (bf16[384,256]{1,0:T(8,128)(2,1)}, bf16[384,256]{1,0:T(8,128)(2,1)S(1)}, u32[]{:S(2)}, u32[]{:S(2)}) collective-permute-start(bf16[384,256]{1,0:T(8,128)(2,1)} %get-tuple-element.40), channel_id=1, source_target_pairs={{0,112},{16,96},{32,16},{48,0},{64,48},{80,32},{96,80},{112,64},{1... | collective-permute-start | bytes 589832 | tf_op jit(solution)/shard_map/ppermute | solution.py:399
  197.6 14.8 %collective-permute-start.10 = (bf16[384,256]{1,0:T(8,128)(2,1)}, bf16[384,256]{1,0:T(8,128)(2,1)S(1)}, u32[]{:S(2)}, u32[]{:S(2)}) collective-permute-start(bf16[384,256]{1,0:T(8,128)(2,1)} %get-tuple-element.42), channel_id=1, source_target_pairs={{0,16},{16,0},{32,48},{48,32},{64,80},{80,64},{96,112},{112,96},{1... | collective-permute-start | bytes 589832 | tf_op jit(solution)/shard_map/ppermute | solution.py:399
  214.3 1.3 copy-start.2

commit v5 on v4

--- a/solution.py
+++ b/solution.py
@@ -142,10 +142,12 @@
     @pl.when(start)
     def _():
         fetches = [fetch(step, at) for step, at in enumerate(blocks)]
-        for copy in copies(0) + fetches + copies(1):
+        for copy in copies(0) + fetches:
             copy.start()
         for copy in copies(0) + fetches:
             copy.wait()
+        for copy in copies(1):
+            copy.start()
 
     both = queries[2 * half + clip].reshape(BLOCK, 2 * HDIM)
     query = both[:, HDIM:]
@@ -256,7 +258,7 @@
         ),
         input_output_aliases={} if filled is None else {len(operands) - 1: 1},
         compiler_params=pltpu.CompilerParams(
-            dimension_semantics=("arbitrary", "arbitrary"), vmem_limit_bytes=60 << 20
+            dimension_semantics=("arbitrary", "arbitrary"), vmem_limit_bytes=28 << 20
         ),
         cost_estimate=pl.CostEstimate(
             flops=2 * 2 * halves * BLOCK * 3 * CLIP * HDIM * 8,
@@ -284,7 +286,7 @@
 
 
 def grad_kernel(place_ref, early_a, early_b, got_a, got_b, late, got_late, cot_ref, *rest):
-    outs, (pair, rows, parts, cut, sem, arrived, left) = rest[:8], rest[8:]
+    outs, (pair, rows, parts, sem, arrived, left) = rest[:8], rest[8:]
     plane, side = place_ref[0], place_ref[1]
     height = 2 * parts.shape[2]
     reads = [
@@ -295,6 +297,8 @@
         )
         for step, dx in enumerate(HOPS)
     ]
+    reads[0].start()
+    reads[1].start()
 
     def load(left_halves, right_halves):
         copies = []
@@ -312,8 +316,6 @@
         for copy in copies:
             copy.wait()
 
-    for copy in reads:
-        copy.start()
     halves = lambda ref: (ref.at[0], ref.at[1])
     own = (early_a.at[0], early_b.at[0])
     far = (got_a.at[0], got_b.at[0])
@@ -322,14 +324,17 @@
     writes = []
     for step, copy in enumerate(reads):
         copy.wait()
+        if step + 2 < len(reads):
+            reads[step + 2].start()
         part = jnp.dot(
             rows[step], pair[...].reshape(2 * CLIP, 2 * HDIM), preferred_element_type=f32
         )
         parts[step] = part.astype(bf16).reshape(2, height // 2, 2 * HDIM)
         for dz in range(2):
             n = 2 * step + dz
-            cut[n] = parts[step, side ^ dz]
-            writes.append(pltpu.make_async_copy(cut.at[n], outs[n], left.at[n]))
+            writes.append(
+                pltpu.make_async_copy(parts.at[step, side ^ dz], outs[n], left.at[n])
+            )
             writes[-1].start()
     for copy in writes:
         copy.wait()
@@ -351,13 +356,12 @@
                 pltpu.VMEM((16, 2 * HALF, 2 * HDIM), bf16),
                 pltpu.VMEM((4, 2 * width, rows), bf16),
                 pltpu.VMEM((4, 2, width, 2 * HDIM), bf16),
-                pltpu.VMEM((8, width, 2 * HDIM), bf16),
                 pltpu.SemaphoreType.DMA((4,)),
                 pltpu.SemaphoreType.DMA((4,)),
                 pltpu.SemaphoreType.DMA((8,)),
             ],
         ),
-        compiler_params=pltpu.CompilerParams(vmem_limit_bytes=60 << 20),
+        compiler_params=pltpu.CompilerParams(vmem_limit_bytes=56 << 20),
         cost_estimate=pl.CostEstimate(
             flops=2 * rows * columns * 2 * HDIM, transcendentals=0, bytes_accessed=15 << 20
         ),
@@ -391,15 +395,14 @@
     terms = grad_terms(
         place, (early1, early2, got1, got2, late, got_late), columns
     )
-    weight_grad = 0.0
+    arrived = []
     for n, term in enumerate(terms):
         dx, dz = HOPS[n // 2], n % 2
-        if (dx, dz) != (0, 0):
-            ring = [(2 * x + z, 2 * ((x + dx) % 4) + (z ^ dz)) for x in range(4) for z in range(2)]
-            term = lax.ppermute(term, CLIPS, ring)
-        weight_grad += term.astype(f32)
-    attended, attended_tangent = unpack(back)
-    return attended, attended_tangent, weight_grad
+        ring = [(2 * x + z, 2 * ((x + dx) % 4) + (z ^ dz)) for x in range(4) for z in range(2)]
+        arrived.append(term if (dx, dz) == (0, 0) else lax.ppermute(term, CLIPS, ring))
+    rows, arrived = lax.optimization_barrier((unpack(back), arrived))
+    weight_grad = sum(term.astype(f32) for term in arrived)
+    return *rows, weight_grad
 
 
 def solution(mesh):

time: 220 us -> 212 us (0.964)
  Pallas kernels: 79.7 us -> 73.9 us
    ppermute x7, waiting for transfers between devices: 17.5 us -> 10.8 us  [on_device(): lax.ppermute(term, CLIPS, ring)]
    all_to_all x1, waiting for transfers between devices: 0.01 us -> 4.32 us  [on_device(): back = lax.all_to_all(sent, PLANE, 0, 0, tiled=True)]
    pallas_call x3, Pallas kernels: 47.7 us -> 43.9 us  [attend(): pl.pallas_call(functools.partial(attend_kernel, loads=loads, sources=len(...]
    ppermute x7, starting transfers between devices: 11.7 us -> 9.32 us  [on_device(): lax.ppermute(term, CLIPS, ring)]
    unnamed x15 -> x23, local copies, waits for them, and re-layouts: 7.96 us -> 8 us
  transfers between devices with their start and end apart: 14 -> 14, of which waited for: 8 -> 8; matrix products, arithmetic and copies ran while one was open for 3% -> 2% of each run, Pallas kernels for 33% -> 33%
where the time goes in v5:
time: 212 us; the launch traced here: 211 us
  waiting for transfers between devices  83.8 us (40%)
  Pallas kernels  73.9 us (35%)
  starting transfers between devices  38.5 us (18%)
  local copies, waits for them, and re-layouts  11.2 us (5%)
  other arithmetic  2.62 us (1%)
    all_to_all x2, waiting for transfers between devices, to_heads(): return lax.all_to_all(sent, PLANE, 0, 0, tiled=True)  60.8 us
    pallas_call x3, Pallas kernels, attend(): pl.pallas_call(functools.partial(attend_kernel, loads=loads, sources=len(...  43.9 us
    all_to_all x2, starting transfers between devices, to_heads(): return lax.all_to_all(sent, PLANE, 0, 0, tiled=True)  15.5 us
    pallas_call x1, Pallas kernels, grad_terms(): pl.pallas_call(grad_kernel, out_shape=[jax.ShapeDtypeStruct((width, 2 * H...  11.7 us
    ppermute x7, waiting for transfers between devices, on_device(): lax.ppermute(term, CLIPS, ring)  10.8 us
    ppermute x7, starting transfers between devices, on_device(): lax.ppermute(term, CLIPS, ring)  9.32 us
    pallas_call x1, Pallas kernels, turned(): pl.pallas_call(turn_kernel, out_shape=jax.ShapeDtypeStruct((columns, rows...  8.43 us
    unnamed x23, local copies, waits for them, and re-layouts  8 us
  transfers between devices with their start and end apart: 14, of which 8 were waited for; matrix products, arithmetic and copies ran while one was open for 2% of the time, Pallas kernels for 33%

profile of v5, /device:TPU:1, one launch (start us, length us, event | category | flops | bytes accessed | tf_op | source)
XLA Modules:
  0.0 210.8 jit_solution(10523073546716068038)
XLA Ops:
  0.6 3.4 %shard_map.105 = bf16[2,16,128,512]{3,2,1,0:T(8,128)(2,1)} custom-call(bf16[128,4096]{1,0:T(8,128)(2,1)} %refs_0_.3, bf16[128,4096]{1,0:T(8,128)(2,1)} %refs_1_.3, bf16[128,4096]{1,0:T(8,128)(2,1)} %refs_2_.1, bf16[128,4096]{1,0:T(8,128)(2,1)} %refs_3_.1), custom_call_target="tpu_custom_call" | custom-call | bytes 8388608 | tf_op jit(solution)/shard_map/pallas_call | solution.py:69
  4.1 9.7 %all-to-all-start.1 = ((bf16[32,128,512]{2,1,0:T(8,128)(2,1)}), bf16[32,128,512]{2,1,0:T(8,128)(2,1)}, u32[]{:S(2)}, u32[]{:S(2)}) async-start(bf16[32,128,512]{2,1,0:T(8,128)(2,1)} %bitcast.5), calls=%async_computation.1 | async-start | bytes 8388608 | tf_op jit(solution)/shard_map/all_to_all | solution.py:88
  13.7 8.4 %shard_map.104.cot_ref = bf16[3072,2048]{1,0:T(8,128)(2,1)S(1)} custom-call(bf16[2048,3072]{1,0:T(8,128)(2,1)} %ref.1), custom_call_target="tpu_custom_call" | custom-call | bytes 25165824 | tf_op jit(solution)/shard_map/pallas_call | solution.py:277
  22.2 4.5 %copy-done.1 = bf16[3072,2048]{1,0:T(8,128)(2,1)} copy-done((bf16[3072,2048]{1,0:T(8,128)(2,1)}, bf16[3072,2048]{1,0:T(8,128)(2,1)S(1)}, u32[]{:S(2)}) %copy-start.1) | copy-done | bytes 12582936
  26.7 2.5 %shard_map.103 = bf16[2,16,128,256]{3,2,1,0:T(8,128)(2,1)} custom-call(bf16[128,4096]{1,0:T(8,128)(2,1)} %refs_0_.2, bf16[128,4096]{1,0:T(8,128)(2,1)} %refs_1_.2), custom_call_target="tpu_custom_call" | custom-call | bytes 4194304 | tf_op jit(solution)/shard_map/pallas_call | solution.py:69
  29.2 36.2 %all-to-all-done.1.rest_0_ = bf16[32,128,512]{2,1,0:T(8,128)(2,1)} async-done(((bf16[32,128,512]{2,1,0:T(8,128)(2,1)}), bf16[32,128,512]{2,1,0:T(8,128)(2,1)}, u32[]{:S(2)}, u32[]{:S(2)}) %all-to-all-start.1) | async-done | bytes 4194336 | tf_op jit(solution)/shard_map/all_to_all | solution.py:88
  65.4 5.9 %all-to-all-start = ((bf16[32,128,256]{2,1,0:T(8,128)(2,1)}), bf16[32,128,256]{2,1,0:T(8,128)(2,1)S(1)}, u32[]{:S(2)}, u32[]{:S(2)}) async-start(bf16[32,128,256]{2,1,0:T(8,128)(2,1)} %bitcast.7), calls=%async_computation | async-start | bytes 4194304 | tf_op jit(solution)/shard_map/all_to_all | solution.py:88
  71.3 3.1 %slice.13 = bf16[16,128,512]{2,1,0:T(8,128)(2,1)} slice(bf16[32,128,512]{2,1,0:T(8,128)(2,1)} %all-to-all-done.1.rest_0_), slice={[16:32], [0:128], [0:512]} | slice | bytes 4194304 | tf_op jit(solution)/shard_map/slice | solution.py:375
  74.4 1.2 collective-permute-start
  75.9 24.6 %all-to-all-done.q_ref = bf16[32,128,256]{2,1,0:T(8,128)(2,1)S(1)} async-done(((bf16[32,128,256]{2,1,0:T(8,128)(2,1)}), bf16[32,128,256]{2,1,0:T(8,128)(2,1)S(1)}, u32[]{:S(2)}, u32[]{:S(2)}) %all-to-all-start) | async-done | bytes 2097184 | tf_op jit(solution)/shard_map/all_to_all | solution.py:88
  100.5 20.9 %shard_map.106 = (bf16[2,16,64,128]{3,2,1,0:T(8,128)(2,1)S(1)}, bf16[32,128,256]{2,1,0:T(8,128)(2,1)S(1)}) custom-call(s32[2,3]{1,0:T(2,128)S(1)} %get-tuple-element.63.slots_ref, bf16[32,128,256]{2,1,0:T(8,128)(2,1)S(1)} %all-to-all-done.q_ref, bf16[32,128,512]{2,1,0:T(8,128)(2,1)} %all-to-all-done.1.rest_0_), custom_call_target="tpu_custom_call" | custom-call | flops 12884901888 | bytes 8388608 | tf_op jit(solution)/shard_map/pallas_call | solution.py:235
  121.4 2.6 %collective-permute-start.1 = (bf16[2,16,64,128]{3,2,1,0:T(8,128)(2,1)S(1)}, bf16[2,16,64,128]{3,2,1,0:T(8,128)(2,1)S(1)}, u32[]{:S(2)}, u32[]{:S(2)}) collective-permute-start(bf16[2,16,64,128]{3,2,1,0:T(8,128)(2,1)S(1)} %get-tuple-element.38.late), channel_id=1, source_target_pairs={{0,16},{1,17},{2,18},{3,19},{4,20},{5,21},{6,22},{7,23},{8,24},{9,... | collective-permute-start | bytes 1572872 | tf_op jit(solution)/shard_map/ppermute | solution.py:388
  124.1 11.5 %shard_map.107 = (bf16[1,16,64,128]{3,2,1,0:T(8,128)(2,1)S(1)}, bf16[32,128,256]{2,1,0:T(8,128)(2,1)S(1)}) custom-call(s32[2,3]{1,0:T(2,128)S(1)} %get-tuple-element.64.slots_ref, bf16[32,128,256]{2,1,0:T(8,128)(2,1)S(1)} %all-to-all-done.q_ref, bf16[32,128,512]{2,1,0:T(8,128)(2,1)} %all-to-all-done.1.rest_0_, ...), custom_call_target="tpu_custom_call", output_to_operand_aliasing={{1}: (4, {})} | custom-call | flops 6442450944 | bytes 8388608 | tf_op jit(solution)/shard_map/pallas_call | solution.py:235
  135.6 1.3 collective-permute-start.2
  136.9 11.5 %shard_map.108 = (bf16[1,16,64,128]{3,2,1,0:T(8,128)(2,1)S(1)}, bf16[32,128,256]{2,1,0:T(8,128)(2,1)S(1)}) custom-call(s32[2,3]{1,0:T(2,128)S(1)} %get-tuple-element.64.slots_ref, bf16[32,128,256]{2,1,0:T(8,128)(2,1)S(1)} %all-to-all-done.q_ref, bf16[32,128,512]{2,1,0:T(8,128)(2,1)} %all-to-all-done.1.rest_0_, ...), custom_call_target="tpu_custom_call", output_to_operand_aliasing={{1}: (4, {})} | custom-call | flops 6442450944 | bytes 8388608 | tf_op jit(solution)/shard_map/pallas_call | solution.py:235
  148.4 1.3 copy-done.2
  149.7 1.3 collective-permute-start.3
  151.0 7.9 %collective-permute-done.3.got_b = bf16[1,16,64,128]{3,2,1,0:T(8,128)(2,1)S(1)} collective-permute-done((bf16[1,16,64,128]{3,2,1,0:T(8,128)(2,1)S(1)}, bf16[1,16,64,128]{3,2,1,0:T(8,128)(2,1)S(1)}, u32[]{:S(2)}, u32[]{:S(2)}) %collective-permute-start.3) | collective-permute-done | bytes 262176 | tf_op jit(solution)/shard_map/ppermute | solution.py:391
  159.6 7.3 %all-to-all-start.2 = ((bf16[32,128,256]{2,1,0:T(8,128)(2,1)}), bf16[32,128,256]{2,1,0:T(8,128)(2,1)S(1)}, u32[]{:S(2)}, u32[]{:S(2)}) async-start(bf16[32,128,256]{2,1,0:T(8,128)(2,1)} %copy-done.2), calls=%async_computation.2 | async-start | bytes 4194304 | tf_op jit(solution)/shard_map/all_to_all | solution.py:393
  167.5 11.7 %shard_map.110 = (bf16[384,256]{1,0:T(8,128)(2,1)}, bf16[384,256]{1,0:T(8,128)(2,1)}, bf16[384,256]{1,0:T(8,128)(2,1)}, bf16[384,256]{1,0:T(8,128)(2,1)}, bf16[3...) custom-call(s32[2]{0:T(128)} %pad_add_fusion.1.place_ref, ...), custom_call_target="tpu_custom_call" | custom-call | flops 3221225472 | bytes 15728640 | tf_op jit(solution)/shard_map/pallas_call | solution.py:347
  179.2 1.6 collective-permute-start.4
  180.8 2.5 %collective-permute-start.5 = (bf16[384,256]{1,0:T(8,128)(2,1)}, bf16[384,256]{1,0:T(8,128)(2,1)S(1)}, u32[]{:S(2)}, u32[]{:S(2)}) collective-permute-start(bf16[384,256]{1,0:T(8,128)(2,1)} %get-tuple-element.46), channel_id=1, source_target_pairs={{0,80},{16,64},{32,112},{48,96},{64,16},{80,0},{96,48},{112,32},{1... | collective-permute-start | bytes 589832 | tf_op jit(solution)/shard_map/ppermute | solution.py:402
  183.4 1.0 collective-permute-start.7
  184.4 1.7 collective-permute-start.8
  186.0 1.0 collective-permute-done.4
  187.0 2.5 %collective-permute-start.9 = (bf16[384,256]{1,0:T(8,128)(2,1)}, bf16[384,256]{1,0:T(8,128)(2,1)S(1)}, u32[]{:S(2)}, u32[]{:S(2)}) collective-permute-start(bf16[384,256]{1,0:T(8,128)(2,1)} %get-tuple-element.50), channel_id=1, source_target_pairs={{0,112},{16,96},{32,16},{48,0},{64,48},{80,32},{96,80},{112,64},{1... | collective-permute-start | bytes 589832 | tf_op jit(solution)/shard_map/ppermute | solution.py:402
  189.5 4.3 %collective-permute-done.5 = bf16[384,256]{1,0:T(8,128)(2,1)S(1)} collective-permute-done((bf16[384,256]{1,0:T(8,128)(2,1)}, bf16[384,256]{1,0:T(8,128)(2,1)S(1)}, u32[]{:S(2)}, u32[]{:S(2)}) %collective-permute-start.5) | collective-permute-done | bytes 196640 | tf_op jit(solution)/shard_map/ppermute | solution.py:402
  193.8 4.3 %all-to-all-done.2 = bf16[32,128,256]{2,1,0:T(8,128)(2,1)S(1)} async-done(((bf16[32,128,256]{2,1,0:T(8,128)(2,1)}), bf16[32,128,256]{2,1,0:T(8,128)(2,1)S(1)}, u32[]{:S(2)}, u32[]{:S(2)}) %all-to-all-start.2) | async-done | bytes 2097184 | tf_op jit(solution)/shard_map/all_to_all | solution.py:393
  198.1 1.4 copy-done.6
  199.5 4.0 %shard_map.109 = (bf16[128,4096]{1,0:T(8,128)(2,1)}, bf16[128,4096]{1,0:T(8,128)(2,1)}) custom-call(bf16[2,16,128,256]{3,2,1,0:T(8,128)(2,1)} %bitcast.6), custom_call_target="tpu_custom_call" | custom-call | bytes 4194304 | tf_op jit(solution)/shard_map/pallas_call | solution.py:102
  204.2 4.7 %collective-permute-done.10 = bf16[384,256]{1,0:T(8,128)(2,1)} collective-permute-done((bf16[384,256]{1,0:T(8,128)(2,1)}, bf16[384,256]{1,0:T(8,128)(2,1)}, u32[]{:S(2)}, u32[]{:S(2)}) %collective-permute-start.10) | collective-permute-done | bytes 196640 | tf_op jit(solution)/shard_map/ppermute | solution.py:402
  208.9 1.9 convert_add_fusion
  (35 shorter events, 2.5 us)
Async XLA Ops:
  0.6 75.0 %copy-start = (s32[16,2]{0,1:T(2,128)S(1)}, s32[16,2]{0,1:T(2,128)}, u32[]{:S(2)}) copy-start(s32[16,2]{0,1:T(2,128)} %param.14) | copy-start | bytes 388
  4.1 61.4 %all-to-all-start.1 = ((bf16[32,128,512]{2,1,0:T(8,128)(2,1)}), bf16[32,128,512]{2,1,0:T(8,128)(2,1)}, u32[]{:S(2)}, u32[]{:S(2)}) async-start(bf16[32,128,512]{2,1,0:T(8,128)(2,1)} %bitcast.5), calls=%async_computation.1 | async-start | bytes 8388608 | tf_op jit(solution)/shard_map/all_to_all | solution.py:88
  22.2 4.5 %copy-start.1 = (bf16[3072,2048]{1,0:T(8,128)(2,1)}, bf16[3072,2048]{1,0:T(8,128)(2,1)S(1)}, u32[]{:S(2)}) copy-start(bf16[3072,2048]{1,0:T(8,128)(2,1)S(1)} %shard_map.104.cot_ref) | copy-start | bytes 37748740
  65.4 35.1 %all-to-all-start = ((bf16[32,128,256]{2,1,0:T(8,128)(2,1)}), bf16[32,128,256]{2,1,0:T(8,128)(2,1)S(1)}, u32[]{:S(2)}, u32[]{:S(2)}) async-start(bf16[32,128,256]{2,1,0:T(8,128)(2,1)} %bitcast.7), calls=%async_computation | async-start | bytes 4194304 | tf_op jit(solution)/shard_map/all_to_all | solution.py:88
  74.4 49.7 %collective-permute-start = (bf16[16,128,512]{2,1,0:T(8,128)(2,1)}, bf16[16,128,512]{2,1,0:T(8,128)(2,1)}, u32[]{:S(2)}, u32[]{:S(2)}) collective-permute-start(bf16[16,128,512]{2,1,0:T(8,128)(2,1)} %slice.13), channel_id=1, source_target_pairs={{0,32},{32,64},{64,96},{96,0},{1,33},{33,65},{65,97},{97,1},{2,34}... | collective-permute-start | bytes 6291464 | tf_op jit(solution)/shard_map/ppermute | solution.py:375
  121.4 14.1 %copy-start.3 = (bf16[2,16,64,128]{3,2,1,0:T(8,128)(2,1)}, bf16[2,16,64,128]{3,2,1,0:T(8,128)(2,1)S(1)}, u32[]{:S(2)}) copy-start(bf16[2,16,64,128]{3,2,1,0:T(8,128)(2,1)S(1)} %get-tuple-element.38.late) | copy-start | bytes 1572868
  121.4 28.3 %collective-permute-start.1 = (bf16[2,16,64,128]{3,2,1,0:T(8,128)(2,1)S(1)}, bf16[2,16,64,128]{3,2,1,0:T(8,128)(2,1)S(1)}, u32[]{:S(2)}, u32[]{:S(2)}) collective-permute-start(bf16[2,16,64,128]{3,2,1,0:T(8,128)(2,1)S(1)} %get-tuple-element.38.late), channel_id=1, source_target_pairs={{0,16},{1,17},{2,18},{3,19},{4,20},{5,21},{6,22},{7,23},{8,24},{9,... | collective-permute-start | bytes 1572872 | tf_op jit(solution)/shard_map/ppermute | solution.py:388
  135.6 12.8 %copy-start.4 = (bf16[1,16,64,128]{3,2,1,0:T(8,128)(2,1)}, bf16[1,16,64,128]{3,2,1,0:T(8,128)(2,1)S(1)}, u32[]{:S(2)}) copy-start(bf16[1,16,64,128]{3,2,1,0:T(8,128)(2,1)S(1)} %get-tuple-element.39.early_a) | copy-start | bytes 786436
  135.6 14.1 %collective-permute-start.2 = (bf16[1,16,64,128]{3,2,1,0:T(8,128)(2,1)S(1)}, bf16[1,16,64,128]{3,2,1,0:T(8,128)(2,1)S(1)}, u32[]{:S(2)}, u32[]{:S(2)}) collective-permute-start(bf16[1,16,64,128]{3,2,1,0:T(8,128)(2,1)S(1)} %get-tuple-element.39.early_a), channel_id=1, source_target_pairs={{16,0},{17,1},{18,2},{19,3},{20,4},{21,5},{22,6},{23,7},{24,8},{25... | collective-permute-start | bytes 786440 | tf_op jit(solution)/shard_map/ppermute | solution.py:389
  148.4 1.3 copy-start.2
  149.7 9.2 %copy-start.5 = (bf16[1,16,64,128]{3,2,1,0:T(8,128)(2,1)}, bf16[1,16,64,128]{3,2,1,0:T(8,128)(2,1)S(1)}, u32[]{:S(2)}) copy-start(bf16[1,16,64,128]{3,2,1,0:T(8,128)(2,1)S(1)} %get-tuple-element.40.early_b) | copy-start | bytes 786436
  149.7 9.2 %copy-start.7 = (bf16[2,16,64,128]{3,2,1,0:T(8,128)(2,1)}, bf16[2,16,64,128]{3,2,1,0:T(8,128)(2,1)S(1)}, u32[]{:S(2)}) copy-start(bf16[2,16,64,128]{3,2,1,0:T(8,128)(2,1)S(1)} %collective-permute-done.1.got_late) | copy-start | bytes 1572868
  149.7 9.2 %copy-start.8 = (bf16[1,16,64,128]{3,2,1,0:T(8,128)(2,1)}, bf16[1,16,64,128]{3,2,1,0:T(8,128)(2,1)S(1)}, u32[]{:S(2)}) copy-start(bf16[1,16,64,128]{3,2,1,0:T(8,128)(2,1)S(1)} %collective-permute-done.2.got_a) | copy-start | bytes 786436
  149.7 9.2 %collective-permute-start.3 = (bf16[1,16,64,128]{3,2,1,0:T(8,128)(2,1)S(1)}, bf16[1,16,64,128]{3,2,1,0:T(8,128)(2,1)S(1)}, u32[]{:S(2)}, u32[]{:S(2)}) collective-permute-start(bf16[1,16,64,128]{3,2,1,0:T(8,128)(2,1)S(1)} %get-tuple-element.40.early_b), channel_id=1, source_target_pairs={{16,0},{17,1},{18,2},{19,3},{20,4},{21,5},{22,6},{23,7},{24,8},{25... | collective-permute-start | bytes 786440 | tf_op jit(solution)/shard_map/ppermute | solution.py:391
  158.9 0.7 copy-start.9
  159.6 38.5 %all-to-all-start.2 = ((bf16[32,128,256]{2,1,0:T(8,128)(2,1)}), bf16[32,128,256]{2,1,0:T(8,128)(2,1)S(1)}, u32[]{:S(2)}, u32[]{:S(2)}) async-start(bf16[32,128,256]{2,1,0:T(8,128)(2,1)} %copy-done.2), calls=%async_computation.2 | async-start | bytes 4194304 | tf_op jit(solution)/shard_map/all_to_all | solution.py:393
  179.2 29.8 %copy-start.10 = (bf16[384,256]{1,0:T(8,128)(2,1)S(1)}, bf16[384,256]{1,0:T(8,128)(2,1)}, u32[]{:S(2)}) copy-start(bf16[384,256]{1,0:T(8,128)(2,1)} %get-tuple-element.61) | copy-start | bytes 589828
  179.2 7.8 %collective-permute-start.4 = (bf16[384,256]{1,0:T(8,128)(2,1)}, bf16[384,256]{1,0:T(8,128)(2,1)S(1)}, u32[]{:S(2)}, u32[]{:S(2)}) collective-permute-start(bf16[384,256]{1,0:T(8,128)(2,1)} %get-tuple-element.45), channel_id=1, source_target_pairs={{0,64},{16,80},{32,96},{48,112},{64,0},{80,16},{96,32},{112,48},{1... | collective-permute-start | bytes 589832 | tf_op jit(solution)/shard_map/ppermute | solution.py:402
  180.8 13.0 %collective-permute-start.5 = (bf16[384,256]{1,0:T(8,128)(2,1)}, bf16[384,256]{1,0:T(8,128)(2,1)S(1)}, u32[]{:S(2)}, u32[]{:S(2)}) collective-permute-start(bf16[384,256]{1,0:T(8,128)(2,1)} %get-tuple-element.46), channel_id=1, source_target_pairs={{0,80},{16,64},{32,112},{48,96},{64,16},{80,0},{96,48},{112,32},{1... | collective-permute-start | bytes 589832 | tf_op jit(solution)/shard_map/ppermute | solution.py:402
  183.4 20.1 %collective-permute-start.6 = (bf16[384,256]{1,0:T(8,128)(2,1)}, bf16[384,256]{1,0:T(8,128)(2,1)S(1)}, u32[]{:S(2)}, u32[]{:S(2)}) collective-permute-start(bf16[384,256]{1,0:T(8,128)(2,1)} %get-tuple-element.47), channel_id=1, source_target_pairs={{0,32},{16,48},{32,64},{48,80},{64,96},{80,112},{96,0},{112,16},{1... | collective-permute-start | bytes 589832 | tf_op jit(solution)/shard_map/ppermute | solution.py:402
  183.4 20.9 %collective-permute-start.7 = (bf16[384,256]{1,0:T(8,128)(2,1)}, bf16[384,256]{1,0:T(8,128)(2,1)S(1)}, u32[]{:S(2)}, u32[]{:S(2)}) collective-permute-start(bf16[384,256]{1,0:T(8,128)(2,1)} %get-tuple-element.48), channel_id=1, source_target_pairs={{0,48},{16,32},{32,80},{48,64},{64,112},{80,96},{96,16},{112,0},{1... | collective-permute-start | bytes 589832 | tf_op jit(solution)/shard_map/ppermute | solution.py:402
  184.4 19.9 %collective-permute-start.8 = (bf16[384,256]{1,0:T(8,128)(2,1)}, bf16[384,256]{1,0:T(8,128)(2,1)S(1)}, u32[]{:S(2)}, u32[]{:S(2)}) collective-permute-start(bf16[384,256]{1,0:T(8,128)(2,1)} %get-tuple-element.49), channel_id=1, source_target_pairs={{0,96},{16,112},{32,0},{48,16},{64,32},{80,48},{96,64},{112,80},{1... | collective-permute-start | bytes 589832 | tf_op jit(solution)/shard_map/ppermute | solution.py:402
  187.0 17.2 %collective-permute-start.9 = (bf16[384,256]{1,0:T(8,128)(2,1)}, bf16[384,256]{1,0:T(8,128)(2,1)S(1)}, u32[]{:S(2)}, u32[]{:S(2)}) collective-permute-start(bf16[384,256]{1,0:T(8,128)(2,1)} %get-tuple-element.50), channel_id=1, source_target_pairs={{0,112},{16,96},{32,16},{48,0},{64,48},{80,32},{96,80},{112,64},{1... | collective-permute-start | bytes 589832 | tf_op jit(solution)/shard_map/ppermute | solution.py:402
  193.8 15.2 %collective-permute-start.10 = (bf16[384,256]{1,0:T(8,128)(2,1)}, bf16[384,256]{1,0:T(8,128)(2,1)}, u32[]{:S(2)}, u32[]{:S(2)}) collective-permute-start(bf16[384,256]{1,0:T(8,128)(2,1)} %get-tuple-element.52), channel_id=1, source_target_pairs={{0,16},{16,0},{32,48},{48,32},{64,80},{80,64},{96,112},{112,96},{1... | collective-permute-start | bytes 589832 | tf_op jit(solution)/shard_map/ppermute | solution.py:402
  198.1 1.4 copy-start.6

commit v6 on v5

--- a/solution.py
+++ b/solution.py
@@ -88,11 +88,12 @@
     return lax.all_to_all(sent, PLANE, 0, 0, tiled=True)
 
 
-def unpack_kernel(ref, out_ref, tan_ref):
+def unpack_kernel(even_ref, odd_ref, out_ref, tan_ref):
     for head in range(8):
         lanes = slice(head * HDIM, (head + 1) * HDIM)
-        out_ref[:, lanes] = ref[head % 2, head // 2, :, :HDIM]
-        tan_ref[:, lanes] = ref[head % 2, head // 2, :, HDIM:]
+        ref = odd_ref if head % 2 else even_ref
+        out_ref[:, lanes] = ref[head // 2, :, :HDIM]
+        tan_ref[:, lanes] = ref[head // 2, :, HDIM:]
 
 
 def unpack(back):
@@ -103,10 +104,13 @@
         unpack_kernel,
         out_shape=(shape, shape),
         grid=(4,),
-        in_specs=[pl.BlockSpec((2, 4, rows, 2 * HDIM), lambda j: (0, j, 0, 0))],
+        in_specs=[
+            pl.BlockSpec((4, rows, 2 * HDIM), lambda j: (j, 0, 0)),
+            pl.BlockSpec((4, rows, 2 * HDIM), lambda j: (4 + j, 0, 0)),
+        ],
         out_specs=(spec, spec),
         cost_estimate=pl.CostEstimate(flops=0, transcendentals=0, bytes_accessed=4 << 20),
-    )(back.reshape(2, 16, rows, 2 * HDIM))
+    )(back, back)
 
 
 def attend_kernel(slots_ref, q_ref, *rest, loads, sources, halves, first, first_half):
@@ -285,10 +289,14 @@
     )(cotangent)
 
 
-def grad_kernel(place_ref, early_a, early_b, got_a, got_b, late, got_late, cot_ref, *rest):
-    outs, (pair, rows, parts, sem, arrived, left) = rest[:8], rest[8:]
+def grad_kernel(place_ref, early_a, early_b, late_a, late_b, cot_ref, *rest, both):
+    if both:
+        other, rest = rest[0], rest[1:]
+    outs, (tokens, rows, parts, sem, arrived, left) = rest[:-6], rest[-6:]
     plane, side = place_ref[0], place_ref[1]
     height = 2 * parts.shape[2]
+    first = slice(0, HDIM)
+    mine = slice(HDIM, 2 * HDIM) if both else first
     reads = [
         pltpu.make_async_copy(
             cot_ref.at[pl.ds(pl.multiple_of((plane + dx) % 4 * height, height), height)],
@@ -297,75 +305,82 @@
         )
         for step, dx in enumerate(HOPS)
     ]
-    reads[0].start()
-    reads[1].start()
-
-    def load(left_halves, right_halves):
-        copies = []
-        for column, halves in enumerate((left_halves, right_halves)):
-            for half, ref in enumerate(halves):
-                copies.append(
-                    pltpu.make_async_copy(
-                        ref,
-                        pair.at[:, pl.ds(half * HALF, HALF), pl.ds(column * HDIM, HDIM)],
-                        sem.at[2 * column + half],
-                    )
-                )
+
+    def load(halves):
+        copies = [
+            pltpu.make_async_copy(ref, tokens.at[:, pl.ds(n * HALF, HALF)], sem.at[n])
+            for n, ref in enumerate(halves)
+        ]
         for copy in copies:
             copy.start()
         for copy in copies:
             copy.wait()
 
-    halves = lambda ref: (ref.at[0], ref.at[1])
-    own = (early_a.at[0], early_b.at[0])
-    far = (got_a.at[0], got_b.at[0])
-    pl.when(side == 0)(lambda: load(own, far))
-    pl.when(side == 1)(lambda: load(halves(got_late), halves(late)))
+    reads[0].start()
+    reads[1].start()
+    pl.when(side == 0)(lambda: load((early_a.at[0], early_b.at[0])))
+    pl.when(side == 1)(lambda: load((late_a.at[0], late_b.at[1])))
+    if both:
+        fill = pltpu.make_async_copy(other, parts.at[:, :, :, pl.ds(0, HDIM)], sem.at[0])
+        fill.start()
     writes = []
     for step, copy in enumerate(reads):
         copy.wait()
         if step + 2 < len(reads):
             reads[step + 2].start()
         part = jnp.dot(
-            rows[step], pair[...].reshape(2 * CLIP, 2 * HDIM), preferred_element_type=f32
-        )
-        parts[step] = part.astype(bf16).reshape(2, height // 2, 2 * HDIM)
-        for dz in range(2):
-            n = 2 * step + dz
-            writes.append(
-                pltpu.make_async_copy(parts.at[step, side ^ dz], outs[n], left.at[n])
-            )
+            rows[step], tokens[...].reshape(2 * CLIP, HDIM), preferred_element_type=f32
+        )
+        parts[step, :, :, mine] = part.astype(bf16).reshape(2, height // 2, HDIM)
+        if both:
+            if step == 0:
+                fill.wait()
+            for dz in range(2):
+                n = 2 * step + dz
+                writes.append(
+                    pltpu.make_async_copy(parts.at[step, side ^ dz], outs[n], left.at[n])
+                )
+                writes[-1].start()
+        else:
+            writes.append(pltpu.make_async_copy(parts.at[step], outs[0].at[step], left.at[step]))
             writes[-1].start()
     for copy in writes:
         copy.wait()
 
 
-def grad_terms(place, attended, cotangent):
+def grad_terms(place, attended, cotangent, other=None):
     columns, rows = cotangent.shape
     width = columns // 8
     anywhere = pl.BlockSpec(memory_space=pl.ANY)
+    both = other is not None
+    held = (2 if both else 1) * HDIM
+    if both:
+        out_shape = [jax.ShapeDtypeStruct((width, held), bf16)] * 8
+    else:
+        out_shape = [jax.ShapeDtypeStruct((4, 2, width, held), bf16)]
+    operands = (*attended, cotangent) + ((other,) if both else ())
     return pl.pallas_call(
-        grad_kernel,
-        out_shape=[jax.ShapeDtypeStruct((width, 2 * HDIM), bf16)] * 8,
+        functools.partial(grad_kernel, both=both),
+        out_shape=out_shape,
         grid_spec=pltpu.PrefetchScalarGridSpec(
             num_scalar_prefetch=1,
             grid=(),
-            in_specs=[anywhere] * 7,
-            out_specs=[anywhere] * 8,
+            in_specs=[anywhere] * len(operands),
+            out_specs=[anywhere] * len(out_shape),
             scratch_shapes=[
-                pltpu.VMEM((16, 2 * HALF, 2 * HDIM), bf16),
+                pltpu.VMEM((16, 2 * HALF, HDIM), bf16),
                 pltpu.VMEM((4, 2 * width, rows), bf16),
-                pltpu.VMEM((4, 2, width, 2 * HDIM), bf16),
-                pltpu.SemaphoreType.DMA((4,)),
+                pltpu.VMEM((4, 2, width, held), bf16),
+                pltpu.SemaphoreType.DMA((2,)),
                 pltpu.SemaphoreType.DMA((4,)),
                 pltpu.SemaphoreType.DMA((8,)),
             ],
         ),
-        compiler_params=pltpu.CompilerParams(vmem_limit_bytes=56 << 20),
+        compiler_params=pltpu.CompilerParams(vmem_limit_bytes=50 << 20),
         cost_estimate=pl.CostEstimate(
             flops=2 * rows * columns * 2 * HDIM, transcendentals=0, bytes_accessed=15 << 20
         ),
-    )(place, *attended, cotangent)
+    )(place, *operands)
 
 
 def on_device(
@@ -389,20 +404,18 @@
     got1 = lax.ppermute(early1, "zl", [(1, 0)])
     last, *_ = lax.optimization_barrier((early2, got_late, got1))
     got2 = lax.ppermute(last, "zl", [(1, 0)])
-    sent, _ = lax.optimization_barrier((sent, got2))
+    place = jnp.stack([lax.axis_index("x"), lax.axis_index("zl")]).astype(jnp.int32)
+    first_columns = grad_terms(place, (early1, early2, got_late, got_late), columns)
+    sent, first_columns, _ = lax.optimization_barrier((sent, first_columns, got2))
     back = lax.all_to_all(sent, PLANE, 0, 0, tiled=True)
-    place = jnp.stack([lax.axis_index("x"), lax.axis_index("zl")]).astype(jnp.int32)
-    terms = grad_terms(
-        place, (early1, early2, got1, got2, late, got_late), columns
-    )
+    terms = grad_terms(place, (got1, got2, late, late), columns, *first_columns)
     arrived = []
     for n, term in enumerate(terms):
         dx, dz = HOPS[n // 2], n % 2
         ring = [(2 * x + z, 2 * ((x + dx) % 4) + (z ^ dz)) for x in range(4) for z in range(2)]
         arrived.append(term if (dx, dz) == (0, 0) else lax.ppermute(term, CLIPS, ring))
-    rows, arrived = lax.optimization_barrier((unpack(back), arrived))
     weight_grad = sum(term.astype(f32) for term in arrived)
-    return *rows, weight_grad
+    return *unpack(back), weight_grad
 
 
 def solution(mesh):

time: 212 us -> 217 us (1.024)
  Pallas kernels: 73.9 us -> 84.6 us
  waiting for transfers between devices: 83.8 us -> 81.3 us
    pallas_call x1 -> x2, Pallas kernels: 11.7 us -> 22.4 us  [grad_terms(): pl.pallas_call(functools.partial(grad_kernel, both=both), out_shape=out_s...]
    ppermute x7, waiting for transfers between devices: 10.8 us -> 20.6 us  [on_device(): lax.ppermute(term, CLIPS, ring)]
    ppermute x1, waiting for transfers between devices: 7.86 us -> 0.01 us  [on_device(): got2 = lax.ppermute(last, 'zl', [(1, 0)])]
    all_to_all x1, waiting for transfers between devices: 4.32 us -> 0.01 us  [on_device(): back = lax.all_to_all(sent, PLANE, 0, 0, tiled=True)]
    unnamed x23 -> x7, local copies, waits for them, and re-layouts: 8 us -> 5.92 us
  transfers between devices with their start and end apart: 14 -> 14, of which waited for: 8 -> 7; matrix products, arithmetic and copies ran while one was open for 2% -> 2% of each run, Pallas kernels for 33% -> 36%
where the time goes in v6:
time: 217 us; the launch traced here: 216 us
  Pallas kernels  84.6 us (39%)
  waiting for transfers between devices  81.3 us (37%)
  starting transfers between devices  39.5 us (18%)
  local copies, waits for them, and re-layouts  9.08 us (4%)
    all_to_all x2, waiting for transfers between devices, to_heads(): return lax.all_to_all(sent, PLANE, 0, 0, tiled=True)  60.8 us
    pallas_call x3, Pallas kernels, attend(): pl.pallas_call(functools.partial(attend_kernel, loads=loads, sources=len(...  43.9 us
    pallas_call x2, Pallas kernels, grad_terms(): pl.pallas_call(functools.partial(grad_kernel, both=both), out_shape=out_s...  22.4 us
    ppermute x7, waiting for transfers between devices, on_device(): lax.ppermute(term, CLIPS, ring)  20.6 us
    all_to_all x2, starting transfers between devices, to_heads(): return lax.all_to_all(sent, PLANE, 0, 0, tiled=True)  15.5 us
    ppermute x7, starting transfers between devices, on_device(): lax.ppermute(term, CLIPS, ring)  9.28 us
    pallas_call x1, Pallas kernels, turned(): pl.pallas_call(turn_kernel, out_shape=jax.ShapeDtypeStruct((columns, rows...  8.43 us
    all_to_all x1, starting transfers between devices, on_device(): back = lax.all_to_all(sent, PLANE, 0, 0, tiled=True)  8.24 us
  transfers between devices with their start and end apart: 14, of which 7 were waited for; matrix products, arithmetic and copies ran while one was open for 2% of the time, Pallas kernels for 36%

profile of v6, /device:TPU:1, one launch (start us, length us, event | category | flops | bytes accessed | tf_op | source)
XLA Modules:
  0.0 216.4 jit_solution(11731963395663606390)
XLA Ops:
  0.6 3.4 %shard_map.105 = bf16[2,16,128,512]{3,2,1,0:T(8,128)(2,1)} custom-call(bf16[128,4096]{1,0:T(8,128)(2,1)} %refs_0_.3, bf16[128,4096]{1,0:T(8,128)(2,1)} %refs_1_.3, bf16[128,4096]{1,0:T(8,128)(2,1)} %refs_2_.1, bf16[128,4096]{1,0:T(8,128)(2,1)} %refs_3_.1), custom_call_target="tpu_custom_call" | custom-call | bytes 8388608 | tf_op jit(solution)/shard_map/pallas_call | solution.py:69
  4.1 9.7 %all-to-all-start.1 = ((bf16[32,128,512]{2,1,0:T(8,128)(2,1)}), bf16[32,128,512]{2,1,0:T(8,128)(2,1)}, u32[]{:S(2)}, u32[]{:S(2)}) async-start(bf16[32,128,512]{2,1,0:T(8,128)(2,1)} %bitcast.4), calls=%async_computation.1 | async-start | bytes 8388608 | tf_op jit(solution)/shard_map/all_to_all | solution.py:88
  13.7 8.4 %shard_map.104.cot_ref = bf16[3072,2048]{1,0:T(8,128)(2,1)S(1)} custom-call(bf16[2048,3072]{1,0:T(8,128)(2,1)} %ref.1), custom_call_target="tpu_custom_call" | custom-call | bytes 25165824 | tf_op jit(solution)/shard_map/pallas_call | solution.py:281
  22.2 4.5 %copy-done.1 = bf16[3072,2048]{1,0:T(8,128)(2,1)} copy-done((bf16[3072,2048]{1,0:T(8,128)(2,1)}, bf16[3072,2048]{1,0:T(8,128)(2,1)S(1)}, u32[]{:S(2)}) %copy-start.1) | copy-done | bytes 12582936
  26.7 2.5 %shard_map.103 = bf16[2,16,128,256]{3,2,1,0:T(8,128)(2,1)} custom-call(bf16[128,4096]{1,0:T(8,128)(2,1)} %refs_0_.2, bf16[128,4096]{1,0:T(8,128)(2,1)} %refs_1_.2), custom_call_target="tpu_custom_call" | custom-call | bytes 4194304 | tf_op jit(solution)/shard_map/pallas_call | solution.py:69
  29.2 36.2 %all-to-all-done.1.rest_0_ = bf16[32,128,512]{2,1,0:T(8,128)(2,1)} async-done(((bf16[32,128,512]{2,1,0:T(8,128)(2,1)}), bf16[32,128,512]{2,1,0:T(8,128)(2,1)}, u32[]{:S(2)}, u32[]{:S(2)}) %all-to-all-start.1) | async-done | bytes 4194336 | tf_op jit(solution)/shard_map/all_to_all | solution.py:88
  65.4 5.9 %all-to-all-start = ((bf16[32,128,256]{2,1,0:T(8,128)(2,1)}), bf16[32,128,256]{2,1,0:T(8,128)(2,1)S(1)}, u32[]{:S(2)}, u32[]{:S(2)}) async-start(bf16[32,128,256]{2,1,0:T(8,128)(2,1)} %bitcast.5), calls=%async_computation | async-start | bytes 4194304 | tf_op jit(solution)/shard_map/all_to_all | solution.py:88
  71.3 3.1 %slice.13 = bf16[16,128,512]{2,1,0:T(8,128)(2,1)} slice(bf16[32,128,512]{2,1,0:T(8,128)(2,1)} %all-to-all-done.1.rest_0_), slice={[16:32], [0:128], [0:512]} | slice | bytes 4194304 | tf_op jit(solution)/shard_map/slice | solution.py:390
  74.4 1.2 collective-permute-start
  76.0 24.5 %all-to-all-done.q_ref = bf16[32,128,256]{2,1,0:T(8,128)(2,1)S(1)} async-done(((bf16[32,128,256]{2,1,0:T(8,128)(2,1)}), bf16[32,128,256]{2,1,0:T(8,128)(2,1)S(1)}, u32[]{:S(2)}, u32[]{:S(2)}) %all-to-all-start) | async-done | bytes 2097184 | tf_op jit(solution)/shard_map/all_to_all | solution.py:88
  100.5 20.9 %shard_map.106 = (bf16[2,16,64,128]{3,2,1,0:T(8,128)(2,1)S(1)}, bf16[32,128,256]{2,1,0:T(8,128)(2,1)S(1)}) custom-call(s32[2,3]{1,0:T(2,128)S(1)} %get-tuple-element.45.slots_ref, bf16[32,128,256]{2,1,0:T(8,128)(2,1)S(1)} %all-to-all-done.q_ref, bf16[32,128,512]{2,1,0:T(8,128)(2,1)} %all-to-all-done.1.rest_0_), custom_call_target="tpu_custom_call" | custom-call | flops 12884901888 | bytes 8388608 | tf_op jit(solution)/shard_map/pallas_call | solution.py:239
  121.4 2.6 %collective-permute-start.1 = (bf16[2,16,64,128]{3,2,1,0:T(8,128)(2,1)S(1)}, bf16[2,16,64,128]{3,2,1,0:T(8,128)(2,1)S(1)}, u32[]{:S(2)}, u32[]{:S(2)}) collective-permute-start(bf16[2,16,64,128]{3,2,1,0:T(8,128)(2,1)S(1)} %get-tuple-element.30.late_a.late_b), channel_id=1, source_target_pairs={{0,16},{1,17},{2,18},{3,19},{4,20},{5,21},{6,22},{7,23},{8,24},{9,... | collective-permute-start | bytes 1572872 | tf_op jit(solution)/shard_map/ppermute | solution.py:403
  124.1 11.5 %shard_map.107 = (bf16[1,16,64,128]{3,2,1,0:T(8,128)(2,1)S(1)}, bf16[32,128,256]{2,1,0:T(8,128)(2,1)S(1)}) custom-call(s32[2,3]{1,0:T(2,128)S(1)} %get-tuple-element.46.slots_ref, bf16[32,128,256]{2,1,0:T(8,128)(2,1)S(1)} %all-to-all-done.q_ref, bf16[32,128,512]{2,1,0:T(8,128)(2,1)} %all-to-all-done.1.rest_0_, ...), custom_call_target="tpu_custom_call", output_to_operand_aliasing={{1}: (4, {})} | custom-call | flops 6442450944 | bytes 8388608 | tf_op jit(solution)/shard_map/pallas_call | solution.py:239
  135.6 1.3 collective-permute-start.2
  136.9 11.5 %shard_map.108 = (bf16[1,16,64,128]{3,2,1,0:T(8,128)(2,1)S(1)}, bf16[32,128,256]{2,1,0:T(8,128)(2,1)S(1)}) custom-call(s32[2,3]{1,0:T(2,128)S(1)} %get-tuple-element.46.slots_ref, bf16[32,128,256]{2,1,0:T(8,128)(2,1)S(1)} %all-to-all-done.q_ref, bf16[32,128,512]{2,1,0:T(8,128)(2,1)} %all-to-all-done.1.rest_0_, ...), custom_call_target="tpu_custom_call", output_to_operand_aliasing={{1}: (4, {})} | custom-call | flops 6442450944 | bytes 8388608 | tf_op jit(solution)/shard_map/pallas_call | solution.py:239
  148.4 1.3 copy-done.2
  149.7 1.3 collective-permute-start.3
  151.0 10.6 %shard_map.109.rest_0_ = bf16[4,2,384,128]{3,2,1,0:T(8,128)(2,1)S(1)} custom-call(s32[2]{0:T(128)S(1)} %pad_add_fusion.1.place_ref, bf16[1,16,64,128]{3,2,1,0:T(8,128)(2,1)S(1)} %get-tuple-element.28.early_a, bf16[1,16,64,128]{3,2,1,0:T(8,128)(2,1)S(1)} %get-tuple-element.32.early_b, bf16[2,16,64,128]{3,2,1,0:T(8,128)(2,1)S(1)} %collective-permute-done.1.late_a.late_b, ...), custom_call_target="tpu_custom_call" | custom-call | flops 3221225472 | bytes 15728640 | tf_op jit(solution)/shard_map/pallas_call | solution.py:362
  161.6 8.2 %all-to-all-start.2 = ((bf16[32,128,256]{2,1,0:T(8,128)(2,1)}), bf16[32,128,256]{2,1,0:T(8,128)(2,1)}, u32[]{:S(2)}, u32[]{:S(2)}) async-start(bf16[32,128,256]{2,1,0:T(8,128)(2,1)} %copy-done.2), calls=%async_computation.2 | async-start | bytes 4194304 | tf_op jit(solution)/shard_map/all_to_all | solution.py:410
  169.9 11.7 %shard_map.111 = (bf16[384,256]{1,0:T(8,128)(2,1)S(1)}, bf16[384,256]{1,0:T(8,128)(2,1)S(1)}, bf16[384,256]{1,0:T(8,128)(2,1)S(1)}, bf16[384,256]{1,0:T(8,128)(2...) custom-call(s32[2]{0:T(128)S(1)} %pad_add_fusion.1.place_ref, ...), custom_call_target="tpu_custom_call" | custom-call | flops 3221225472 | bytes 15728640 | tf_op jit(solution)/shard_map/pallas_call | solution.py:362
  181.6 1.6 collective-permute-start.4
  183.2 2.5 %collective-permute-start.5 = (bf16[384,256]{1,0:T(8,128)(2,1)S(1)}, bf16[384,256]{1,0:T(8,128)(2,1)S(1)}, u32[]{:S(2)}, u32[]{:S(2)}) collective-permute-start(bf16[384,256]{1,0:T(8,128)(2,1)S(1)} %get-tuple-element.38), channel_id=1, source_target_pairs={{0,80},{16,64},{32,112},{48,96},{64,16},{80,0},{96,48},{112,32},{1... | collective-permute-start | bytes 589832 | tf_op jit(solution)/shard_map/ppermute | solution.py:416
  185.8 1.0 collective-permute-start.7
  186.8 1.7 collective-permute-start.8
  188.4 1.0 collective-permute-done.4
  189.5 2.2 %collective-permute-start.9 = (bf16[384,256]{1,0:T(8,128)(2,1)S(1)}, bf16[384,256]{1,0:T(8,128)(2,1)S(1)}, u32[]{:S(2)}, u32[]{:S(2)}) collective-permute-start(bf16[384,256]{1,0:T(8,128)(2,1)S(1)} %get-tuple-element.42), channel_id=1, source_target_pairs={{0,112},{16,96},{32,16},{48,0},{64,48},{80,32},{96,80},{112,64},{1... | collective-permute-start | bytes 589832 | tf_op jit(solution)/shard_map/ppermute | solution.py:416
  191.7 4.7 %collective-permute-done.5 = bf16[384,256]{1,0:T(8,128)(2,1)S(1)} collective-permute-done((bf16[384,256]{1,0:T(8,128)(2,1)S(1)}, bf16[384,256]{1,0:T(8,128)(2,1)S(1)}, u32[]{:S(2)}, u32[]{:S(2)}) %collective-permute-start.5) | collective-permute-done | bytes 196640 | tf_op jit(solution)/shard_map/ppermute | solution.py:416
  196.6 1.8 collective-permute-done.6
  198.4 8.0 %collective-permute-done.7 = bf16[384,256]{1,0:T(8,128)(2,1)S(1)} collective-permute-done((bf16[384,256]{1,0:T(8,128)(2,1)S(1)}, bf16[384,256]{1,0:T(8,128)(2,1)S(1)}, u32[]{:S(2)}, u32[]{:S(2)}) %collective-permute-start.7) | collective-permute-done | bytes 196640 | tf_op jit(solution)/shard_map/ppermute | solution.py:416
  206.5 5.0 %collective-permute-done.10 = bf16[384,256]{1,0:T(8,128)(2,1)S(1)} collective-permute-done((bf16[384,256]{1,0:T(8,128)(2,1)S(1)}, bf16[384,256]{1,0:T(8,128)(2,1)S(1)}, u32[]{:S(2)}, u32[]{:S(2)}) %collective-permute-start.10) | collective-permute-done | bytes 196640 | tf_op jit(solution)/shard_map/ppermute | solution.py:416
  211.5 0.9 convert_add_fusion
  212.4 4.0 %shard_map.110 = (bf16[128,4096]{1,0:T(8,128)(2,1)}, bf16[128,4096]{1,0:T(8,128)(2,1)}) custom-call(bf16[32,128,256]{2,1,0:T(8,128)(2,1)} %all-to-all-done.2.even_ref.odd_ref, bf16[32,128,256]{2,1,0:T(8,128)(2,1)} %all-to-all-done.2.even_ref.odd_ref), custom_call_target="tpu_custom_call" | custom-call | bytes 4194304 | tf_op jit(solution)/shard_map/pallas_call | solution.py:103
  (20 shorter events, 0.6 us)
Async XLA Ops:
  0.6 75.0 %copy-start = (s32[16,2]{0,1:T(2,128)S(1)}, s32[16,2]{0,1:T(2,128)}, u32[]{:S(2)}) copy-start(s32[16,2]{0,1:T(2,128)} %param.14) | copy-start | bytes 388
  4.1 61.4 %all-to-all-start.1 = ((bf16[32,128,512]{2,1,0:T(8,128)(2,1)}), bf16[32,128,512]{2,1,0:T(8,128)(2,1)}, u32[]{:S(2)}, u32[]{:S(2)}) async-start(bf16[32,128,512]{2,1,0:T(8,128)(2,1)} %bitcast.4), calls=%async_computation.1 | async-start | bytes 8388608 | tf_op jit(solution)/shard_map/all_to_all | solution.py:88
  22.2 4.5 %copy-start.1 = (bf16[3072,2048]{1,0:T(8,128)(2,1)}, bf16[3072,2048]{1,0:T(8,128)(2,1)S(1)}, u32[]{:S(2)}) copy-start(bf16[3072,2048]{1,0:T(8,128)(2,1)S(1)} %shard_map.104.cot_ref) | copy-start | bytes 37748740
  65.4 35.1 %all-to-all-start = ((bf16[32,128,256]{2,1,0:T(8,128)(2,1)}), bf16[32,128,256]{2,1,0:T(8,128)(2,1)S(1)}, u32[]{:S(2)}, u32[]{:S(2)}) async-start(bf16[32,128,256]{2,1,0:T(8,128)(2,1)} %bitcast.5), calls=%async_computation | async-start | bytes 4194304 | tf_op jit(solution)/shard_map/all_to_all | solution.py:88
  74.4 49.7 %collective-permute-start = (bf16[16,128,512]{2,1,0:T(8,128)(2,1)}, bf16[16,128,512]{2,1,0:T(8,128)(2,1)}, u32[]{:S(2)}, u32[]{:S(2)}) collective-permute-start(bf16[16,128,512]{2,1,0:T(8,128)(2,1)} %slice.13), channel_id=1, source_target_pairs={{0,32},{32,64},{64,96},{96,0},{1,33},{33,65},{65,97},{97,1},{2,34}... | collective-permute-start | bytes 6291464 | tf_op jit(solution)/shard_map/ppermute | solution.py:390
  121.4 28.2 %collective-permute-start.1 = (bf16[2,16,64,128]{3,2,1,0:T(8,128)(2,1)S(1)}, bf16[2,16,64,128]{3,2,1,0:T(8,128)(2,1)S(1)}, u32[]{:S(2)}, u32[]{:S(2)}) collective-permute-start(bf16[2,16,64,128]{3,2,1,0:T(8,128)(2,1)S(1)} %get-tuple-element.30.late_a.late_b), channel_id=1, source_target_pairs={{0,16},{1,17},{2,18},{3,19},{4,20},{5,21},{6,22},{7,23},{8,24},{9,... | collective-permute-start | bytes 1572872 | tf_op jit(solution)/shard_map/ppermute | solution.py:403
  135.6 14.1 %collective-permute-start.2 = (bf16[1,16,64,128]{3,2,1,0:T(8,128)(2,1)S(1)}, bf16[1,16,64,128]{3,2,1,0:T(8,128)(2,1)S(1)}, u32[]{:S(2)}, u32[]{:S(2)}) collective-permute-start(bf16[1,16,64,128]{3,2,1,0:T(8,128)(2,1)S(1)} %get-tuple-element.28.early_a), channel_id=1, source_target_pairs={{16,0},{17,1},{18,2},{19,3},{20,4},{21,5},{22,6},{23,7},{24,8},{25... | collective-permute-start | bytes 786440 | tf_op jit(solution)/shard_map/ppermute | solution.py:404
  148.4 1.3 copy-start.2
  149.7 11.9 %collective-permute-start.3 = (bf16[1,16,64,128]{3,2,1,0:T(8,128)(2,1)S(1)}, bf16[1,16,64,128]{3,2,1,0:T(8,128)(2,1)S(1)}, u32[]{:S(2)}, u32[]{:S(2)}) collective-permute-start(bf16[1,16,64,128]{3,2,1,0:T(8,128)(2,1)S(1)} %get-tuple-element.32.early_b), channel_id=1, source_target_pairs={{16,0},{17,1},{18,2},{19,3},{20,4},{21,5},{22,6},{23,7},{24,8},{25... | collective-permute-start | bytes 786440 | tf_op jit(solution)/shard_map/ppermute | solution.py:406
  161.6 50.8 %all-to-all-start.2 = ((bf16[32,128,256]{2,1,0:T(8,128)(2,1)}), bf16[32,128,256]{2,1,0:T(8,128)(2,1)}, u32[]{:S(2)}, u32[]{:S(2)}) async-start(bf16[32,128,256]{2,1,0:T(8,128)(2,1)} %copy-done.2), calls=%async_computation.2 | async-start | bytes 4194304 | tf_op jit(solution)/shard_map/all_to_all | solution.py:410
  181.6 7.9 %collective-permute-start.4 = (bf16[384,256]{1,0:T(8,128)(2,1)S(1)}, bf16[384,256]{1,0:T(8,128)(2,1)S(1)}, u32[]{:S(2)}, u32[]{:S(2)}) collective-permute-start(bf16[384,256]{1,0:T(8,128)(2,1)S(1)} %get-tuple-element.37), channel_id=1, source_target_pairs={{0,64},{16,80},{32,96},{48,112},{64,0},{80,16},{96,32},{112,48},{1... | collective-permute-start | bytes 589832 | tf_op jit(solution)/shard_map/ppermute | solution.py:416
  183.2 13.2 %collective-permute-start.5 = (bf16[384,256]{1,0:T(8,128)(2,1)S(1)}, bf16[384,256]{1,0:T(8,128)(2,1)S(1)}, u32[]{:S(2)}, u32[]{:S(2)}) collective-permute-start(bf16[384,256]{1,0:T(8,128)(2,1)S(1)} %get-tuple-element.38), channel_id=1, source_target_pairs={{0,80},{16,64},{32,112},{48,96},{64,16},{80,0},{96,48},{112,32},{1... | collective-permute-start | bytes 589832 | tf_op jit(solution)/shard_map/ppermute | solution.py:416
  185.8 12.7 %collective-permute-start.6 = (bf16[384,256]{1,0:T(8,128)(2,1)S(1)}, bf16[384,256]{1,0:T(8,128)(2,1)S(1)}, u32[]{:S(2)}, u32[]{:S(2)}) collective-permute-start(bf16[384,256]{1,0:T(8,128)(2,1)S(1)} %get-tuple-element.39), channel_id=1, source_target_pairs={{0,32},{16,48},{32,64},{48,80},{64,96},{80,112},{96,0},{112,16},{1... | collective-permute-start | bytes 589832 | tf_op jit(solution)/shard_map/ppermute | solution.py:416
  185.8 20.7 %collective-permute-start.7 = (bf16[384,256]{1,0:T(8,128)(2,1)S(1)}, bf16[384,256]{1,0:T(8,128)(2,1)S(1)}, u32[]{:S(2)}, u32[]{:S(2)}) collective-permute-start(bf16[384,256]{1,0:T(8,128)(2,1)S(1)} %get-tuple-element.40), channel_id=1, source_target_pairs={{0,48},{16,32},{32,80},{48,64},{64,112},{80,96},{96,16},{112,0},{1... | collective-permute-start | bytes 589832 | tf_op jit(solution)/shard_map/ppermute | solution.py:416
  186.8 19.7 %collective-permute-start.8 = (bf16[384,256]{1,0:T(8,128)(2,1)S(1)}, bf16[384,256]{1,0:T(8,128)(2,1)S(1)}, u32[]{:S(2)}, u32[]{:S(2)}) collective-permute-start(bf16[384,256]{1,0:T(8,128)(2,1)S(1)} %get-tuple-element.41), channel_id=1, source_target_pairs={{0,96},{16,112},{32,0},{48,16},{64,32},{80,48},{96,64},{112,80},{1... | collective-permute-start | bytes 589832 | tf_op jit(solution)/shard_map/ppermute | solution.py:416
  189.5 17.0 %collective-permute-start.9 = (bf16[384,256]{1,0:T(8,128)(2,1)S(1)}, bf16[384,256]{1,0:T(8,128)(2,1)S(1)}, u32[]{:S(2)}, u32[]{:S(2)}) collective-permute-start(bf16[384,256]{1,0:T(8,128)(2,1)S(1)} %get-tuple-element.42), channel_id=1, source_target_pairs={{0,112},{16,96},{32,16},{48,0},{64,48},{80,32},{96,80},{112,64},{1... | collective-permute-start | bytes 589832 | tf_op jit(solution)/shard_map/ppermute | solution.py:416
  196.4 15.0 %collective-permute-start.10 = (bf16[384,256]{1,0:T(8,128)(2,1)S(1)}, bf16[384,256]{1,0:T(8,128)(2,1)S(1)}, u32[]{:S(2)}, u32[]{:S(2)}) collective-permute-start(bf16[384,256]{1,0:T(8,128)(2,1)S(1)} %get-tuple-element.44), channel_id=1, source_target_pairs={{0,16},{16,0},{32,48},{48,32},{64,80},{80,64},{96,112},{112,96},{1... | collective-permute-start | bytes 589832 | tf_op jit(solution)/shard_map/ppermute | solution.py:416

commit v7 on v5

--- a/solution.py
+++ b/solution.py
@@ -88,11 +88,12 @@
     return lax.all_to_all(sent, PLANE, 0, 0, tiled=True)
 
 
-def unpack_kernel(ref, out_ref, tan_ref):
+def unpack_kernel(even_ref, odd_ref, out_ref, tan_ref):
     for head in range(8):
         lanes = slice(head * HDIM, (head + 1) * HDIM)
-        out_ref[:, lanes] = ref[head % 2, head // 2, :, :HDIM]
-        tan_ref[:, lanes] = ref[head % 2, head // 2, :, HDIM:]
+        ref = odd_ref if head % 2 else even_ref
+        out_ref[:, lanes] = ref[head // 2, :, :HDIM]
+        tan_ref[:, lanes] = ref[head // 2, :, HDIM:]
 
 
 def unpack(back):
@@ -103,10 +104,13 @@
         unpack_kernel,
         out_shape=(shape, shape),
         grid=(4,),
-        in_specs=[pl.BlockSpec((2, 4, rows, 2 * HDIM), lambda j: (0, j, 0, 0))],
+        in_specs=[
+            pl.BlockSpec((4, rows, 2 * HDIM), lambda j: (j, 0, 0)),
+            pl.BlockSpec((4, rows, 2 * HDIM), lambda j: (4 + j, 0, 0)),
+        ],
         out_specs=(spec, spec),
         cost_estimate=pl.CostEstimate(flops=0, transcendentals=0, bytes_accessed=4 << 20),
-    )(back.reshape(2, 16, rows, 2 * HDIM))
+    )(back, back)
 
 
 def attend_kernel(slots_ref, q_ref, *rest, loads, sources, halves, first, first_half):
@@ -326,10 +330,14 @@
         copy.wait()
         if step + 2 < len(reads):
             reads[step + 2].start()
-        part = jnp.dot(
-            rows[step], pair[...].reshape(2 * CLIP, 2 * HDIM), preferred_element_type=f32
-        )
-        parts[step] = part.astype(bf16).reshape(2, height // 2, 2 * HDIM)
+        for row in range(0, height, 128):
+            part = jnp.dot(
+                rows[step, row : row + 128],
+                pair[...].reshape(2 * CLIP, 2 * HDIM),
+                preferred_element_type=f32,
+            )
+            at = row % (height // 2)
+            parts[step, 2 * row // height, at : at + 128] = part.astype(bf16)
         for dz in range(2):
             n = 2 * step + dz
             writes.append(
@@ -400,9 +408,8 @@
         dx, dz = HOPS[n // 2], n % 2
         ring = [(2 * x + z, 2 * ((x + dx) % 4) + (z ^ dz)) for x in range(4) for z in range(2)]
         arrived.append(term if (dx, dz) == (0, 0) else lax.ppermute(term, CLIPS, ring))
-    rows, arrived = lax.optimization_barrier((unpack(back), arrived))
     weight_grad = sum(term.astype(f32) for term in arrived)
-    return *rows, weight_grad
+    return *unpack(back), weight_grad
 
 
 def solution(mesh):

time: 212 us -> 216 us (1.019)
  waiting for transfers between devices: 83.8 us -> 91.4 us
  Pallas kernels: 73.9 us -> 71.2 us
    ppermute x7, waiting for transfers between devices: 10.8 us -> 22.7 us  [on_device(): lax.ppermute(term, CLIPS, ring)]
    all_to_all x1, waiting for transfers between devices: 4.32 us -> 0.01 us  [on_device(): back = lax.all_to_all(sent, PLANE, 0, 0, tiled=True)]
    pallas_call x1, Pallas kernels: 11.7 us -> 8.92 us  [grad_terms(): pl.pallas_call(grad_kernel, out_shape=[jax.ShapeDtypeStruct((width, 2 * H...]
    unnamed x23 -> x21, local copies, waits for them, and re-layouts: 8 us -> 8 us
  transfers between devices with their start and end apart: 14 -> 14, of which waited for: 8 -> 9; matrix products, arithmetic and copies ran while one was open for 2% -> 3% of each run, Pallas kernels for 33% -> 30%
where the time goes in v7:
time: 216 us
  waiting for transfers between devices  91.4 us (42%)
  Pallas kernels  71.2 us (33%)
  starting transfers between devices  38.6 us (18%)
  local copies, waits for them, and re-layouts  11.2 us (5%)
  other arithmetic  2.62 us (1%)
    all_to_all x2, waiting for transfers between devices, to_heads(): return lax.all_to_all(sent, PLANE, 0, 0, tiled=True)  60.8 us
    pallas_call x3, Pallas kernels, attend(): pl.pallas_call(functools.partial(attend_kernel, loads=loads, sources=len(...  43.9 us
    ppermute x7, waiting for transfers between devices, on_device(): lax.ppermute(term, CLIPS, ring)  22.7 us
    all_to_all x2, starting transfers between devices, to_heads(): return lax.all_to_all(sent, PLANE, 0, 0, tiled=True)  15.5 us
    ppermute x7, starting transfers between devices, on_device(): lax.ppermute(term, CLIPS, ring)  9.37 us
    pallas_call x1, Pallas kernels, grad_terms(): pl.pallas_call(grad_kernel, out_shape=[jax.ShapeDtypeStruct((width, 2 * H...  8.92 us
    pallas_call x1, Pallas kernels, turned(): pl.pallas_call(turn_kernel, out_shape=jax.ShapeDtypeStruct((columns, rows...  8.43 us
    unnamed x21, local copies, waits for them, and re-layouts  8 us
  transfers between devices with their start and end apart: 14, of which 9 were waited for; matrix products, arithmetic and copies ran while one was open for 3% of the time, Pallas kernels for 30%

profile of v7, /device:TPU:1, one launch (start us, length us, event | category | flops | bytes accessed | tf_op | source)
XLA Modules:
  0.0 215.7 jit_solution(2965875469919280152)
XLA Ops:
  0.6 3.4 %shard_map.105 = bf16[2,16,128,512]{3,2,1,0:T(8,128)(2,1)} custom-call(bf16[128,4096]{1,0:T(8,128)(2,1)} %refs_0_.3, bf16[128,4096]{1,0:T(8,128)(2,1)} %refs_1_.3, bf16[128,4096]{1,0:T(8,128)(2,1)} %refs_2_.1, bf16[128,4096]{1,0:T(8,128)(2,1)} %refs_3_.1), custom_call_target="tpu_custom_call" | custom-call | bytes 8388608 | tf_op jit(solution)/shard_map/pallas_call | solution.py:69
  4.1 9.7 %all-to-all-start.1 = ((bf16[32,128,512]{2,1,0:T(8,128)(2,1)}), bf16[32,128,512]{2,1,0:T(8,128)(2,1)}, u32[]{:S(2)}, u32[]{:S(2)}) async-start(bf16[32,128,512]{2,1,0:T(8,128)(2,1)} %bitcast.4), calls=%async_computation.1 | async-start | bytes 8388608 | tf_op jit(solution)/shard_map/all_to_all | solution.py:88
  13.7 8.4 %shard_map.104.cot_ref = bf16[3072,2048]{1,0:T(8,128)(2,1)S(1)} custom-call(bf16[2048,3072]{1,0:T(8,128)(2,1)} %ref.1), custom_call_target="tpu_custom_call" | custom-call | bytes 25165824 | tf_op jit(solution)/shard_map/pallas_call | solution.py:281
  22.2 4.5 %copy-done.1 = bf16[3072,2048]{1,0:T(8,128)(2,1)} copy-done((bf16[3072,2048]{1,0:T(8,128)(2,1)}, bf16[3072,2048]{1,0:T(8,128)(2,1)S(1)}, u32[]{:S(2)}) %copy-start.1) | copy-done | bytes 12582936
  26.7 2.5 %shard_map.103 = bf16[2,16,128,256]{3,2,1,0:T(8,128)(2,1)} custom-call(bf16[128,4096]{1,0:T(8,128)(2,1)} %refs_0_.2, bf16[128,4096]{1,0:T(8,128)(2,1)} %refs_1_.2), custom_call_target="tpu_custom_call" | custom-call | bytes 4194304 | tf_op jit(solution)/shard_map/pallas_call | solution.py:69
  29.2 36.2 %all-to-all-done.1.rest_0_ = bf16[32,128,512]{2,1,0:T(8,128)(2,1)} async-done(((bf16[32,128,512]{2,1,0:T(8,128)(2,1)}), bf16[32,128,512]{2,1,0:T(8,128)(2,1)}, u32[]{:S(2)}, u32[]{:S(2)}) %all-to-all-start.1) | async-done | bytes 4194336 | tf_op jit(solution)/shard_map/all_to_all | solution.py:88
  65.4 5.9 %all-to-all-start = ((bf16[32,128,256]{2,1,0:T(8,128)(2,1)}), bf16[32,128,256]{2,1,0:T(8,128)(2,1)S(1)}, u32[]{:S(2)}, u32[]{:S(2)}) async-start(bf16[32,128,256]{2,1,0:T(8,128)(2,1)} %bitcast.5), calls=%async_computation | async-start | bytes 4194304 | tf_op jit(solution)/shard_map/all_to_all | solution.py:88
  71.3 3.1 %slice.13 = bf16[16,128,512]{2,1,0:T(8,128)(2,1)} slice(bf16[32,128,512]{2,1,0:T(8,128)(2,1)} %all-to-all-done.1.rest_0_), slice={[16:32], [0:128], [0:512]} | slice | bytes 4194304 | tf_op jit(solution)/shard_map/slice | solution.py:383
  74.4 1.2 collective-permute-start
  75.9 24.6 %all-to-all-done.q_ref = bf16[32,128,256]{2,1,0:T(8,128)(2,1)S(1)} async-done(((bf16[32,128,256]{2,1,0:T(8,128)(2,1)}), bf16[32,128,256]{2,1,0:T(8,128)(2,1)S(1)}, u32[]{:S(2)}, u32[]{:S(2)}) %all-to-all-start) | async-done | bytes 2097184 | tf_op jit(solution)/shard_map/all_to_all | solution.py:88
  100.5 20.9 %shard_map.106 = (bf16[2,16,64,128]{3,2,1,0:T(8,128)(2,1)S(1)}, bf16[32,128,256]{2,1,0:T(8,128)(2,1)S(1)}) custom-call(s32[2,3]{1,0:T(2,128)S(1)} %get-tuple-element.43.slots_ref, bf16[32,128,256]{2,1,0:T(8,128)(2,1)S(1)} %all-to-all-done.q_ref, bf16[32,128,512]{2,1,0:T(8,128)(2,1)} %all-to-all-done.1.rest_0_), custom_call_target="tpu_custom_call" | custom-call | flops 12884901888 | bytes 8388608 | tf_op jit(solution)/shard_map/pallas_call | solution.py:239
  121.5 2.6 %collective-permute-start.1 = (bf16[2,16,64,128]{3,2,1,0:T(8,128)(2,1)S(1)}, bf16[2,16,64,128]{3,2,1,0:T(8,128)(2,1)S(1)}, u32[]{:S(2)}, u32[]{:S(2)}) collective-permute-start(bf16[2,16,64,128]{3,2,1,0:T(8,128)(2,1)S(1)} %get-tuple-element.28.late), channel_id=1, source_target_pairs={{0,16},{1,17},{2,18},{3,19},{4,20},{5,21},{6,22},{7,23},{8,24},{9,... | collective-permute-start | bytes 1572872 | tf_op jit(solution)/shard_map/ppermute | solution.py:396
  124.1 11.5 %shard_map.107 = (bf16[1,16,64,128]{3,2,1,0:T(8,128)(2,1)S(1)}, bf16[32,128,256]{2,1,0:T(8,128)(2,1)S(1)}) custom-call(s32[2,3]{1,0:T(2,128)S(1)} %get-tuple-element.44.slots_ref, bf16[32,128,256]{2,1,0:T(8,128)(2,1)S(1)} %all-to-all-done.q_ref, bf16[32,128,512]{2,1,0:T(8,128)(2,1)} %all-to-all-done.1.rest_0_, ...), custom_call_target="tpu_custom_call", output_to_operand_aliasing={{1}: (4, {})} | custom-call | flops 6442450944 | bytes 8388608 | tf_op jit(solution)/shard_map/pallas_call | solution.py:239
  135.6 1.3 collective-permute-start.2
  136.9 11.5 %shard_map.108 = (bf16[1,16,64,128]{3,2,1,0:T(8,128)(2,1)S(1)}, bf16[32,128,256]{2,1,0:T(8,128)(2,1)S(1)}) custom-call(s32[2,3]{1,0:T(2,128)S(1)} %get-tuple-element.44.slots_ref, bf16[32,128,256]{2,1,0:T(8,128)(2,1)S(1)} %all-to-all-done.q_ref, bf16[32,128,512]{2,1,0:T(8,128)(2,1)} %all-to-all-done.1.rest_0_, ...), custom_call_target="tpu_custom_call", output_to_operand_aliasing={{1}: (4, {})} | custom-call | flops 6442450944 | bytes 8388608 | tf_op jit(solution)/shard_map/pallas_call | solution.py:239
  148.4 1.3 copy-done.2
  149.7 1.3 collective-permute-start.3
  151.0 7.9 %collective-permute-done.3.got_b = bf16[1,16,64,128]{3,2,1,0:T(8,128)(2,1)S(1)} collective-permute-done((bf16[1,16,64,128]{3,2,1,0:T(8,128)(2,1)S(1)}, bf16[1,16,64,128]{3,2,1,0:T(8,128)(2,1)S(1)}, u32[]{:S(2)}, u32[]{:S(2)}) %collective-permute-start.3) | collective-permute-done | bytes 262176 | tf_op jit(solution)/shard_map/ppermute | solution.py:399
  159.6 7.3 %all-to-all-start.2 = ((bf16[32,128,256]{2,1,0:T(8,128)(2,1)}), bf16[32,128,256]{2,1,0:T(8,128)(2,1)S(1)}, u32[]{:S(2)}, u32[]{:S(2)}) async-start(bf16[32,128,256]{2,1,0:T(8,128)(2,1)} %copy-done.2), calls=%async_computation.2 | async-start | bytes 4194304 | tf_op jit(solution)/shard_map/all_to_all | solution.py:401
  167.5 8.9 %shard_map.110 = (bf16[384,256]{1,0:T(8,128)(2,1)}, bf16[384,256]{1,0:T(8,128)(2,1)}, bf16[384,256]{1,0:T(8,128)(2,1)}, bf16[384,256]{1,0:T(8,128)(2,1)}, bf16[3...) custom-call(s32[2]{0:T(128)} %pad_add_fusion.1.place_ref, ...), custom_call_target="tpu_custom_call" | custom-call | flops 3221225472 | bytes 15728640 | tf_op jit(solution)/shard_map/pallas_call | solution.py:355
  176.5 1.6 collective-permute-start.4
  178.1 2.5 %collective-permute-start.5 = (bf16[384,256]{1,0:T(8,128)(2,1)}, bf16[384,256]{1,0:T(8,128)(2,1)S(1)}, u32[]{:S(2)}, u32[]{:S(2)}) collective-permute-start(bf16[384,256]{1,0:T(8,128)(2,1)} %get-tuple-element.36), channel_id=1, source_target_pairs={{0,80},{16,64},{32,112},{48,96},{64,16},{80,0},{96,48},{112,32},{1... | collective-permute-start | bytes 589832 | tf_op jit(solution)/shard_map/ppermute | solution.py:410
  180.6 1.0 collective-permute-start.7
  181.6 1.7 collective-permute-start.8
  183.3 0.9 collective-permute-done.4
  184.2 2.5 %collective-permute-start.9 = (bf16[384,256]{1,0:T(8,128)(2,1)}, bf16[384,256]{1,0:T(8,128)(2,1)S(1)}, u32[]{:S(2)}, u32[]{:S(2)}) collective-permute-start(bf16[384,256]{1,0:T(8,128)(2,1)} %get-tuple-element.40), channel_id=1, source_target_pairs={{0,112},{16,96},{32,16},{48,0},{64,48},{80,32},{96,80},{112,64},{1... | collective-permute-start | bytes 589832 | tf_op jit(solution)/shard_map/ppermute | solution.py:410
  186.8 5.9 %collective-permute-done.5 = bf16[384,256]{1,0:T(8,128)(2,1)S(1)} collective-permute-done((bf16[384,256]{1,0:T(8,128)(2,1)}, bf16[384,256]{1,0:T(8,128)(2,1)S(1)}, u32[]{:S(2)}, u32[]{:S(2)}) %collective-permute-start.5) | collective-permute-done | bytes 196640 | tf_op jit(solution)/shard_map/ppermute | solution.py:410
  193.5 9.0 %collective-permute-done.7 = bf16[384,256]{1,0:T(8,128)(2,1)S(1)} collective-permute-done((bf16[384,256]{1,0:T(8,128)(2,1)}, bf16[384,256]{1,0:T(8,128)(2,1)S(1)}, u32[]{:S(2)}, u32[]{:S(2)}) %collective-permute-start.7) | collective-permute-done | bytes 196640 | tf_op jit(solution)/shard_map/ppermute | solution.py:410
  202.9 5.6 %collective-permute-done.10 = bf16[384,256]{1,0:T(8,128)(2,1)S(1)} collective-permute-done((bf16[384,256]{1,0:T(8,128)(2,1)}, bf16[384,256]{1,0:T(8,128)(2,1)S(1)}, u32[]{:S(2)}, u32[]{:S(2)}) %collective-permute-start.10) | collective-permute-done | bytes 196640 | tf_op jit(solution)/shard_map/ppermute | solution.py:410
  208.5 1.9 convert_add_fusion
  210.4 1.4 copy-done.6
  211.7 4.0 %shard_map.109 = (bf16[128,4096]{1,0:T(8,128)(2,1)}, bf16[128,4096]{1,0:T(8,128)(2,1)}) custom-call(bf16[32,128,256]{2,1,0:T(8,128)(2,1)} %copy-done.6, bf16[32,128,256]{2,1,0:T(8,128)(2,1)} %copy-done.6), custom_call_target="tpu_custom_call" | custom-call | bytes 4194304 | tf_op jit(solution)/shard_map/pallas_call | solution.py:103
  (33 shorter events, 2.9 us)
Async XLA Ops:
  0.6 75.0 %copy-start = (s32[16,2]{0,1:T(2,128)S(1)}, s32[16,2]{0,1:T(2,128)}, u32[]{:S(2)}) copy-start(s32[16,2]{0,1:T(2,128)} %param.14) | copy-start | bytes 388
  4.1 61.4 %all-to-all-start.1 = ((bf16[32,128,512]{2,1,0:T(8,128)(2,1)}), bf16[32,128,512]{2,1,0:T(8,128)(2,1)}, u32[]{:S(2)}, u32[]{:S(2)}) async-start(bf16[32,128,512]{2,1,0:T(8,128)(2,1)} %bitcast.4), calls=%async_computation.1 | async-start | bytes 8388608 | tf_op jit(solution)/shard_map/all_to_all | solution.py:88
  22.2 4.5 %copy-start.1 = (bf16[3072,2048]{1,0:T(8,128)(2,1)}, bf16[3072,2048]{1,0:T(8,128)(2,1)S(1)}, u32[]{:S(2)}) copy-start(bf16[3072,2048]{1,0:T(8,128)(2,1)S(1)} %shard_map.104.cot_ref) | copy-start | bytes 37748740
  65.4 35.1 %all-to-all-start = ((bf16[32,128,256]{2,1,0:T(8,128)(2,1)}), bf16[32,128,256]{2,1,0:T(8,128)(2,1)S(1)}, u32[]{:S(2)}, u32[]{:S(2)}) async-start(bf16[32,128,256]{2,1,0:T(8,128)(2,1)} %bitcast.5), calls=%async_computation | async-start | bytes 4194304 | tf_op jit(solution)/shard_map/all_to_all | solution.py:88
  74.4 49.6 %collective-permute-start = (bf16[16,128,512]{2,1,0:T(8,128)(2,1)}, bf16[16,128,512]{2,1,0:T(8,128)(2,1)}, u32[]{:S(2)}, u32[]{:S(2)}) collective-permute-start(bf16[16,128,512]{2,1,0:T(8,128)(2,1)} %slice.13), channel_id=1, source_target_pairs={{0,32},{32,64},{64,96},{96,0},{1,33},{33,65},{65,97},{97,1},{2,34}... | collective-permute-start | bytes 6291464 | tf_op jit(solution)/shard_map/ppermute | solution.py:383
  121.5 14.1 %copy-start.3 = (bf16[2,16,64,128]{3,2,1,0:T(8,128)(2,1)}, bf16[2,16,64,128]{3,2,1,0:T(8,128)(2,1)S(1)}, u32[]{:S(2)}) copy-start(bf16[2,16,64,128]{3,2,1,0:T(8,128)(2,1)S(1)} %get-tuple-element.28.late) | copy-start | bytes 1572868
  121.5 28.2 %collective-permute-start.1 = (bf16[2,16,64,128]{3,2,1,0:T(8,128)(2,1)S(1)}, bf16[2,16,64,128]{3,2,1,0:T(8,128)(2,1)S(1)}, u32[]{:S(2)}, u32[]{:S(2)}) collective-permute-start(bf16[2,16,64,128]{3,2,1,0:T(8,128)(2,1)S(1)} %get-tuple-element.28.late), channel_id=1, source_target_pairs={{0,16},{1,17},{2,18},{3,19},{4,20},{5,21},{6,22},{7,23},{8,24},{9,... | collective-permute-start | bytes 1572872 | tf_op jit(solution)/shard_map/ppermute | solution.py:396
  135.6 12.8 %copy-start.4 = (bf16[1,16,64,128]{3,2,1,0:T(8,128)(2,1)}, bf16[1,16,64,128]{3,2,1,0:T(8,128)(2,1)S(1)}, u32[]{:S(2)}) copy-start(bf16[1,16,64,128]{3,2,1,0:T(8,128)(2,1)S(1)} %get-tuple-element.29.early_a) | copy-start | bytes 786436
  135.6 14.1 %collective-permute-start.2 = (bf16[1,16,64,128]{3,2,1,0:T(8,128)(2,1)S(1)}, bf16[1,16,64,128]{3,2,1,0:T(8,128)(2,1)S(1)}, u32[]{:S(2)}, u32[]{:S(2)}) collective-permute-start(bf16[1,16,64,128]{3,2,1,0:T(8,128)(2,1)S(1)} %get-tuple-element.29.early_a), channel_id=1, source_target_pairs={{16,0},{17,1},{18,2},{19,3},{20,4},{21,5},{22,6},{23,7},{24,8},{25... | collective-permute-start | bytes 786440 | tf_op jit(solution)/shard_map/ppermute | solution.py:397
  148.4 1.3 copy-start.2
  149.7 9.2 %copy-start.5 = (bf16[1,16,64,128]{3,2,1,0:T(8,128)(2,1)}, bf16[1,16,64,128]{3,2,1,0:T(8,128)(2,1)S(1)}, u32[]{:S(2)}) copy-start(bf16[1,16,64,128]{3,2,1,0:T(8,128)(2,1)S(1)} %get-tuple-element.30.early_b) | copy-start | bytes 786436
  149.7 9.2 %copy-start.7 = (bf16[2,16,64,128]{3,2,1,0:T(8,128)(2,1)}, bf16[2,16,64,128]{3,2,1,0:T(8,128)(2,1)S(1)}, u32[]{:S(2)}) copy-start(bf16[2,16,64,128]{3,2,1,0:T(8,128)(2,1)S(1)} %collective-permute-done.1.got_late) | copy-start | bytes 1572868
  149.7 9.2 %copy-start.8 = (bf16[1,16,64,128]{3,2,1,0:T(8,128)(2,1)}, bf16[1,16,64,128]{3,2,1,0:T(8,128)(2,1)S(1)}, u32[]{:S(2)}) copy-start(bf16[1,16,64,128]{3,2,1,0:T(8,128)(2,1)S(1)} %collective-permute-done.2.got_a) | copy-start | bytes 786436
  149.7 9.2 %collective-permute-start.3 = (bf16[1,16,64,128]{3,2,1,0:T(8,128)(2,1)S(1)}, bf16[1,16,64,128]{3,2,1,0:T(8,128)(2,1)S(1)}, u32[]{:S(2)}, u32[]{:S(2)}) collective-permute-start(bf16[1,16,64,128]{3,2,1,0:T(8,128)(2,1)S(1)} %get-tuple-element.30.early_b), channel_id=1, source_target_pairs={{16,0},{17,1},{18,2},{19,3},{20,4},{21,5},{22,6},{23,7},{24,8},{25... | collective-permute-start | bytes 786440 | tf_op jit(solution)/shard_map/ppermute | solution.py:399
  158.9 0.7 copy-start.9
  159.6 50.8 %all-to-all-start.2 = ((bf16[32,128,256]{2,1,0:T(8,128)(2,1)}), bf16[32,128,256]{2,1,0:T(8,128)(2,1)S(1)}, u32[]{:S(2)}, u32[]{:S(2)}) async-start(bf16[32,128,256]{2,1,0:T(8,128)(2,1)} %copy-done.2), calls=%async_computation.2 | async-start | bytes 4194304 | tf_op jit(solution)/shard_map/all_to_all | solution.py:401
  176.5 7.8 %collective-permute-start.4 = (bf16[384,256]{1,0:T(8,128)(2,1)}, bf16[384,256]{1,0:T(8,128)(2,1)S(1)}, u32[]{:S(2)}, u32[]{:S(2)}) collective-permute-start(bf16[384,256]{1,0:T(8,128)(2,1)} %get-tuple-element.35), channel_id=1, source_target_pairs={{0,64},{16,80},{32,96},{48,112},{64,0},{80,16},{96,32},{112,48},{1... | collective-permute-start | bytes 589832 | tf_op jit(solution)/shard_map/ppermute | solution.py:410
  178.1 14.6 %collective-permute-start.5 = (bf16[384,256]{1,0:T(8,128)(2,1)}, bf16[384,256]{1,0:T(8,128)(2,1)S(1)}, u32[]{:S(2)}, u32[]{:S(2)}) collective-permute-start(bf16[384,256]{1,0:T(8,128)(2,1)} %get-tuple-element.36), channel_id=1, source_target_pairs={{0,80},{16,64},{32,112},{48,96},{64,16},{80,0},{96,48},{112,32},{1... | collective-permute-start | bytes 589832 | tf_op jit(solution)/shard_map/ppermute | solution.py:410
  180.6 12.9 %collective-permute-start.6 = (bf16[384,256]{1,0:T(8,128)(2,1)}, bf16[384,256]{1,0:T(8,128)(2,1)S(1)}, u32[]{:S(2)}, u32[]{:S(2)}) collective-permute-start(bf16[384,256]{1,0:T(8,128)(2,1)} %get-tuple-element.37), channel_id=1, source_target_pairs={{0,32},{16,48},{32,64},{48,80},{64,96},{80,112},{96,0},{112,16},{1... | collective-permute-start | bytes 589832 | tf_op jit(solution)/shard_map/ppermute | solution.py:410
  180.6 21.9 %collective-permute-start.7 = (bf16[384,256]{1,0:T(8,128)(2,1)}, bf16[384,256]{1,0:T(8,128)(2,1)S(1)}, u32[]{:S(2)}, u32[]{:S(2)}) collective-permute-start(bf16[384,256]{1,0:T(8,128)(2,1)} %get-tuple-element.38), channel_id=1, source_target_pairs={{0,48},{16,32},{32,80},{48,64},{64,112},{80,96},{96,16},{112,0},{1... | collective-permute-start | bytes 589832 | tf_op jit(solution)/shard_map/ppermute | solution.py:410
  181.6 20.9 %collective-permute-start.8 = (bf16[384,256]{1,0:T(8,128)(2,1)}, bf16[384,256]{1,0:T(8,128)(2,1)S(1)}, u32[]{:S(2)}, u32[]{:S(2)}) collective-permute-start(bf16[384,256]{1,0:T(8,128)(2,1)} %get-tuple-element.39), channel_id=1, source_target_pairs={{0,96},{16,112},{32,0},{48,16},{64,32},{80,48},{96,64},{112,80},{1... | collective-permute-start | bytes 589832 | tf_op jit(solution)/shard_map/ppermute | solution.py:410
  184.2 18.7 %collective-permute-start.9 = (bf16[384,256]{1,0:T(8,128)(2,1)}, bf16[384,256]{1,0:T(8,128)(2,1)S(1)}, u32[]{:S(2)}, u32[]{:S(2)}) collective-permute-start(bf16[384,256]{1,0:T(8,128)(2,1)} %get-tuple-element.40), channel_id=1, source_target_pairs={{0,112},{16,96},{32,16},{48,0},{64,48},{80,32},{96,80},{112,64},{1... | collective-permute-start | bytes 589832 | tf_op jit(solution)/shard_map/ppermute | solution.py:410
  192.6 15.9 %collective-permute-start.10 = (bf16[384,256]{1,0:T(8,128)(2,1)}, bf16[384,256]{1,0:T(8,128)(2,1)S(1)}, u32[]{:S(2)}, u32[]{:S(2)}) collective-permute-start(bf16[384,256]{1,0:T(8,128)(2,1)} %get-tuple-element.42), channel_id=1, source_target_pairs={{0,16},{16,0},{32,48},{48,32},{64,80},{80,64},{96,112},{112,96},{1... | collective-permute-start | bytes 589832 | tf_op jit(solution)/shard_map/ppermute | solution.py:410
  210.4 1.4 copy-start.6

commit v8 on v7

--- a/solution.py
+++ b/solution.py
@@ -109,6 +109,7 @@
             pl.BlockSpec((4, rows, 2 * HDIM), lambda j: (4 + j, 0, 0)),
         ],
         out_specs=(spec, spec),
+        compiler_params=pltpu.CompilerParams(vmem_limit_bytes=8 << 20),
         cost_estimate=pl.CostEstimate(flops=0, transcendentals=0, bytes_accessed=4 << 20),
     )(back, back)
 
@@ -381,7 +382,10 @@
 ):
     own = to_heads(packed(key_rows, key_tangent, value_rows, value_tangent))
     halo = lax.ppermute(own[16:], "x", [(i, (i + 1) % 4) for i in range(4)])
-    query, columns = lax.optimization_barrier((packed(query_tangent, queries), turned(cotangent)))
+    place = jnp.stack([lax.axis_index("x"), lax.axis_index("zl")]).astype(jnp.int32)
+    query, columns, place = lax.optimization_barrier(
+        (packed(query_tangent, queries), turned(cotangent), place)
+    )
     query = to_heads(query)
 
     plane = lax.axis_index("x") * 4
@@ -399,7 +403,6 @@
     got2 = lax.ppermute(last, "zl", [(1, 0)])
     sent, _ = lax.optimization_barrier((sent, got2))
     back = lax.all_to_all(sent, PLANE, 0, 0, tiled=True)
-    place = jnp.stack([lax.axis_index("x"), lax.axis_index("zl")]).astype(jnp.int32)
     terms = grad_terms(
         place, (early1, early2, got1, got2, late, got_late), columns
     )
@@ -408,8 +411,9 @@
         dx, dz = HOPS[n // 2], n % 2
         ring = [(2 * x + z, 2 * ((x + dx) % 4) + (z ^ dz)) for x in range(4) for z in range(2)]
         arrived.append(term if (dx, dz) == (0, 0) else lax.ppermute(term, CLIPS, ring))
+    rows, arrived = lax.optimization_barrier((unpack(back), arrived))
     weight_grad = sum(term.astype(f32) for term in arrived)
-    return *unpack(back), weight_grad
+    return *rows, weight_grad
 
 
 def solution(mesh):

time: 216 us -> 211 us (0.977)
    ppermute x7, waiting for transfers between devices: 22.7 us -> 8.84 us  [on_device(): lax.ppermute(term, CLIPS, ring)]
    all_to_all x1, waiting for transfers between devices: 0.01 us -> 12.6 us  [on_device(): back = lax.all_to_all(sent, PLANE, 0, 0, tiled=True)]
  transfers between devices with their start and end apart: 14 -> 14, of which waited for: 9 -> 7; matrix products, arithmetic and copies ran while one was open for 3% -> 2% of each run, Pallas kernels for 30% -> 31%
where the time goes in v8:
time: 211 us; the launch traced here: 210 us
  waiting for transfers between devices  89.4 us (42%)
  Pallas kernels  69.2 us (33%)
  starting transfers between devices  38.6 us (18%)
  local copies, waits for them, and re-layouts  9.81 us (5%)
  other arithmetic  2.64 us (1%)
    all_to_all x2, waiting for transfers between devices, to_heads(): return lax.all_to_all(sent, PLANE, 0, 0, tiled=True)  60.1 us
    pallas_call x3, Pallas kernels, attend(): pl.pallas_call(functools.partial(attend_kernel, loads=loads, sources=len(...  43.9 us
    all_to_all x2, starting transfers between devices, to_heads(): return lax.all_to_all(sent, PLANE, 0, 0, tiled=True)  15.5 us
    all_to_all x1, waiting for transfers between devices, on_device(): back = lax.all_to_all(sent, PLANE, 0, 0, tiled=True)  12.6 us
    ppermute x7, starting transfers between devices, on_device(): lax.ppermute(term, CLIPS, ring)  9.38 us
    pallas_call x1, Pallas kernels, grad_terms(): pl.pallas_call(grad_kernel, out_shape=[jax.ShapeDtypeStruct((width, 2 * H...  8.9 us
    ppermute x7, waiting for transfers between devices, on_device(): lax.ppermute(term, CLIPS, ring)  8.84 us
    pallas_call x1, Pallas kernels, turned(): pl.pallas_call(turn_kernel, out_shape=jax.ShapeDtypeStruct((columns, rows...  8.43 us
  transfers between devices with their start and end apart: 14, of which 7 were waited for; matrix products, arithmetic and copies ran while one was open for 2% of the time, Pallas kernels for 31%

profile of v8, /device:TPU:1, one launch (start us, length us, event | category | flops | bytes accessed | tf_op | source)
XLA Modules:
  0.0 210.5 jit_solution(14801850536663141692)
XLA Ops:
  0.6 3.4 %shard_map.105 = bf16[2,16,128,512]{3,2,1,0:T(8,128)(2,1)} custom-call(bf16[128,4096]{1,0:T(8,128)(2,1)} %refs_0_.3, bf16[128,4096]{1,0:T(8,128)(2,1)} %refs_1_.3, bf16[128,4096]{1,0:T(8,128)(2,1)} %refs_2_.1, bf16[128,4096]{1,0:T(8,128)(2,1)} %refs_3_.1), custom_call_target="tpu_custom_call" | custom-call | bytes 8388608 | tf_op jit(solution)/shard_map/pallas_call | solution.py:69
  4.1 9.7 %all-to-all-start.1 = ((bf16[32,128,512]{2,1,0:T(8,128)(2,1)}), bf16[32,128,512]{2,1,0:T(8,128)(2,1)}, u32[]{:S(2)}, u32[]{:S(2)}) async-start(bf16[32,128,512]{2,1,0:T(8,128)(2,1)} %bitcast.4), calls=%async_computation.1 | async-start | bytes 8388608 | tf_op jit(solution)/shard_map/all_to_all | solution.py:88
  13.7 8.4 %shard_map.104.cot_ref = bf16[3072,2048]{1,0:T(8,128)(2,1)S(1)} custom-call(bf16[2048,3072]{1,0:T(8,128)(2,1)} %ref.1), custom_call_target="tpu_custom_call" | custom-call | bytes 25165824 | tf_op jit(solution)/shard_map/pallas_call | solution.py:282
  22.2 4.5 %copy-done.1 = bf16[3072,2048]{1,0:T(8,128)(2,1)} copy-done((bf16[3072,2048]{1,0:T(8,128)(2,1)}, bf16[3072,2048]{1,0:T(8,128)(2,1)S(1)}, u32[]{:S(2)}) %copy-start.1) | copy-done | bytes 12582936
  26.7 2.5 %shard_map.103 = bf16[2,16,128,256]{3,2,1,0:T(8,128)(2,1)} custom-call(bf16[128,4096]{1,0:T(8,128)(2,1)} %refs_0_.2, bf16[128,4096]{1,0:T(8,128)(2,1)} %refs_1_.2), custom_call_target="tpu_custom_call" | custom-call | bytes 4194304 | tf_op jit(solution)/shard_map/pallas_call | solution.py:69
  29.9 35.5 %all-to-all-done.1.rest_0_ = bf16[32,128,512]{2,1,0:T(8,128)(2,1)} async-done(((bf16[32,128,512]{2,1,0:T(8,128)(2,1)}), bf16[32,128,512]{2,1,0:T(8,128)(2,1)}, u32[]{:S(2)}, u32[]{:S(2)}) %all-to-all-start.1) | async-done | bytes 4194336 | tf_op jit(solution)/shard_map/all_to_all | solution.py:88
  65.4 5.9 %all-to-all-start = ((bf16[32,128,256]{2,1,0:T(8,128)(2,1)}), bf16[32,128,256]{2,1,0:T(8,128)(2,1)S(1)}, u32[]{:S(2)}, u32[]{:S(2)}) async-start(bf16[32,128,256]{2,1,0:T(8,128)(2,1)} %bitcast.5), calls=%async_computation | async-start | bytes 4194304 | tf_op jit(solution)/shard_map/all_to_all | solution.py:88
  71.3 3.1 %slice.13 = bf16[16,128,512]{2,1,0:T(8,128)(2,1)} slice(bf16[32,128,512]{2,1,0:T(8,128)(2,1)} %all-to-all-done.1.rest_0_), slice={[16:32], [0:128], [0:512]} | slice | bytes 4194304 | tf_op jit(solution)/shard_map/slice | solution.py:384
  74.4 1.2 collective-permute-start
  75.9 24.6 %all-to-all-done.q_ref = bf16[32,128,256]{2,1,0:T(8,128)(2,1)S(1)} async-done(((bf16[32,128,256]{2,1,0:T(8,128)(2,1)}), bf16[32,128,256]{2,1,0:T(8,128)(2,1)S(1)}, u32[]{:S(2)}, u32[]{:S(2)}) %all-to-all-start) | async-done | bytes 2097184 | tf_op jit(solution)/shard_map/all_to_all | solution.py:88
  100.5 20.9 %shard_map.106 = (bf16[2,16,64,128]{3,2,1,0:T(8,128)(2,1)S(1)}, bf16[32,128,256]{2,1,0:T(8,128)(2,1)S(1)}) custom-call(s32[2,3]{1,0:T(2,128)S(1)} %get-tuple-element.65.slots_ref, bf16[32,128,256]{2,1,0:T(8,128)(2,1)S(1)} %all-to-all-done.q_ref, bf16[32,128,512]{2,1,0:T(8,128)(2,1)} %all-to-all-done.1.rest_0_), custom_call_target="tpu_custom_call" | custom-call | flops 12884901888 | bytes 8388608 | tf_op jit(solution)/shard_map/pallas_call | solution.py:240
  121.4 2.6 %collective-permute-start.1 = (bf16[2,16,64,128]{3,2,1,0:T(8,128)(2,1)S(1)}, bf16[2,16,64,128]{3,2,1,0:T(8,128)(2,1)S(1)}, u32[]{:S(2)}, u32[]{:S(2)}) collective-permute-start(bf16[2,16,64,128]{3,2,1,0:T(8,128)(2,1)S(1)} %get-tuple-element.39.late), channel_id=1, source_target_pairs={{0,16},{1,17},{2,18},{3,19},{4,20},{5,21},{6,22},{7,23},{8,24},{9,... | collective-permute-start | bytes 1572872 | tf_op jit(solution)/shard_map/ppermute | solution.py:400
  124.1 11.5 %shard_map.107 = (bf16[1,16,64,128]{3,2,1,0:T(8,128)(2,1)S(1)}, bf16[32,128,256]{2,1,0:T(8,128)(2,1)S(1)}) custom-call(s32[2,3]{1,0:T(2,128)S(1)} %get-tuple-element.66.slots_ref, bf16[32,128,256]{2,1,0:T(8,128)(2,1)S(1)} %all-to-all-done.q_ref, bf16[32,128,512]{2,1,0:T(8,128)(2,1)} %all-to-all-done.1.rest_0_, ...), custom_call_target="tpu_custom_call", output_to_operand_aliasing={{1}: (4, {})} | custom-call | flops 6442450944 | bytes 8388608 | tf_op jit(solution)/shard_map/pallas_call | solution.py:240
  135.6 1.3 collective-permute-start.2
  136.9 11.5 %shard_map.108 = (bf16[1,16,64,128]{3,2,1,0:T(8,128)(2,1)S(1)}, bf16[32,128,256]{2,1,0:T(8,128)(2,1)S(1)}) custom-call(s32[2,3]{1,0:T(2,128)S(1)} %get-tuple-element.66.slots_ref, bf16[32,128,256]{2,1,0:T(8,128)(2,1)S(1)} %all-to-all-done.q_ref, bf16[32,128,512]{2,1,0:T(8,128)(2,1)} %all-to-all-done.1.rest_0_, ...), custom_call_target="tpu_custom_call", output_to_operand_aliasing={{1}: (4, {})} | custom-call | flops 6442450944 | bytes 8388608 | tf_op jit(solution)/shard_map/pallas_call | solution.py:240
  148.4 1.3 copy-done.2
  149.7 1.3 collective-permute-start.3
  151.0 7.9 %collective-permute-done.3.got_b = bf16[1,16,64,128]{3,2,1,0:T(8,128)(2,1)S(1)} collective-permute-done((bf16[1,16,64,128]{3,2,1,0:T(8,128)(2,1)S(1)}, bf16[1,16,64,128]{3,2,1,0:T(8,128)(2,1)S(1)}, u32[]{:S(2)}, u32[]{:S(2)}) %collective-permute-start.3) | collective-permute-done | bytes 262176 | tf_op jit(solution)/shard_map/ppermute | solution.py:403
  158.9 0.7 copy-done.8
  159.6 7.3 %all-to-all-start.2 = ((bf16[32,128,256]{2,1,0:T(8,128)(2,1)}), bf16[32,128,256]{2,1,0:T(8,128)(2,1)S(1)}, u32[]{:S(2)}, u32[]{:S(2)}) async-start(bf16[32,128,256]{2,1,0:T(8,128)(2,1)} %copy-done.2), calls=%async_computation.2 | async-start | bytes 4194304 | tf_op jit(solution)/shard_map/all_to_all | solution.py:405
  166.9 8.9 %shard_map.110 = (bf16[384,256]{1,0:T(8,128)(2,1)}, bf16[384,256]{1,0:T(8,128)(2,1)}, bf16[384,256]{1,0:T(8,128)(2,1)}, bf16[384,256]{1,0:T(8,128)(2,1)}, bf16[3...) custom-call(s32[2]{0:T(128)} %pad_add_fusion.1.place_ref, ...), custom_call_target="tpu_custom_call" | custom-call | flops 3221225472 | bytes 15728640 | tf_op jit(solution)/shard_map/pallas_call | solution.py:356
  175.8 1.6 collective-permute-start.4
  177.4 2.6 %collective-permute-start.5 = (bf16[384,256]{1,0:T(8,128)(2,1)}, bf16[384,256]{1,0:T(8,128)(2,1)S(1)}, u32[]{:S(2)}, u32[]{:S(2)}) collective-permute-start(bf16[384,256]{1,0:T(8,128)(2,1)} %get-tuple-element.48), channel_id=1, source_target_pairs={{0,80},{16,64},{32,112},{48,96},{64,16},{80,0},{96,48},{112,32},{1... | collective-permute-start | bytes 589832 | tf_op jit(solution)/shard_map/ppermute | solution.py:413
  180.0 1.0 collective-permute-start.7
  180.9 1.7 collective-permute-start.8
  182.6 0.9 collective-permute-done.4
  183.6 2.5 %collective-permute-start.9 = (bf16[384,256]{1,0:T(8,128)(2,1)}, bf16[384,256]{1,0:T(8,128)(2,1)S(1)}, u32[]{:S(2)}, u32[]{:S(2)}) collective-permute-start(bf16[384,256]{1,0:T(8,128)(2,1)} %get-tuple-element.52), channel_id=1, source_target_pairs={{0,112},{16,96},{32,16},{48,0},{64,48},{80,32},{96,80},{112,64},{1... | collective-permute-start | bytes 589832 | tf_op jit(solution)/shard_map/ppermute | solution.py:413
  186.1 5.6 %collective-permute-done.5 = bf16[384,256]{1,0:T(8,128)(2,1)S(1)} collective-permute-done((bf16[384,256]{1,0:T(8,128)(2,1)}, bf16[384,256]{1,0:T(8,128)(2,1)S(1)}, u32[]{:S(2)}, u32[]{:S(2)}) %collective-permute-start.5) | collective-permute-done | bytes 196640 | tf_op jit(solution)/shard_map/ppermute | solution.py:413
  191.7 12.6 %all-to-all-done.2.even_ref.odd_ref = bf16[32,128,256]{2,1,0:T(8,128)(2,1)S(1)} async-done(((bf16[32,128,256]{2,1,0:T(8,128)(2,1)}), bf16[32,128,256]{2,1,0:T(8,128)(2,1)S(1)}, u32[]{:S(2)}, u32[]{:S(2)}) %all-to-all-start.2) | async-done | bytes 2097184 | tf_op jit(solution)/shard_map/all_to_all | solution.py:405
  204.3 2.0 shard_map.109
  206.4 2.3 %collective-permute-done.10 = bf16[384,256]{1,0:T(8,128)(2,1)} collective-permute-done((bf16[384,256]{1,0:T(8,128)(2,1)}, bf16[384,256]{1,0:T(8,128)(2,1)}, u32[]{:S(2)}, u32[]{:S(2)}) %collective-permute-start.10) | collective-permute-done | bytes 196640 | tf_op jit(solution)/shard_map/ppermute | solution.py:413
  208.6 1.9 convert_add_fusion
  (33 shorter events, 1.0 us)
Async XLA Ops:
  0.6 75.0 %copy-start = (s32[16,2]{0,1:T(2,128)S(1)}, s32[16,2]{0,1:T(2,128)}, u32[]{:S(2)}) copy-start(s32[16,2]{0,1:T(2,128)} %param.14) | copy-start | bytes 388
  4.1 61.4 %all-to-all-start.1 = ((bf16[32,128,512]{2,1,0:T(8,128)(2,1)}), bf16[32,128,512]{2,1,0:T(8,128)(2,1)}, u32[]{:S(2)}, u32[]{:S(2)}) async-start(bf16[32,128,512]{2,1,0:T(8,128)(2,1)} %bitcast.4), calls=%async_computation.1 | async-start | bytes 8388608 | tf_op jit(solution)/shard_map/all_to_all | solution.py:88
  22.2 4.5 %copy-start.1 = (bf16[3072,2048]{1,0:T(8,128)(2,1)}, bf16[3072,2048]{1,0:T(8,128)(2,1)S(1)}, u32[]{:S(2)}) copy-start(bf16[3072,2048]{1,0:T(8,128)(2,1)S(1)} %shard_map.104.cot_ref) | copy-start | bytes 37748740
  65.4 35.1 %all-to-all-start = ((bf16[32,128,256]{2,1,0:T(8,128)(2,1)}), bf16[32,128,256]{2,1,0:T(8,128)(2,1)S(1)}, u32[]{:S(2)}, u32[]{:S(2)}) async-start(bf16[32,128,256]{2,1,0:T(8,128)(2,1)} %bitcast.5), calls=%async_computation | async-start | bytes 4194304 | tf_op jit(solution)/shard_map/all_to_all | solution.py:88
  74.4 49.6 %collective-permute-start = (bf16[16,128,512]{2,1,0:T(8,128)(2,1)}, bf16[16,128,512]{2,1,0:T(8,128)(2,1)}, u32[]{:S(2)}, u32[]{:S(2)}) collective-permute-start(bf16[16,128,512]{2,1,0:T(8,128)(2,1)} %slice.13), channel_id=1, source_target_pairs={{0,32},{32,64},{64,96},{96,0},{1,33},{33,65},{65,97},{97,1},{2,34}... | collective-permute-start | bytes 6291464 | tf_op jit(solution)/shard_map/ppermute | solution.py:384
  121.4 14.1 %copy-start.3 = (bf16[2,16,64,128]{3,2,1,0:T(8,128)(2,1)}, bf16[2,16,64,128]{3,2,1,0:T(8,128)(2,1)S(1)}, u32[]{:S(2)}) copy-start(bf16[2,16,64,128]{3,2,1,0:T(8,128)(2,1)S(1)} %get-tuple-element.39.late) | copy-start | bytes 1572868
  121.4 28.3 %collective-permute-start.1 = (bf16[2,16,64,128]{3,2,1,0:T(8,128)(2,1)S(1)}, bf16[2,16,64,128]{3,2,1,0:T(8,128)(2,1)S(1)}, u32[]{:S(2)}, u32[]{:S(2)}) collective-permute-start(bf16[2,16,64,128]{3,2,1,0:T(8,128)(2,1)S(1)} %get-tuple-element.39.late), channel_id=1, source_target_pairs={{0,16},{1,17},{2,18},{3,19},{4,20},{5,21},{6,22},{7,23},{8,24},{9,... | collective-permute-start | bytes 1572872 | tf_op jit(solution)/shard_map/ppermute | solution.py:400
  135.6 12.8 %copy-start.4 = (bf16[1,16,64,128]{3,2,1,0:T(8,128)(2,1)}, bf16[1,16,64,128]{3,2,1,0:T(8,128)(2,1)S(1)}, u32[]{:S(2)}) copy-start(bf16[1,16,64,128]{3,2,1,0:T(8,128)(2,1)S(1)} %get-tuple-element.40.early_a) | copy-start | bytes 786436
  135.6 14.1 %collective-permute-start.2 = (bf16[1,16,64,128]{3,2,1,0:T(8,128)(2,1)S(1)}, bf16[1,16,64,128]{3,2,1,0:T(8,128)(2,1)S(1)}, u32[]{:S(2)}, u32[]{:S(2)}) collective-permute-start(bf16[1,16,64,128]{3,2,1,0:T(8,128)(2,1)S(1)} %get-tuple-element.40.early_a), channel_id=1, source_target_pairs={{16,0},{17,1},{18,2},{19,3},{20,4},{21,5},{22,6},{23,7},{24,8},{25... | collective-permute-start | bytes 786440 | tf_op jit(solution)/shard_map/ppermute | solution.py:401
  148.4 1.3 copy-start.2
  149.7 9.2 %copy-start.5 = (bf16[1,16,64,128]{3,2,1,0:T(8,128)(2,1)}, bf16[1,16,64,128]{3,2,1,0:T(8,128)(2,1)S(1)}, u32[]{:S(2)}) copy-start(bf16[1,16,64,128]{3,2,1,0:T(8,128)(2,1)S(1)} %get-tuple-element.41.early_b) | copy-start | bytes 786436
  149.7 9.2 %copy-start.6 = (bf16[2,16,64,128]{3,2,1,0:T(8,128)(2,1)}, bf16[2,16,64,128]{3,2,1,0:T(8,128)(2,1)S(1)}, u32[]{:S(2)}) copy-start(bf16[2,16,64,128]{3,2,1,0:T(8,128)(2,1)S(1)} %collective-permute-done.1.got_late) | copy-start | bytes 1572868
  149.7 9.2 %copy-start.7 = (bf16[1,16,64,128]{3,2,1,0:T(8,128)(2,1)}, bf16[1,16,64,128]{3,2,1,0:T(8,128)(2,1)S(1)}, u32[]{:S(2)}) copy-start(bf16[1,16,64,128]{3,2,1,0:T(8,128)(2,1)S(1)} %collective-permute-done.2.got_a) | copy-start | bytes 786436
  149.7 9.2 %collective-permute-start.3 = (bf16[1,16,64,128]{3,2,1,0:T(8,128)(2,1)S(1)}, bf16[1,16,64,128]{3,2,1,0:T(8,128)(2,1)S(1)}, u32[]{:S(2)}, u32[]{:S(2)}) collective-permute-start(bf16[1,16,64,128]{3,2,1,0:T(8,128)(2,1)S(1)} %get-tuple-element.41.early_b), channel_id=1, source_target_pairs={{16,0},{17,1},{18,2},{19,3},{20,4},{21,5},{22,6},{23,7},{24,8},{25... | collective-permute-start | bytes 786440 | tf_op jit(solution)/shard_map/ppermute | solution.py:403
  158.9 0.7 copy-start.8
  159.6 44.7 %all-to-all-start.2 = ((bf16[32,128,256]{2,1,0:T(8,128)(2,1)}), bf16[32,128,256]{2,1,0:T(8,128)(2,1)S(1)}, u32[]{:S(2)}, u32[]{:S(2)}) async-start(bf16[32,128,256]{2,1,0:T(8,128)(2,1)} %copy-done.2), calls=%async_computation.2 | async-start | bytes 4194304 | tf_op jit(solution)/shard_map/all_to_all | solution.py:405
  175.8 7.8 %collective-permute-start.4 = (bf16[384,256]{1,0:T(8,128)(2,1)}, bf16[384,256]{1,0:T(8,128)(2,1)S(1)}, u32[]{:S(2)}, u32[]{:S(2)}) collective-permute-start(bf16[384,256]{1,0:T(8,128)(2,1)} %get-tuple-element.47), channel_id=1, source_target_pairs={{0,64},{16,80},{32,96},{48,112},{64,0},{80,16},{96,32},{112,48},{1... | collective-permute-start | bytes 589832 | tf_op jit(solution)/shard_map/ppermute | solution.py:413
  177.4 14.4 %collective-permute-start.5 = (bf16[384,256]{1,0:T(8,128)(2,1)}, bf16[384,256]{1,0:T(8,128)(2,1)S(1)}, u32[]{:S(2)}, u32[]{:S(2)}) collective-permute-start(bf16[384,256]{1,0:T(8,128)(2,1)} %get-tuple-element.48), channel_id=1, source_target_pairs={{0,80},{16,64},{32,112},{48,96},{64,16},{80,0},{96,48},{112,32},{1... | collective-permute-start | bytes 589832 | tf_op jit(solution)/shard_map/ppermute | solution.py:413
  180.0 26.4 %collective-permute-start.6 = (bf16[384,256]{1,0:T(8,128)(2,1)}, bf16[384,256]{1,0:T(8,128)(2,1)S(1)}, u32[]{:S(2)}, u32[]{:S(2)}) collective-permute-start(bf16[384,256]{1,0:T(8,128)(2,1)} %get-tuple-element.49), channel_id=1, source_target_pairs={{0,32},{16,48},{32,64},{48,80},{64,96},{80,112},{96,0},{112,16},{1... | collective-permute-start | bytes 589832 | tf_op jit(solution)/shard_map/ppermute | solution.py:413
  180.0 26.4 %collective-permute-start.7 = (bf16[384,256]{1,0:T(8,128)(2,1)}, bf16[384,256]{1,0:T(8,128)(2,1)S(1)}, u32[]{:S(2)}, u32[]{:S(2)}) collective-permute-start(bf16[384,256]{1,0:T(8,128)(2,1)} %get-tuple-element.50), channel_id=1, source_target_pairs={{0,48},{16,32},{32,80},{48,64},{64,112},{80,96},{96,16},{112,0},{1... | collective-permute-start | bytes 589832 | tf_op jit(solution)/shard_map/ppermute | solution.py:413
  180.9 25.4 %collective-permute-start.8 = (bf16[384,256]{1,0:T(8,128)(2,1)}, bf16[384,256]{1,0:T(8,128)(2,1)S(1)}, u32[]{:S(2)}, u32[]{:S(2)}) collective-permute-start(bf16[384,256]{1,0:T(8,128)(2,1)} %get-tuple-element.51), channel_id=1, source_target_pairs={{0,96},{16,112},{32,0},{48,16},{64,32},{80,48},{96,64},{112,80},{1... | collective-permute-start | bytes 589832 | tf_op jit(solution)/shard_map/ppermute | solution.py:413
  183.6 22.8 %collective-permute-start.9 = (bf16[384,256]{1,0:T(8,128)(2,1)}, bf16[384,256]{1,0:T(8,128)(2,1)S(1)}, u32[]{:S(2)}, u32[]{:S(2)}) collective-permute-start(bf16[384,256]{1,0:T(8,128)(2,1)} %get-tuple-element.52), channel_id=1, source_target_pairs={{0,112},{16,96},{32,16},{48,0},{64,48},{80,32},{96,80},{112,64},{1... | collective-permute-start | bytes 589832 | tf_op jit(solution)/shard_map/ppermute | solution.py:413
  191.7 16.9 %copy-start.9 = (bf16[384,256]{1,0:T(8,128)(2,1)S(1)}, bf16[384,256]{1,0:T(8,128)(2,1)}, u32[]{:S(2)}) copy-start(bf16[384,256]{1,0:T(8,128)(2,1)} %get-tuple-element.63) | copy-start | bytes 589828
  191.7 16.9 %collective-permute-start.10 = (bf16[384,256]{1,0:T(8,128)(2,1)}, bf16[384,256]{1,0:T(8,128)(2,1)}, u32[]{:S(2)}, u32[]{:S(2)}) collective-permute-start(bf16[384,256]{1,0:T(8,128)(2,1)} %get-tuple-element.54), channel_id=1, source_target_pairs={{0,16},{16,0},{32,48},{48,32},{64,80},{80,64},{96,112},{112,96},{1... | collective-permute-start | bytes 589832 | tf_op jit(solution)/shard_map/ppermute | solution.py:413

commit v9 on v8

--- a/solution.py
+++ b/solution.py
@@ -407,13 +407,13 @@
         place, (early1, early2, got1, got2, late, got_late), columns
     )
     arrived = []
-    for n, term in enumerate(terms):
-        dx, dz = HOPS[n // 2], n % 2
-        ring = [(2 * x + z, 2 * ((x + dx) % 4) + (z ^ dz)) for x in range(4) for z in range(2)]
-        arrived.append(term if (dx, dz) == (0, 0) else lax.ppermute(term, CLIPS, ring))
-    rows, arrived = lax.optimization_barrier((unpack(back), arrived))
+    for dz in (1, 0):
+        for step, dx in enumerate(HOPS):
+            term = terms[2 * step + dz]
+            ring = [(2 * x + z, 2 * ((x + dx) % 4) + (z ^ dz)) for x in range(4) for z in range(2)]
+            arrived.append(term if (dx, dz) == (0, 0) else lax.ppermute(term, CLIPS, ring))
     weight_grad = sum(term.astype(f32) for term in arrived)
-    return *rows, weight_grad
+    return *unpack(back), weight_grad
 
 
 def solution(mesh):

time: 211 us -> 214 us (1.014)
    ppermute x7, waiting for transfers between devices: 8.84 us -> 23.3 us  [on_device(): lax.ppermute(term, CLIPS, ring)]
    all_to_all x1, waiting for transfers between devices: 12.6 us -> 0.01 us  [on_device(): back = lax.all_to_all(sent, PLANE, 0, 0, tiled=True)]
    unnamed x21 -> x19, local copies, waits for them, and re-layouts: 6.64 us -> 6.62 us
  transfers between devices with their start and end apart: 14 -> 14, of which waited for: 7 -> 6; matrix products, arithmetic and copies ran while one was open for 2% -> 3% of each run, Pallas kernels for 31% -> 30%
where the time goes in v9:
time: 214 us; the launch traced here: 212 us
  waiting for transfers between devices  91.4 us (43%)
  Pallas kernels  69.2 us (32%)
  starting transfers between devices  38.6 us (18%)
  local copies, waits for them, and re-layouts  9.78 us (5%)
  other arithmetic  2.56 us (1%)
    all_to_all x2, waiting for transfers between devices, to_heads(): return lax.all_to_all(sent, PLANE, 0, 0, tiled=True)  60.2 us
    pallas_call x3, Pallas kernels, attend(): pl.pallas_call(functools.partial(attend_kernel, loads=loads, sources=len(...  43.9 us
    ppermute x7, waiting for transfers between devices, on_device(): lax.ppermute(term, CLIPS, ring)  23.3 us
    all_to_all x2, starting transfers between devices, to_heads(): return lax.all_to_all(sent, PLANE, 0, 0, tiled=True)  15.5 us
    ppermute x7, starting transfers between devices, on_device(): lax.ppermute(term, CLIPS, ring)  9.43 us
    pallas_call x1, Pallas kernels, grad_terms(): pl.pallas_call(grad_kernel, out_shape=[jax.ShapeDtypeStruct((width, 2 * H...  8.93 us
    pallas_call x1, Pallas kernels, turned(): pl.pallas_call(turn_kernel, out_shape=jax.ShapeDtypeStruct((columns, rows...  8.43 us
    ppermute x1, waiting for transfers between devices, on_device(): got2 = lax.ppermute(last, 'zl', [(1, 0)])  7.86 us
  transfers between devices with their start and end apart: 14, of which 6 were waited for; matrix products, arithmetic and copies ran while one was open for 3% of the time, Pallas kernels for 30%

profile of v9, /device:TPU:1, one launch (start us, length us, event | category | flops | bytes accessed | tf_op | source)
XLA Modules:
  0.0 212.4 jit_solution(16368713344758552752)
XLA Ops:
  0.6 3.4 %shard_map.105 = bf16[2,16,128,512]{3,2,1,0:T(8,128)(2,1)} custom-call(bf16[128,4096]{1,0:T(8,128)(2,1)} %refs_0_.3, bf16[128,4096]{1,0:T(8,128)(2,1)} %refs_1_.3, bf16[128,4096]{1,0:T(8,128)(2,1)} %refs_2_.1, bf16[128,4096]{1,0:T(8,128)(2,1)} %refs_3_.1), custom_call_target="tpu_custom_call" | custom-call | bytes 8388608 | tf_op jit(solution)/shard_map/pallas_call | solution.py:69
  4.1 9.7 %all-to-all-start.1 = ((bf16[32,128,512]{2,1,0:T(8,128)(2,1)}), bf16[32,128,512]{2,1,0:T(8,128)(2,1)}, u32[]{:S(2)}, u32[]{:S(2)}) async-start(bf16[32,128,512]{2,1,0:T(8,128)(2,1)} %bitcast.4), calls=%async_computation.1 | async-start | bytes 8388608 | tf_op jit(solution)/shard_map/all_to_all | solution.py:88
  13.7 8.4 %shard_map.104.cot_ref = bf16[3072,2048]{1,0:T(8,128)(2,1)S(1)} custom-call(bf16[2048,3072]{1,0:T(8,128)(2,1)} %ref.1), custom_call_target="tpu_custom_call" | custom-call | bytes 25165824 | tf_op jit(solution)/shard_map/pallas_call | solution.py:282
  22.2 4.5 %copy-done.1 = bf16[3072,2048]{1,0:T(8,128)(2,1)} copy-done((bf16[3072,2048]{1,0:T(8,128)(2,1)}, bf16[3072,2048]{1,0:T(8,128)(2,1)S(1)}, u32[]{:S(2)}) %copy-start.1) | copy-done | bytes 12582936
  26.7 2.5 %shard_map.103 = bf16[2,16,128,256]{3,2,1,0:T(8,128)(2,1)} custom-call(bf16[128,4096]{1,0:T(8,128)(2,1)} %refs_0_.2, bf16[128,4096]{1,0:T(8,128)(2,1)} %refs_1_.2), custom_call_target="tpu_custom_call" | custom-call | bytes 4194304 | tf_op jit(solution)/shard_map/pallas_call | solution.py:69
  29.2 0.6 pad_add_fusion.1.place_ref
  29.8 35.6 %all-to-all-done.1.rest_0_ = bf16[32,128,512]{2,1,0:T(8,128)(2,1)} async-done(((bf16[32,128,512]{2,1,0:T(8,128)(2,1)}), bf16[32,128,512]{2,1,0:T(8,128)(2,1)}, u32[]{:S(2)}, u32[]{:S(2)}) %all-to-all-start.1) | async-done | bytes 4194336 | tf_op jit(solution)/shard_map/all_to_all | solution.py:88
  65.4 5.9 %all-to-all-start = ((bf16[32,128,256]{2,1,0:T(8,128)(2,1)}), bf16[32,128,256]{2,1,0:T(8,128)(2,1)S(1)}, u32[]{:S(2)}, u32[]{:S(2)}) async-start(bf16[32,128,256]{2,1,0:T(8,128)(2,1)} %bitcast.5), calls=%async_computation | async-start | bytes 4194304 | tf_op jit(solution)/shard_map/all_to_all | solution.py:88
  71.3 3.1 %slice.13 = bf16[16,128,512]{2,1,0:T(8,128)(2,1)} slice(bf16[32,128,512]{2,1,0:T(8,128)(2,1)} %all-to-all-done.1.rest_0_), slice={[16:32], [0:128], [0:512]} | slice | bytes 4194304 | tf_op jit(solution)/shard_map/slice | solution.py:384
  74.4 1.2 collective-permute-start
  75.9 24.6 %all-to-all-done.q_ref = bf16[32,128,256]{2,1,0:T(8,128)(2,1)S(1)} async-done(((bf16[32,128,256]{2,1,0:T(8,128)(2,1)}), bf16[32,128,256]{2,1,0:T(8,128)(2,1)S(1)}, u32[]{:S(2)}, u32[]{:S(2)}) %all-to-all-start) | async-done | bytes 2097184 | tf_op jit(solution)/shard_map/all_to_all | solution.py:88
  100.5 20.9 %shard_map.106 = (bf16[2,16,64,128]{3,2,1,0:T(8,128)(2,1)S(1)}, bf16[32,128,256]{2,1,0:T(8,128)(2,1)S(1)}) custom-call(s32[2,3]{1,0:T(2,128)S(1)} %get-tuple-element.45.slots_ref, bf16[32,128,256]{2,1,0:T(8,128)(2,1)S(1)} %all-to-all-done.q_ref, bf16[32,128,512]{2,1,0:T(8,128)(2,1)} %all-to-all-done.1.rest_0_), custom_call_target="tpu_custom_call" | custom-call | flops 12884901888 | bytes 8388608 | tf_op jit(solution)/shard_map/pallas_call | solution.py:240
  121.5 2.6 %collective-permute-start.1 = (bf16[2,16,64,128]{3,2,1,0:T(8,128)(2,1)S(1)}, bf16[2,16,64,128]{3,2,1,0:T(8,128)(2,1)S(1)}, u32[]{:S(2)}, u32[]{:S(2)}) collective-permute-start(bf16[2,16,64,128]{3,2,1,0:T(8,128)(2,1)S(1)} %get-tuple-element.29.late), channel_id=1, source_target_pairs={{0,16},{1,17},{2,18},{3,19},{4,20},{5,21},{6,22},{7,23},{8,24},{9,... | collective-permute-start | bytes 1572872 | tf_op jit(solution)/shard_map/ppermute | solution.py:400
  124.1 11.5 %shard_map.107 = (bf16[1,16,64,128]{3,2,1,0:T(8,128)(2,1)S(1)}, bf16[32,128,256]{2,1,0:T(8,128)(2,1)S(1)}) custom-call(s32[2,3]{1,0:T(2,128)S(1)} %get-tuple-element.46.slots_ref, bf16[32,128,256]{2,1,0:T(8,128)(2,1)S(1)} %all-to-all-done.q_ref, bf16[32,128,512]{2,1,0:T(8,128)(2,1)} %all-to-all-done.1.rest_0_, ...), custom_call_target="tpu_custom_call", output_to_operand_aliasing={{1}: (4, {})} | custom-call | flops 6442450944 | bytes 8388608 | tf_op jit(solution)/shard_map/pallas_call | solution.py:240
  135.6 1.3 collective-permute-start.2
  136.9 11.5 %shard_map.108 = (bf16[1,16,64,128]{3,2,1,0:T(8,128)(2,1)S(1)}, bf16[32,128,256]{2,1,0:T(8,128)(2,1)S(1)}) custom-call(s32[2,3]{1,0:T(2,128)S(1)} %get-tuple-element.46.slots_ref, bf16[32,128,256]{2,1,0:T(8,128)(2,1)S(1)} %all-to-all-done.q_ref, bf16[32,128,512]{2,1,0:T(8,128)(2,1)} %all-to-all-done.1.rest_0_, ...), custom_call_target="tpu_custom_call", output_to_operand_aliasing={{1}: (4, {})} | custom-call | flops 6442450944 | bytes 8388608 | tf_op jit(solution)/shard_map/pallas_call | solution.py:240
  148.4 1.3 copy-done.2
  149.7 1.3 collective-permute-start.3
  151.0 7.9 %collective-permute-done.3.got_b = bf16[1,16,64,128]{3,2,1,0:T(8,128)(2,1)S(1)} collective-permute-done((bf16[1,16,64,128]{3,2,1,0:T(8,128)(2,1)S(1)}, bf16[1,16,64,128]{3,2,1,0:T(8,128)(2,1)S(1)}, u32[]{:S(2)}, u32[]{:S(2)}) %collective-permute-start.3) | collective-permute-done | bytes 262176 | tf_op jit(solution)/shard_map/ppermute | solution.py:403
  158.9 0.7 copy-done.8
  159.6 7.3 %all-to-all-start.2 = ((bf16[32,128,256]{2,1,0:T(8,128)(2,1)}), bf16[32,128,256]{2,1,0:T(8,128)(2,1)S(1)}, u32[]{:S(2)}, u32[]{:S(2)}) async-start(bf16[32,128,256]{2,1,0:T(8,128)(2,1)} %copy-done.2), calls=%async_computation.2 | async-start | bytes 4194304 | tf_op jit(solution)/shard_map/all_to_all | solution.py:405
  166.8 8.9 %shard_map.110 = (bf16[384,256]{1,0:T(8,128)(2,1)}, bf16[384,256]{1,0:T(8,128)(2,1)}, bf16[384,256]{1,0:T(8,128)(2,1)}, bf16[384,256]{1,0:T(8,128)(2,1)}, bf16[3...) custom-call(s32[2]{0:T(128)} %pad_add_fusion.1.place_ref, ...), custom_call_target="tpu_custom_call" | custom-call | flops 3221225472 | bytes 15728640 | tf_op jit(solution)/shard_map/pallas_call | solution.py:356
  175.8 2.7 %collective-permute-start.4 = (bf16[384,256]{1,0:T(8,128)(2,1)}, bf16[384,256]{1,0:T(8,128)(2,1)S(1)}, u32[]{:S(2)}, u32[]{:S(2)}) collective-permute-start(bf16[384,256]{1,0:T(8,128)(2,1)} %get-tuple-element.37), channel_id=1, source_target_pairs={{0,80},{16,64},{32,112},{48,96},{64,16},{80,0},{96,48},{112,32},{1... | collective-permute-start | bytes 589832 | tf_op jit(solution)/shard_map/ppermute | solution.py:414
  178.6 3.5 %collective-permute-start.6 = (bf16[384,256]{1,0:T(8,128)(2,1)}, bf16[384,256]{1,0:T(8,128)(2,1)S(1)}, u32[]{:S(2)}, u32[]{:S(2)}) collective-permute-start(bf16[384,256]{1,0:T(8,128)(2,1)} %get-tuple-element.39), channel_id=1, source_target_pairs={{0,112},{16,96},{32,16},{48,0},{64,48},{80,32},{96,80},{112,64},{1... | collective-permute-start | bytes 589832 | tf_op jit(solution)/shard_map/ppermute | solution.py:414
  182.2 0.2 collective-permute-start.8
  182.4 6.1 %collective-permute-done.4 = bf16[384,256]{1,0:T(8,128)(2,1)S(1)} collective-permute-done((bf16[384,256]{1,0:T(8,128)(2,1)}, bf16[384,256]{1,0:T(8,128)(2,1)S(1)}, u32[]{:S(2)}, u32[]{:S(2)}) %collective-permute-start.4) | collective-permute-done | bytes 196640 | tf_op jit(solution)/shard_map/ppermute | solution.py:414
  188.5 1.6 collective-permute-start.9
  190.1 10.9 %collective-permute-done.5 = bf16[384,256]{1,0:T(8,128)(2,1)S(1)} collective-permute-done((bf16[384,256]{1,0:T(8,128)(2,1)}, bf16[384,256]{1,0:T(8,128)(2,1)S(1)}, u32[]{:S(2)}, u32[]{:S(2)}) %collective-permute-start.5) | collective-permute-done | bytes 196640 | tf_op jit(solution)/shard_map/ppermute | solution.py:414
  201.0 1.3 collective-permute-start.10
  202.2 6.2 %collective-permute-done.7 = bf16[384,256]{1,0:T(8,128)(2,1)S(1)} collective-permute-done((bf16[384,256]{1,0:T(8,128)(2,1)}, bf16[384,256]{1,0:T(8,128)(2,1)S(1)}, u32[]{:S(2)}, u32[]{:S(2)}) %collective-permute-start.7) | collective-permute-done | bytes 196640 | tf_op jit(solution)/shard_map/ppermute | solution.py:414
  208.5 1.9 convert_add_fusion
  210.4 2.0 shard_map.109
  (31 shorter events, 0.5 us)
Async XLA Ops:
  0.6 75.0 %copy-start = (s32[16,2]{0,1:T(2,128)S(1)}, s32[16,2]{0,1:T(2,128)}, u32[]{:S(2)}) copy-start(s32[16,2]{0,1:T(2,128)} %param.14) | copy-start | bytes 388
  4.1 61.4 %all-to-all-start.1 = ((bf16[32,128,512]{2,1,0:T(8,128)(2,1)}), bf16[32,128,512]{2,1,0:T(8,128)(2,1)}, u32[]{:S(2)}, u32[]{:S(2)}) async-start(bf16[32,128,512]{2,1,0:T(8,128)(2,1)} %bitcast.4), calls=%async_computation.1 | async-start | bytes 8388608 | tf_op jit(solution)/shard_map/all_to_all | solution.py:88
  22.2 4.5 %copy-start.1 = (bf16[3072,2048]{1,0:T(8,128)(2,1)}, bf16[3072,2048]{1,0:T(8,128)(2,1)S(1)}, u32[]{:S(2)}) copy-start(bf16[3072,2048]{1,0:T(8,128)(2,1)S(1)} %shard_map.104.cot_ref) | copy-start | bytes 37748740
  65.4 35.1 %all-to-all-start = ((bf16[32,128,256]{2,1,0:T(8,128)(2,1)}), bf16[32,128,256]{2,1,0:T(8,128)(2,1)S(1)}, u32[]{:S(2)}, u32[]{:S(2)}) async-start(bf16[32,128,256]{2,1,0:T(8,128)(2,1)} %bitcast.5), calls=%async_computation | async-start | bytes 4194304 | tf_op jit(solution)/shard_map/all_to_all | solution.py:88
  74.4 49.7 %collective-permute-start = (bf16[16,128,512]{2,1,0:T(8,128)(2,1)}, bf16[16,128,512]{2,1,0:T(8,128)(2,1)}, u32[]{:S(2)}, u32[]{:S(2)}) collective-permute-start(bf16[16,128,512]{2,1,0:T(8,128)(2,1)} %slice.13), channel_id=1, source_target_pairs={{0,32},{32,64},{64,96},{96,0},{1,33},{33,65},{65,97},{97,1},{2,34}... | collective-permute-start | bytes 6291464 | tf_op jit(solution)/shard_map/ppermute | solution.py:384
  121.5 14.1 %copy-start.3 = (bf16[2,16,64,128]{3,2,1,0:T(8,128)(2,1)}, bf16[2,16,64,128]{3,2,1,0:T(8,128)(2,1)S(1)}, u32[]{:S(2)}) copy-start(bf16[2,16,64,128]{3,2,1,0:T(8,128)(2,1)S(1)} %get-tuple-element.29.late) | copy-start | bytes 1572868
  121.5 28.2 %collective-permute-start.1 = (bf16[2,16,64,128]{3,2,1,0:T(8,128)(2,1)S(1)}, bf16[2,16,64,128]{3,2,1,0:T(8,128)(2,1)S(1)}, u32[]{:S(2)}, u32[]{:S(2)}) collective-permute-start(bf16[2,16,64,128]{3,2,1,0:T(8,128)(2,1)S(1)} %get-tuple-element.29.late), channel_id=1, source_target_pairs={{0,16},{1,17},{2,18},{3,19},{4,20},{5,21},{6,22},{7,23},{8,24},{9,... | collective-permute-start | bytes 1572872 | tf_op jit(solution)/shard_map/ppermute | solution.py:400
  135.6 12.8 %copy-start.4 = (bf16[1,16,64,128]{3,2,1,0:T(8,128)(2,1)}, bf16[1,16,64,128]{3,2,1,0:T(8,128)(2,1)S(1)}, u32[]{:S(2)}) copy-start(bf16[1,16,64,128]{3,2,1,0:T(8,128)(2,1)S(1)} %get-tuple-element.30.early_a) | copy-start | bytes 786436
  135.6 14.1 %collective-permute-start.2 = (bf16[1,16,64,128]{3,2,1,0:T(8,128)(2,1)S(1)}, bf16[1,16,64,128]{3,2,1,0:T(8,128)(2,1)S(1)}, u32[]{:S(2)}, u32[]{:S(2)}) collective-permute-start(bf16[1,16,64,128]{3,2,1,0:T(8,128)(2,1)S(1)} %get-tuple-element.30.early_a), channel_id=1, source_target_pairs={{16,0},{17,1},{18,2},{19,3},{20,4},{21,5},{22,6},{23,7},{24,8},{25... | collective-permute-start | bytes 786440 | tf_op jit(solution)/shard_map/ppermute | solution.py:401
  148.4 1.3 copy-start.2
  149.7 9.2 %copy-start.5 = (bf16[1,16,64,128]{3,2,1,0:T(8,128)(2,1)}, bf16[1,16,64,128]{3,2,1,0:T(8,128)(2,1)S(1)}, u32[]{:S(2)}) copy-start(bf16[1,16,64,128]{3,2,1,0:T(8,128)(2,1)S(1)} %get-tuple-element.31.early_b) | copy-start | bytes 786436
  149.7 9.2 %copy-start.6 = (bf16[2,16,64,128]{3,2,1,0:T(8,128)(2,1)}, bf16[2,16,64,128]{3,2,1,0:T(8,128)(2,1)S(1)}, u32[]{:S(2)}) copy-start(bf16[2,16,64,128]{3,2,1,0:T(8,128)(2,1)S(1)} %collective-permute-done.1.got_late) | copy-start | bytes 1572868
  149.7 9.2 %copy-start.7 = (bf16[1,16,64,128]{3,2,1,0:T(8,128)(2,1)}, bf16[1,16,64,128]{3,2,1,0:T(8,128)(2,1)S(1)}, u32[]{:S(2)}) copy-start(bf16[1,16,64,128]{3,2,1,0:T(8,128)(2,1)S(1)} %collective-permute-done.2.got_a) | copy-start | bytes 786436
  149.7 9.2 %collective-permute-start.3 = (bf16[1,16,64,128]{3,2,1,0:T(8,128)(2,1)S(1)}, bf16[1,16,64,128]{3,2,1,0:T(8,128)(2,1)S(1)}, u32[]{:S(2)}, u32[]{:S(2)}) collective-permute-start(bf16[1,16,64,128]{3,2,1,0:T(8,128)(2,1)S(1)} %get-tuple-element.31.early_b), channel_id=1, source_target_pairs={{16,0},{17,1},{18,2},{19,3},{20,4},{21,5},{22,6},{23,7},{24,8},{25... | collective-permute-start | bytes 786440 | tf_op jit(solution)/shard_map/ppermute | solution.py:403
  158.9 0.7 copy-start.8
  159.6 50.8 %all-to-all-start.2 = ((bf16[32,128,256]{2,1,0:T(8,128)(2,1)}), bf16[32,128,256]{2,1,0:T(8,128)(2,1)S(1)}, u32[]{:S(2)}, u32[]{:S(2)}) async-start(bf16[32,128,256]{2,1,0:T(8,128)(2,1)} %copy-done.2), calls=%async_computation.2 | async-start | bytes 4194304 | tf_op jit(solution)/shard_map/all_to_all | solution.py:405
  175.8 12.7 %collective-permute-start.4 = (bf16[384,256]{1,0:T(8,128)(2,1)}, bf16[384,256]{1,0:T(8,128)(2,1)S(1)}, u32[]{:S(2)}, u32[]{:S(2)}) collective-permute-start(bf16[384,256]{1,0:T(8,128)(2,1)} %get-tuple-element.37), channel_id=1, source_target_pairs={{0,80},{16,64},{32,112},{48,96},{64,16},{80,0},{96,48},{112,32},{1... | collective-permute-start | bytes 589832 | tf_op jit(solution)/shard_map/ppermute | solution.py:414
  178.5 22.5 %collective-permute-start.5 = (bf16[384,256]{1,0:T(8,128)(2,1)}, bf16[384,256]{1,0:T(8,128)(2,1)S(1)}, u32[]{:S(2)}, u32[]{:S(2)}) collective-permute-start(bf16[384,256]{1,0:T(8,128)(2,1)} %get-tuple-element.38), channel_id=1, source_target_pairs={{0,48},{16,32},{32,80},{48,64},{64,112},{80,96},{96,16},{112,0},{1... | collective-permute-start | bytes 589832 | tf_op jit(solution)/shard_map/ppermute | solution.py:414
  178.6 23.6 %collective-permute-start.6 = (bf16[384,256]{1,0:T(8,128)(2,1)}, bf16[384,256]{1,0:T(8,128)(2,1)S(1)}, u32[]{:S(2)}, u32[]{:S(2)}) collective-permute-start(bf16[384,256]{1,0:T(8,128)(2,1)} %get-tuple-element.39), channel_id=1, source_target_pairs={{0,112},{16,96},{32,16},{48,0},{64,48},{80,32},{96,80},{112,64},{1... | collective-permute-start | bytes 589832 | tf_op jit(solution)/shard_map/ppermute | solution.py:414
  182.1 26.4 %collective-permute-start.7 = (bf16[384,256]{1,0:T(8,128)(2,1)}, bf16[384,256]{1,0:T(8,128)(2,1)S(1)}, u32[]{:S(2)}, u32[]{:S(2)}) collective-permute-start(bf16[384,256]{1,0:T(8,128)(2,1)} %get-tuple-element.40), channel_id=1, source_target_pairs={{0,16},{16,0},{32,48},{48,32},{64,80},{80,64},{96,112},{112,96},{1... | collective-permute-start | bytes 589832 | tf_op jit(solution)/shard_map/ppermute | solution.py:414
  182.2 26.3 %collective-permute-start.8 = (bf16[384,256]{1,0:T(8,128)(2,1)}, bf16[384,256]{1,0:T(8,128)(2,1)S(1)}, u32[]{:S(2)}, u32[]{:S(2)}) collective-permute-start(bf16[384,256]{1,0:T(8,128)(2,1)} %get-tuple-element.41), channel_id=1, source_target_pairs={{0,64},{16,80},{32,96},{48,112},{64,0},{80,16},{96,32},{112,48},{1... | collective-permute-start | bytes 589832 | tf_op jit(solution)/shard_map/ppermute | solution.py:414
  188.5 20.0 %collective-permute-start.9 = (bf16[384,256]{1,0:T(8,128)(2,1)}, bf16[384,256]{1,0:T(8,128)(2,1)S(1)}, u32[]{:S(2)}, u32[]{:S(2)}) collective-permute-start(bf16[384,256]{1,0:T(8,128)(2,1)} %get-tuple-element.42), channel_id=1, source_target_pairs={{0,32},{16,48},{32,64},{48,80},{64,96},{80,112},{96,0},{112,16},{1... | collective-permute-start | bytes 589832 | tf_op jit(solution)/shard_map/ppermute | solution.py:414
  201.0 7.5 %collective-permute-start.10 = (bf16[384,256]{1,0:T(8,128)(2,1)}, bf16[384,256]{1,0:T(8,128)(2,1)S(1)}, u32[]{:S(2)}, u32[]{:S(2)}) collective-permute-start(bf16[384,256]{1,0:T(8,128)(2,1)} %get-tuple-element.43), channel_id=1, source_target_pairs={{0,96},{16,112},{32,0},{48,16},{64,32},{80,48},{96,64},{112,80},{1... | collective-permute-start | bytes 589832 | tf_op jit(solution)/shard_map/ppermute | solution.py:414

commit v10 on v8

--- a/solution.py
+++ b/solution.py
@@ -407,8 +407,8 @@
         place, (early1, early2, got1, got2, late, got_late), columns
     )
     arrived = []
-    for n, term in enumerate(terms):
-        dx, dz = HOPS[n // 2], n % 2
+    for dx, dz in ((2, 0), (1, 0), (2, 1), (1, 1), (3, 1), (0, 1), (3, 0), (0, 0)):
+        term = terms[2 * HOPS.index(dx) + dz]
         ring = [(2 * x + z, 2 * ((x + dx) % 4) + (z ^ dz)) for x in range(4) for z in range(2)]
         arrived.append(term if (dx, dz) == (0, 0) else lax.ppermute(term, CLIPS, ring))
     rows, arrived = lax.optimization_barrier((unpack(back), arrived))

time: 211 us -> 211 us (level)
    ppermute x7, waiting for transfers between devices: 8.84 us -> 6.4 us  [on_device(): lax.ppermute(term, CLIPS, ring)]
    all_to_all x1, waiting for transfers between devices: 12.6 us -> 14.9 us  [on_device(): back = lax.all_to_all(sent, PLANE, 0, 0, tiled=True)]
  transfers between devices with their start and end apart: 14 -> 14, of which waited for: 7 -> 6; matrix products, arithmetic and copies ran while one was open for 2% -> 2% of each run, Pallas kernels for 31% -> 31%
where the time goes in v10:
time: 211 us; the launch traced here: 210 us
  waiting for transfers between devices  89.3 us (42%)
  Pallas kernels  69.2 us (33%)
  starting transfers between devices  38.6 us (18%)
  local copies, waits for them, and re-layouts  9.81 us (5%)
  other arithmetic  2.64 us (1%)
    all_to_all x2, waiting for transfers between devices, to_heads(): return lax.all_to_all(sent, PLANE, 0, 0, tiled=True)  60.1 us
    pallas_call x3, Pallas kernels, attend(): pl.pallas_call(functools.partial(attend_kernel, loads=loads, sources=len(...  43.9 us
    all_to_all x2, starting transfers between devices, to_heads(): return lax.all_to_all(sent, PLANE, 0, 0, tiled=True)  15.5 us
    all_to_all x1, waiting for transfers between devices, on_device(): back = lax.all_to_all(sent, PLANE, 0, 0, tiled=True)  14.9 us
    ppermute x7, starting transfers between devices, on_device(): lax.ppermute(term, CLIPS, ring)  9.37 us
    pallas_call x1, Pallas kernels, grad_terms(): pl.pallas_call(grad_kernel, out_shape=[jax.ShapeDtypeStruct((width, 2 * H...  8.9 us
    pallas_call x1, Pallas kernels, turned(): pl.pallas_call(turn_kernel, out_shape=jax.ShapeDtypeStruct((columns, rows...  8.43 us
    ppermute x1, waiting for transfers between devices, on_device(): got2 = lax.ppermute(last, 'zl', [(1, 0)])  7.86 us
  transfers between devices with their start and end apart: 14, of which 6 were waited for; matrix products, arithmetic and copies ran while one was open for 2% of the time, Pallas kernels for 31%

profile of v10, /device:TPU:1, one launch (start us, length us, event | category | flops | bytes accessed | tf_op | source)
XLA Modules:
  0.0 210.4 jit_solution(7380044219125331562)
XLA Ops:
  0.6 3.4 %shard_map.105 = bf16[2,16,128,512]{3,2,1,0:T(8,128)(2,1)} custom-call(bf16[128,4096]{1,0:T(8,128)(2,1)} %refs_0_.3, bf16[128,4096]{1,0:T(8,128)(2,1)} %refs_1_.3, bf16[128,4096]{1,0:T(8,128)(2,1)} %refs_2_.1, bf16[128,4096]{1,0:T(8,128)(2,1)} %refs_3_.1), custom_call_target="tpu_custom_call" | custom-call | bytes 8388608 | tf_op jit(solution)/shard_map/pallas_call | solution.py:69
  4.1 9.7 %all-to-all-start.1 = ((bf16[32,128,512]{2,1,0:T(8,128)(2,1)}), bf16[32,128,512]{2,1,0:T(8,128)(2,1)}, u32[]{:S(2)}, u32[]{:S(2)}) async-start(bf16[32,128,512]{2,1,0:T(8,128)(2,1)} %bitcast.4), calls=%async_computation.1 | async-start | bytes 8388608 | tf_op jit(solution)/shard_map/all_to_all | solution.py:88
  13.7 8.4 %shard_map.104.cot_ref = bf16[3072,2048]{1,0:T(8,128)(2,1)S(1)} custom-call(bf16[2048,3072]{1,0:T(8,128)(2,1)} %ref.1), custom_call_target="tpu_custom_call" | custom-call | bytes 25165824 | tf_op jit(solution)/shard_map/pallas_call | solution.py:282
  22.2 4.5 %copy-done.1 = bf16[3072,2048]{1,0:T(8,128)(2,1)} copy-done((bf16[3072,2048]{1,0:T(8,128)(2,1)}, bf16[3072,2048]{1,0:T(8,128)(2,1)S(1)}, u32[]{:S(2)}) %copy-start.1) | copy-done | bytes 12582936
  26.7 2.5 %shard_map.103 = bf16[2,16,128,256]{3,2,1,0:T(8,128)(2,1)} custom-call(bf16[128,4096]{1,0:T(8,128)(2,1)} %refs_0_.2, bf16[128,4096]{1,0:T(8,128)(2,1)} %refs_1_.2), custom_call_target="tpu_custom_call" | custom-call | bytes 4194304 | tf_op jit(solution)/shard_map/pallas_call | solution.py:69
  29.2 0.7 pad_add_fusion.1.place_ref
  29.9 35.5 %all-to-all-done.1.rest_0_ = bf16[32,128,512]{2,1,0:T(8,128)(2,1)} async-done(((bf16[32,128,512]{2,1,0:T(8,128)(2,1)}), bf16[32,128,512]{2,1,0:T(8,128)(2,1)}, u32[]{:S(2)}, u32[]{:S(2)}) %all-to-all-start.1) | async-done | bytes 4194336 | tf_op jit(solution)/shard_map/all_to_all | solution.py:88
  65.4 5.9 %all-to-all-start = ((bf16[32,128,256]{2,1,0:T(8,128)(2,1)}), bf16[32,128,256]{2,1,0:T(8,128)(2,1)S(1)}, u32[]{:S(2)}, u32[]{:S(2)}) async-start(bf16[32,128,256]{2,1,0:T(8,128)(2,1)} %bitcast.5), calls=%async_computation | async-start | bytes 4194304 | tf_op jit(solution)/shard_map/all_to_all | solution.py:88
  71.3 3.1 %slice.13 = bf16[16,128,512]{2,1,0:T(8,128)(2,1)} slice(bf16[32,128,512]{2,1,0:T(8,128)(2,1)} %all-to-all-done.1.rest_0_), slice={[16:32], [0:128], [0:512]} | slice | bytes 4194304 | tf_op jit(solution)/shard_map/slice | solution.py:384
  74.4 1.2 collective-permute-start
  75.9 24.6 %all-to-all-done.q_ref = bf16[32,128,256]{2,1,0:T(8,128)(2,1)S(1)} async-done(((bf16[32,128,256]{2,1,0:T(8,128)(2,1)}), bf16[32,128,256]{2,1,0:T(8,128)(2,1)S(1)}, u32[]{:S(2)}, u32[]{:S(2)}) %all-to-all-start) | async-done | bytes 2097184 | tf_op jit(solution)/shard_map/all_to_all | solution.py:88
  100.5 20.9 %shard_map.106 = (bf16[2,16,64,128]{3,2,1,0:T(8,128)(2,1)S(1)}, bf16[32,128,256]{2,1,0:T(8,128)(2,1)S(1)}) custom-call(s32[2,3]{1,0:T(2,128)S(1)} %get-tuple-element.65.slots_ref, bf16[32,128,256]{2,1,0:T(8,128)(2,1)S(1)} %all-to-all-done.q_ref, bf16[32,128,512]{2,1,0:T(8,128)(2,1)} %all-to-all-done.1.rest_0_), custom_call_target="tpu_custom_call" | custom-call | flops 12884901888 | bytes 8388608 | tf_op jit(solution)/shard_map/pallas_call | solution.py:240
  121.4 2.6 %collective-permute-start.1 = (bf16[2,16,64,128]{3,2,1,0:T(8,128)(2,1)S(1)}, bf16[2,16,64,128]{3,2,1,0:T(8,128)(2,1)S(1)}, u32[]{:S(2)}, u32[]{:S(2)}) collective-permute-start(bf16[2,16,64,128]{3,2,1,0:T(8,128)(2,1)S(1)} %get-tuple-element.39.late), channel_id=1, source_target_pairs={{0,16},{1,17},{2,18},{3,19},{4,20},{5,21},{6,22},{7,23},{8,24},{9,... | collective-permute-start | bytes 1572872 | tf_op jit(solution)/shard_map/ppermute | solution.py:400
  124.1 11.5 %shard_map.107 = (bf16[1,16,64,128]{3,2,1,0:T(8,128)(2,1)S(1)}, bf16[32,128,256]{2,1,0:T(8,128)(2,1)S(1)}) custom-call(s32[2,3]{1,0:T(2,128)S(1)} %get-tuple-element.66.slots_ref, bf16[32,128,256]{2,1,0:T(8,128)(2,1)S(1)} %all-to-all-done.q_ref, bf16[32,128,512]{2,1,0:T(8,128)(2,1)} %all-to-all-done.1.rest_0_, ...), custom_call_target="tpu_custom_call", output_to_operand_aliasing={{1}: (4, {})} | custom-call | flops 6442450944 | bytes 8388608 | tf_op jit(solution)/shard_map/pallas_call | solution.py:240
  135.6 1.3 collective-permute-start.2
  136.9 11.5 %shard_map.108 = (bf16[1,16,64,128]{3,2,1,0:T(8,128)(2,1)S(1)}, bf16[32,128,256]{2,1,0:T(8,128)(2,1)S(1)}) custom-call(s32[2,3]{1,0:T(2,128)S(1)} %get-tuple-element.66.slots_ref, bf16[32,128,256]{2,1,0:T(8,128)(2,1)S(1)} %all-to-all-done.q_ref, bf16[32,128,512]{2,1,0:T(8,128)(2,1)} %all-to-all-done.1.rest_0_, ...), custom_call_target="tpu_custom_call", output_to_operand_aliasing={{1}: (4, {})} | custom-call | flops 6442450944 | bytes 8388608 | tf_op jit(solution)/shard_map/pallas_call | solution.py:240
  148.4 1.3 copy-done.2
  149.7 1.3 collective-permute-start.3
  151.0 7.9 %collective-permute-done.3.got_b = bf16[1,16,64,128]{3,2,1,0:T(8,128)(2,1)S(1)} collective-permute-done((bf16[1,16,64,128]{3,2,1,0:T(8,128)(2,1)S(1)}, bf16[1,16,64,128]{3,2,1,0:T(8,128)(2,1)S(1)}, u32[]{:S(2)}, u32[]{:S(2)}) %collective-permute-start.3) | collective-permute-done | bytes 262176 | tf_op jit(solution)/shard_map/ppermute | solution.py:403
  158.9 0.7 copy-done.8
  159.6 7.3 %all-to-all-start.2 = ((bf16[32,128,256]{2,1,0:T(8,128)(2,1)}), bf16[32,128,256]{2,1,0:T(8,128)(2,1)S(1)}, u32[]{:S(2)}, u32[]{:S(2)}) async-start(bf16[32,128,256]{2,1,0:T(8,128)(2,1)} %copy-done.2), calls=%async_computation.2 | async-start | bytes 4194304 | tf_op jit(solution)/shard_map/all_to_all | solution.py:405
  166.9 8.9 %shard_map.110 = (bf16[384,256]{1,0:T(8,128)(2,1)}, bf16[384,256]{1,0:T(8,128)(2,1)}, bf16[384,256]{1,0:T(8,128)(2,1)}, bf16[384,256]{1,0:T(8,128)(2,1)}, bf16[3...) custom-call(s32[2]{0:T(128)} %pad_add_fusion.1.place_ref, ...), custom_call_target="tpu_custom_call" | custom-call | flops 3221225472 | bytes 15728640 | tf_op jit(solution)/shard_map/pallas_call | solution.py:356
  175.8 1.6 collective-permute-start.4
  177.7 2.8 %collective-permute-start.6 = (bf16[384,256]{1,0:T(8,128)(2,1)}, bf16[384,256]{1,0:T(8,128)(2,1)S(1)}, u32[]{:S(2)}, u32[]{:S(2)}) collective-permute-start(bf16[384,256]{1,0:T(8,128)(2,1)} %get-tuple-element.49), channel_id=1, source_target_pairs={{0,80},{16,64},{32,112},{48,96},{64,16},{80,0},{96,48},{112,32},{1... | collective-permute-start | bytes 589832 | tf_op jit(solution)/shard_map/ppermute | solution.py:413
  180.6 1.0 collective-permute-start.7
  181.5 2.6 %collective-permute-start.8 = (bf16[384,256]{1,0:T(8,128)(2,1)}, bf16[384,256]{1,0:T(8,128)(2,1)S(1)}, u32[]{:S(2)}, u32[]{:S(2)}) collective-permute-start(bf16[384,256]{1,0:T(8,128)(2,1)} %get-tuple-element.51), channel_id=1, source_target_pairs={{0,112},{16,96},{32,16},{48,0},{64,48},{80,32},{96,80},{112,64},{1... | collective-permute-start | bytes 589832 | tf_op jit(solution)/shard_map/ppermute | solution.py:413
  184.1 1.0 collective-permute-start.9
  185.2 4.2 %collective-permute-done.5 = bf16[384,256]{1,0:T(8,128)(2,1)S(1)} collective-permute-done((bf16[384,256]{1,0:T(8,128)(2,1)}, bf16[384,256]{1,0:T(8,128)(2,1)S(1)}, u32[]{:S(2)}, u32[]{:S(2)}) %collective-permute-start.5) | collective-permute-done | bytes 196640 | tf_op jit(solution)/shard_map/ppermute | solution.py:413
  189.4 14.9 %all-to-all-done.2.even_ref.odd_ref = bf16[32,128,256]{2,1,0:T(8,128)(2,1)S(1)} async-done(((bf16[32,128,256]{2,1,0:T(8,128)(2,1)}), bf16[32,128,256]{2,1,0:T(8,128)(2,1)S(1)}, u32[]{:S(2)}, u32[]{:S(2)}) %all-to-all-start.2) | async-done | bytes 2097184 | tf_op jit(solution)/shard_map/all_to_all | solution.py:405
  204.3 2.0 shard_map.109
  206.4 2.2 %collective-permute-done.9 = bf16[384,256]{1,0:T(8,128)(2,1)S(1)} collective-permute-done((bf16[384,256]{1,0:T(8,128)(2,1)}, bf16[384,256]{1,0:T(8,128)(2,1)S(1)}, u32[]{:S(2)}, u32[]{:S(2)}) %collective-permute-start.9) | collective-permute-done | bytes 196640 | tf_op jit(solution)/shard_map/ppermute | solution.py:413
  208.5 1.9 convert_add_fusion
  (33 shorter events, 0.7 us)
Async XLA Ops:
  0.6 75.0 %copy-start = (s32[16,2]{0,1:T(2,128)S(1)}, s32[16,2]{0,1:T(2,128)}, u32[]{:S(2)}) copy-start(s32[16,2]{0,1:T(2,128)} %param.14) | copy-start | bytes 388
  4.1 61.4 %all-to-all-start.1 = ((bf16[32,128,512]{2,1,0:T(8,128)(2,1)}), bf16[32,128,512]{2,1,0:T(8,128)(2,1)}, u32[]{:S(2)}, u32[]{:S(2)}) async-start(bf16[32,128,512]{2,1,0:T(8,128)(2,1)} %bitcast.4), calls=%async_computation.1 | async-start | bytes 8388608 | tf_op jit(solution)/shard_map/all_to_all | solution.py:88
  22.2 4.5 %copy-start.1 = (bf16[3072,2048]{1,0:T(8,128)(2,1)}, bf16[3072,2048]{1,0:T(8,128)(2,1)S(1)}, u32[]{:S(2)}) copy-start(bf16[3072,2048]{1,0:T(8,128)(2,1)S(1)} %shard_map.104.cot_ref) | copy-start | bytes 37748740
  65.4 35.1 %all-to-all-start = ((bf16[32,128,256]{2,1,0:T(8,128)(2,1)}), bf16[32,128,256]{2,1,0:T(8,128)(2,1)S(1)}, u32[]{:S(2)}, u32[]{:S(2)}) async-start(bf16[32,128,256]{2,1,0:T(8,128)(2,1)} %bitcast.5), calls=%async_computation | async-start | bytes 4194304 | tf_op jit(solution)/shard_map/all_to_all | solution.py:88
  74.4 49.6 %collective-permute-start = (bf16[16,128,512]{2,1,0:T(8,128)(2,1)}, bf16[16,128,512]{2,1,0:T(8,128)(2,1)}, u32[]{:S(2)}, u32[]{:S(2)}) collective-permute-start(bf16[16,128,512]{2,1,0:T(8,128)(2,1)} %slice.13), channel_id=1, source_target_pairs={{0,32},{32,64},{64,96},{96,0},{1,33},{33,65},{65,97},{97,1},{2,34}... | collective-permute-start | bytes 6291464 | tf_op jit(solution)/shard_map/ppermute | solution.py:384
  121.4 14.1 %copy-start.3 = (bf16[2,16,64,128]{3,2,1,0:T(8,128)(2,1)}, bf16[2,16,64,128]{3,2,1,0:T(8,128)(2,1)S(1)}, u32[]{:S(2)}) copy-start(bf16[2,16,64,128]{3,2,1,0:T(8,128)(2,1)S(1)} %get-tuple-element.39.late) | copy-start | bytes 1572868
  121.4 28.3 %collective-permute-start.1 = (bf16[2,16,64,128]{3,2,1,0:T(8,128)(2,1)S(1)}, bf16[2,16,64,128]{3,2,1,0:T(8,128)(2,1)S(1)}, u32[]{:S(2)}, u32[]{:S(2)}) collective-permute-start(bf16[2,16,64,128]{3,2,1,0:T(8,128)(2,1)S(1)} %get-tuple-element.39.late), channel_id=1, source_target_pairs={{0,16},{1,17},{2,18},{3,19},{4,20},{5,21},{6,22},{7,23},{8,24},{9,... | collective-permute-start | bytes 1572872 | tf_op jit(solution)/shard_map/ppermute | solution.py:400
  135.6 12.8 %copy-start.4 = (bf16[1,16,64,128]{3,2,1,0:T(8,128)(2,1)}, bf16[1,16,64,128]{3,2,1,0:T(8,128)(2,1)S(1)}, u32[]{:S(2)}) copy-start(bf16[1,16,64,128]{3,2,1,0:T(8,128)(2,1)S(1)} %get-tuple-element.40.early_a) | copy-start | bytes 786436
  135.6 14.1 %collective-permute-start.2 = (bf16[1,16,64,128]{3,2,1,0:T(8,128)(2,1)S(1)}, bf16[1,16,64,128]{3,2,1,0:T(8,128)(2,1)S(1)}, u32[]{:S(2)}, u32[]{:S(2)}) collective-permute-start(bf16[1,16,64,128]{3,2,1,0:T(8,128)(2,1)S(1)} %get-tuple-element.40.early_a), channel_id=1, source_target_pairs={{16,0},{17,1},{18,2},{19,3},{20,4},{21,5},{22,6},{23,7},{24,8},{25... | collective-permute-start | bytes 786440 | tf_op jit(solution)/shard_map/ppermute | solution.py:401
  148.4 1.3 copy-start.2
  149.7 9.2 %copy-start.5 = (bf16[1,16,64,128]{3,2,1,0:T(8,128)(2,1)}, bf16[1,16,64,128]{3,2,1,0:T(8,128)(2,1)S(1)}, u32[]{:S(2)}) copy-start(bf16[1,16,64,128]{3,2,1,0:T(8,128)(2,1)S(1)} %get-tuple-element.41.early_b) | copy-start | bytes 786436
  149.7 9.2 %copy-start.6 = (bf16[2,16,64,128]{3,2,1,0:T(8,128)(2,1)}, bf16[2,16,64,128]{3,2,1,0:T(8,128)(2,1)S(1)}, u32[]{:S(2)}) copy-start(bf16[2,16,64,128]{3,2,1,0:T(8,128)(2,1)S(1)} %collective-permute-done.1.got_late) | copy-start | bytes 1572868
  149.7 9.2 %copy-start.7 = (bf16[1,16,64,128]{3,2,1,0:T(8,128)(2,1)}, bf16[1,16,64,128]{3,2,1,0:T(8,128)(2,1)S(1)}, u32[]{:S(2)}) copy-start(bf16[1,16,64,128]{3,2,1,0:T(8,128)(2,1)S(1)} %collective-permute-done.2.got_a) | copy-start | bytes 786436
  149.7 9.2 %collective-permute-start.3 = (bf16[1,16,64,128]{3,2,1,0:T(8,128)(2,1)S(1)}, bf16[1,16,64,128]{3,2,1,0:T(8,128)(2,1)S(1)}, u32[]{:S(2)}, u32[]{:S(2)}) collective-permute-start(bf16[1,16,64,128]{3,2,1,0:T(8,128)(2,1)S(1)} %get-tuple-element.41.early_b), channel_id=1, source_target_pairs={{16,0},{17,1},{18,2},{19,3},{20,4},{21,5},{22,6},{23,7},{24,8},{25... | collective-permute-start | bytes 786440 | tf_op jit(solution)/shard_map/ppermute | solution.py:403
  158.9 0.7 copy-start.8
  159.6 44.7 %all-to-all-start.2 = ((bf16[32,128,256]{2,1,0:T(8,128)(2,1)}), bf16[32,128,256]{2,1,0:T(8,128)(2,1)S(1)}, u32[]{:S(2)}, u32[]{:S(2)}) async-start(bf16[32,128,256]{2,1,0:T(8,128)(2,1)} %copy-done.2), calls=%async_computation.2 | async-start | bytes 4194304 | tf_op jit(solution)/shard_map/all_to_all | solution.py:405
  175.8 8.4 %collective-permute-start.4 = (bf16[384,256]{1,0:T(8,128)(2,1)}, bf16[384,256]{1,0:T(8,128)(2,1)S(1)}, u32[]{:S(2)}, u32[]{:S(2)}) collective-permute-start(bf16[384,256]{1,0:T(8,128)(2,1)} %get-tuple-element.47), channel_id=1, source_target_pairs={{0,64},{16,80},{32,96},{48,112},{64,0},{80,16},{96,32},{112,48},{1... | collective-permute-start | bytes 589832 | tf_op jit(solution)/shard_map/ppermute | solution.py:413
  177.4 12.0 %collective-permute-start.5 = (bf16[384,256]{1,0:T(8,128)(2,1)}, bf16[384,256]{1,0:T(8,128)(2,1)S(1)}, u32[]{:S(2)}, u32[]{:S(2)}) collective-permute-start(bf16[384,256]{1,0:T(8,128)(2,1)} %get-tuple-element.48), channel_id=1, source_target_pairs={{0,32},{16,48},{32,64},{48,80},{64,96},{80,112},{96,0},{112,16},{1... | collective-permute-start | bytes 589832 | tf_op jit(solution)/shard_map/ppermute | solution.py:413
  177.7 28.6 %collective-permute-start.6 = (bf16[384,256]{1,0:T(8,128)(2,1)}, bf16[384,256]{1,0:T(8,128)(2,1)S(1)}, u32[]{:S(2)}, u32[]{:S(2)}) collective-permute-start(bf16[384,256]{1,0:T(8,128)(2,1)} %get-tuple-element.49), channel_id=1, source_target_pairs={{0,80},{16,64},{32,112},{48,96},{64,16},{80,0},{96,48},{112,32},{1... | collective-permute-start | bytes 589832 | tf_op jit(solution)/shard_map/ppermute | solution.py:413
  180.6 25.8 %collective-permute-start.7 = (bf16[384,256]{1,0:T(8,128)(2,1)}, bf16[384,256]{1,0:T(8,128)(2,1)S(1)}, u32[]{:S(2)}, u32[]{:S(2)}) collective-permute-start(bf16[384,256]{1,0:T(8,128)(2,1)} %get-tuple-element.50), channel_id=1, source_target_pairs={{0,48},{16,32},{32,80},{48,64},{64,112},{80,96},{96,16},{112,0},{1... | collective-permute-start | bytes 589832 | tf_op jit(solution)/shard_map/ppermute | solution.py:413
  181.5 24.8 %collective-permute-start.8 = (bf16[384,256]{1,0:T(8,128)(2,1)}, bf16[384,256]{1,0:T(8,128)(2,1)S(1)}, u32[]{:S(2)}, u32[]{:S(2)}) collective-permute-start(bf16[384,256]{1,0:T(8,128)(2,1)} %get-tuple-element.51), channel_id=1, source_target_pairs={{0,112},{16,96},{32,16},{48,0},{64,48},{80,32},{96,80},{112,64},{1... | collective-permute-start | bytes 589832 | tf_op jit(solution)/shard_map/ppermute | solution.py:413
  184.1 24.4 %collective-permute-start.9 = (bf16[384,256]{1,0:T(8,128)(2,1)}, bf16[384,256]{1,0:T(8,128)(2,1)S(1)}, u32[]{:S(2)}, u32[]{:S(2)}) collective-permute-start(bf16[384,256]{1,0:T(8,128)(2,1)} %get-tuple-element.52), channel_id=1, source_target_pairs={{0,16},{16,0},{32,48},{48,32},{64,80},{80,64},{96,112},{112,96},{1... | collective-permute-start | bytes 589832 | tf_op jit(solution)/shard_map/ppermute | solution.py:413
  189.4 19.1 %copy-start.9 = (bf16[384,256]{1,0:T(8,128)(2,1)S(1)}, bf16[384,256]{1,0:T(8,128)(2,1)}, u32[]{:S(2)}) copy-start(bf16[384,256]{1,0:T(8,128)(2,1)} %get-tuple-element.64) | copy-start | bytes 589828
  189.4 19.1 %collective-permute-start.10 = (bf16[384,256]{1,0:T(8,128)(2,1)}, bf16[384,256]{1,0:T(8,128)(2,1)}, u32[]{:S(2)}, u32[]{:S(2)}) collective-permute-start(bf16[384,256]{1,0:T(8,128)(2,1)} %get-tuple-element.53), channel_id=1, source_target_pairs={{0,96},{16,112},{32,0},{48,16},{64,32},{80,48},{96,64},{112,80},{1... | collective-permute-start | bytes 589832 | tf_op jit(solution)/shard_map/ppermute | solution.py:413

commit v11 on v10

--- a/solution.py
+++ b/solution.py
@@ -331,14 +331,14 @@
         copy.wait()
         if step + 2 < len(reads):
             reads[step + 2].start()
-        for row in range(0, height, 128):
+        for row in range(0, height, 192):
             part = jnp.dot(
-                rows[step, row : row + 128],
+                rows[step, row : row + 192],
                 pair[...].reshape(2 * CLIP, 2 * HDIM),
                 preferred_element_type=f32,
             )
             at = row % (height // 2)
-            parts[step, 2 * row // height, at : at + 128] = part.astype(bf16)
+            parts[step, 2 * row // height, at : at + 192] = part.astype(bf16)
         for dz in range(2):
             n = 2 * step + dz
             writes.append(

time: 211 us -> 211 us (level)
  no operation moved by 1% of the time
where the time goes in v11:
time: 211 us; the launch traced here: 210 us
  waiting for transfers between devices  89.3 us (42%)
  Pallas kernels  69.2 us (33%)
  starting transfers between devices  38.6 us (18%)
  local copies, waits for them, and re-layouts  9.81 us (5%)
  other arithmetic  2.64 us (1%)
    all_to_all x2, waiting for transfers between devices, to_heads(): return lax.all_to_all(sent, PLANE, 0, 0, tiled=True)  60.1 us
    pallas_call x3, Pallas kernels, attend(): pl.pallas_call(functools.partial(attend_kernel, loads=loads, sources=len(...  43.9 us
    all_to_all x2, starting transfers between devices, to_heads(): return lax.all_to_all(sent, PLANE, 0, 0, tiled=True)  15.5 us
    all_to_all x1, waiting for transfers between devices, on_device(): back = lax.all_to_all(sent, PLANE, 0, 0, tiled=True)  14.9 us
    ppermute x7, starting transfers between devices, on_device(): lax.ppermute(term, CLIPS, ring)  9.39 us
    pallas_call x1, Pallas kernels, grad_terms(): pl.pallas_call(grad_kernel, out_shape=[jax.ShapeDtypeStruct((width, 2 * H...  8.92 us
    pallas_call x1, Pallas kernels, turned(): pl.pallas_call(turn_kernel, out_shape=jax.ShapeDtypeStruct((columns, rows...  8.43 us
    ppermute x1, waiting for transfers between devices, on_device(): got2 = lax.ppermute(last, 'zl', [(1, 0)])  7.86 us
  transfers between devices with their start and end apart: 14, of which 6 were waited for; matrix products, arithmetic and copies ran while one was open for 2% of the time, Pallas kernels for 31%

profile of v11, /device:TPU:1, one launch (start us, length us, event | category | flops | bytes accessed | tf_op | source)
XLA Modules:
  0.0 210.4 jit_solution(15973489995296993941)
XLA Ops:
  0.6 3.4 %shard_map.105 = bf16[2,16,128,512]{3,2,1,0:T(8,128)(2,1)} custom-call(bf16[128,4096]{1,0:T(8,128)(2,1)} %refs_0_.3, bf16[128,4096]{1,0:T(8,128)(2,1)} %refs_1_.3, bf16[128,4096]{1,0:T(8,128)(2,1)} %refs_2_.1, bf16[128,4096]{1,0:T(8,128)(2,1)} %refs_3_.1), custom_call_target="tpu_custom_call" | custom-call | bytes 8388608 | tf_op jit(solution)/shard_map/pallas_call | solution.py:69
  4.1 9.7 %all-to-all-start.1 = ((bf16[32,128,512]{2,1,0:T(8,128)(2,1)}), bf16[32,128,512]{2,1,0:T(8,128)(2,1)}, u32[]{:S(2)}, u32[]{:S(2)}) async-start(bf16[32,128,512]{2,1,0:T(8,128)(2,1)} %bitcast.4), calls=%async_computation.1 | async-start | bytes 8388608 | tf_op jit(solution)/shard_map/all_to_all | solution.py:88
  13.7 8.4 %shard_map.104.cot_ref = bf16[3072,2048]{1,0:T(8,128)(2,1)S(1)} custom-call(bf16[2048,3072]{1,0:T(8,128)(2,1)} %ref.1), custom_call_target="tpu_custom_call" | custom-call | bytes 25165824 | tf_op jit(solution)/shard_map/pallas_call | solution.py:282
  22.2 4.5 %copy-done.1 = bf16[3072,2048]{1,0:T(8,128)(2,1)} copy-done((bf16[3072,2048]{1,0:T(8,128)(2,1)}, bf16[3072,2048]{1,0:T(8,128)(2,1)S(1)}, u32[]{:S(2)}) %copy-start.1) | copy-done | bytes 12582936
  26.7 2.5 %shard_map.103 = bf16[2,16,128,256]{3,2,1,0:T(8,128)(2,1)} custom-call(bf16[128,4096]{1,0:T(8,128)(2,1)} %refs_0_.2, bf16[128,4096]{1,0:T(8,128)(2,1)} %refs_1_.2), custom_call_target="tpu_custom_call" | custom-call | bytes 4194304 | tf_op jit(solution)/shard_map/pallas_call | solution.py:69
  29.2 0.7 pad_add_fusion.1.place_ref
  29.9 35.5 %all-to-all-done.1.rest_0_ = bf16[32,128,512]{2,1,0:T(8,128)(2,1)} async-done(((bf16[32,128,512]{2,1,0:T(8,128)(2,1)}), bf16[32,128,512]{2,1,0:T(8,128)(2,1)}, u32[]{:S(2)}, u32[]{:S(2)}) %all-to-all-start.1) | async-done | bytes 4194336 | tf_op jit(solution)/shard_map/all_to_all | solution.py:88
  65.4 5.9 %all-to-all-start = ((bf16[32,128,256]{2,1,0:T(8,128)(2,1)}), bf16[32,128,256]{2,1,0:T(8,128)(2,1)S(1)}, u32[]{:S(2)}, u32[]{:S(2)}) async-start(bf16[32,128,256]{2,1,0:T(8,128)(2,1)} %bitcast.5), calls=%async_computation | async-start | bytes 4194304 | tf_op jit(solution)/shard_map/all_to_all | solution.py:88
  71.3 3.1 %slice.13 = bf16[16,128,512]{2,1,0:T(8,128)(2,1)} slice(bf16[32,128,512]{2,1,0:T(8,128)(2,1)} %all-to-all-done.1.rest_0_), slice={[16:32], [0:128], [0:512]} | slice | bytes 4194304 | tf_op jit(solution)/shard_map/slice | solution.py:384
  74.4 1.2 collective-permute-start
  75.9 24.6 %all-to-all-done.q_ref = bf16[32,128,256]{2,1,0:T(8,128)(2,1)S(1)} async-done(((bf16[32,128,256]{2,1,0:T(8,128)(2,1)}), bf16[32,128,256]{2,1,0:T(8,128)(2,1)S(1)}, u32[]{:S(2)}, u32[]{:S(2)}) %all-to-all-start) | async-done | bytes 2097184 | tf_op jit(solution)/shard_map/all_to_all | solution.py:88
  100.5 20.9 %shard_map.106 = (bf16[2,16,64,128]{3,2,1,0:T(8,128)(2,1)S(1)}, bf16[32,128,256]{2,1,0:T(8,128)(2,1)S(1)}) custom-call(s32[2,3]{1,0:T(2,128)S(1)} %get-tuple-element.65.slots_ref, bf16[32,128,256]{2,1,0:T(8,128)(2,1)S(1)} %all-to-all-done.q_ref, bf16[32,128,512]{2,1,0:T(8,128)(2,1)} %all-to-all-done.1.rest_0_), custom_call_target="tpu_custom_call" | custom-call | flops 12884901888 | bytes 8388608 | tf_op jit(solution)/shard_map/pallas_call | solution.py:240
  121.4 2.6 %collective-permute-start.1 = (bf16[2,16,64,128]{3,2,1,0:T(8,128)(2,1)S(1)}, bf16[2,16,64,128]{3,2,1,0:T(8,128)(2,1)S(1)}, u32[]{:S(2)}, u32[]{:S(2)}) collective-permute-start(bf16[2,16,64,128]{3,2,1,0:T(8,128)(2,1)S(1)} %get-tuple-element.39.late), channel_id=1, source_target_pairs={{0,16},{1,17},{2,18},{3,19},{4,20},{5,21},{6,22},{7,23},{8,24},{9,... | collective-permute-start | bytes 1572872 | tf_op jit(solution)/shard_map/ppermute | solution.py:400
  124.1 11.5 %shard_map.107 = (bf16[1,16,64,128]{3,2,1,0:T(8,128)(2,1)S(1)}, bf16[32,128,256]{2,1,0:T(8,128)(2,1)S(1)}) custom-call(s32[2,3]{1,0:T(2,128)S(1)} %get-tuple-element.66.slots_ref, bf16[32,128,256]{2,1,0:T(8,128)(2,1)S(1)} %all-to-all-done.q_ref, bf16[32,128,512]{2,1,0:T(8,128)(2,1)} %all-to-all-done.1.rest_0_, ...), custom_call_target="tpu_custom_call", output_to_operand_aliasing={{1}: (4, {})} | custom-call | flops 6442450944 | bytes 8388608 | tf_op jit(solution)/shard_map/pallas_call | solution.py:240
  135.6 1.3 collective-permute-start.2
  136.9 11.5 %shard_map.108 = (bf16[1,16,64,128]{3,2,1,0:T(8,128)(2,1)S(1)}, bf16[32,128,256]{2,1,0:T(8,128)(2,1)S(1)}) custom-call(s32[2,3]{1,0:T(2,128)S(1)} %get-tuple-element.66.slots_ref, bf16[32,128,256]{2,1,0:T(8,128)(2,1)S(1)} %all-to-all-done.q_ref, bf16[32,128,512]{2,1,0:T(8,128)(2,1)} %all-to-all-done.1.rest_0_, ...), custom_call_target="tpu_custom_call", output_to_operand_aliasing={{1}: (4, {})} | custom-call | flops 6442450944 | bytes 8388608 | tf_op jit(solution)/shard_map/pallas_call | solution.py:240
  148.4 1.3 copy-done.2
  149.7 1.3 collective-permute-start.3
  151.0 7.9 %collective-permute-done.3.got_b = bf16[1,16,64,128]{3,2,1,0:T(8,128)(2,1)S(1)} collective-permute-done((bf16[1,16,64,128]{3,2,1,0:T(8,128)(2,1)S(1)}, bf16[1,16,64,128]{3,2,1,0:T(8,128)(2,1)S(1)}, u32[]{:S(2)}, u32[]{:S(2)}) %collective-permute-start.3) | collective-permute-done | bytes 262176 | tf_op jit(solution)/shard_map/ppermute | solution.py:403
  158.9 0.7 copy-done.8
  159.6 7.3 %all-to-all-start.2 = ((bf16[32,128,256]{2,1,0:T(8,128)(2,1)}), bf16[32,128,256]{2,1,0:T(8,128)(2,1)S(1)}, u32[]{:S(2)}, u32[]{:S(2)}) async-start(bf16[32,128,256]{2,1,0:T(8,128)(2,1)} %copy-done.2), calls=%async_computation.2 | async-start | bytes 4194304 | tf_op jit(solution)/shard_map/all_to_all | solution.py:405
  166.9 8.9 %shard_map.110 = (bf16[384,256]{1,0:T(8,128)(2,1)}, bf16[384,256]{1,0:T(8,128)(2,1)}, bf16[384,256]{1,0:T(8,128)(2,1)}, bf16[384,256]{1,0:T(8,128)(2,1)}, bf16[3...) custom-call(s32[2]{0:T(128)} %pad_add_fusion.1.place_ref, ...), custom_call_target="tpu_custom_call" | custom-call | flops 3221225472 | bytes 15728640 | tf_op jit(solution)/shard_map/pallas_call | solution.py:356
  175.8 1.6 collective-permute-start.4
  177.7 2.8 %collective-permute-start.6 = (bf16[384,256]{1,0:T(8,128)(2,1)}, bf16[384,256]{1,0:T(8,128)(2,1)S(1)}, u32[]{:S(2)}, u32[]{:S(2)}) collective-permute-start(bf16[384,256]{1,0:T(8,128)(2,1)} %get-tuple-element.49), channel_id=1, source_target_pairs={{0,80},{16,64},{32,112},{48,96},{64,16},{80,0},{96,48},{112,32},{1... | collective-permute-start | bytes 589832 | tf_op jit(solution)/shard_map/ppermute | solution.py:413
  180.6 1.0 collective-permute-start.7
  181.6 2.6 %collective-permute-start.8 = (bf16[384,256]{1,0:T(8,128)(2,1)}, bf16[384,256]{1,0:T(8,128)(2,1)S(1)}, u32[]{:S(2)}, u32[]{:S(2)}) collective-permute-start(bf16[384,256]{1,0:T(8,128)(2,1)} %get-tuple-element.51), channel_id=1, source_target_pairs={{0,112},{16,96},{32,16},{48,0},{64,48},{80,32},{96,80},{112,64},{1... | collective-permute-start | bytes 589832 | tf_op jit(solution)/shard_map/ppermute | solution.py:413
  184.2 1.0 collective-permute-start.9
  185.2 4.2 %collective-permute-done.5 = bf16[384,256]{1,0:T(8,128)(2,1)S(1)} collective-permute-done((bf16[384,256]{1,0:T(8,128)(2,1)}, bf16[384,256]{1,0:T(8,128)(2,1)S(1)}, u32[]{:S(2)}, u32[]{:S(2)}) %collective-permute-start.5) | collective-permute-done | bytes 196640 | tf_op jit(solution)/shard_map/ppermute | solution.py:413
  189.4 14.9 %all-to-all-done.2.even_ref.odd_ref = bf16[32,128,256]{2,1,0:T(8,128)(2,1)S(1)} async-done(((bf16[32,128,256]{2,1,0:T(8,128)(2,1)}), bf16[32,128,256]{2,1,0:T(8,128)(2,1)S(1)}, u32[]{:S(2)}, u32[]{:S(2)}) %all-to-all-start.2) | async-done | bytes 2097184 | tf_op jit(solution)/shard_map/all_to_all | solution.py:405
  204.3 2.0 shard_map.109
  206.4 2.2 %collective-permute-done.9 = bf16[384,256]{1,0:T(8,128)(2,1)S(1)} collective-permute-done((bf16[384,256]{1,0:T(8,128)(2,1)}, bf16[384,256]{1,0:T(8,128)(2,1)S(1)}, u32[]{:S(2)}, u32[]{:S(2)}) %collective-permute-start.9) | collective-permute-done | bytes 196640 | tf_op jit(solution)/shard_map/ppermute | solution.py:413
  208.5 1.9 convert_add_fusion
  (33 shorter events, 0.7 us)
Async XLA Ops:
  0.6 75.0 %copy-start = (s32[16,2]{0,1:T(2,128)S(1)}, s32[16,2]{0,1:T(2,128)}, u32[]{:S(2)}) copy-start(s32[16,2]{0,1:T(2,128)} %param.14) | copy-start | bytes 388
  4.1 61.4 %all-to-all-start.1 = ((bf16[32,128,512]{2,1,0:T(8,128)(2,1)}), bf16[32,128,512]{2,1,0:T(8,128)(2,1)}, u32[]{:S(2)}, u32[]{:S(2)}) async-start(bf16[32,128,512]{2,1,0:T(8,128)(2,1)} %bitcast.4), calls=%async_computation.1 | async-start | bytes 8388608 | tf_op jit(solution)/shard_map/all_to_all | solution.py:88
  22.2 4.5 %copy-start.1 = (bf16[3072,2048]{1,0:T(8,128)(2,1)}, bf16[3072,2048]{1,0:T(8,128)(2,1)S(1)}, u32[]{:S(2)}) copy-start(bf16[3072,2048]{1,0:T(8,128)(2,1)S(1)} %shard_map.104.cot_ref) | copy-start | bytes 37748740
  65.4 35.1 %all-to-all-start = ((bf16[32,128,256]{2,1,0:T(8,128)(2,1)}), bf16[32,128,256]{2,1,0:T(8,128)(2,1)S(1)}, u32[]{:S(2)}, u32[]{:S(2)}) async-start(bf16[32,128,256]{2,1,0:T(8,128)(2,1)} %bitcast.5), calls=%async_computation | async-start | bytes 4194304 | tf_op jit(solution)/shard_map/all_to_all | solution.py:88
  74.4 49.6 %collective-permute-start = (bf16[16,128,512]{2,1,0:T(8,128)(2,1)}, bf16[16,128,512]{2,1,0:T(8,128)(2,1)}, u32[]{:S(2)}, u32[]{:S(2)}) collective-permute-start(bf16[16,128,512]{2,1,0:T(8,128)(2,1)} %slice.13), channel_id=1, source_target_pairs={{0,32},{32,64},{64,96},{96,0},{1,33},{33,65},{65,97},{97,1},{2,34}... | collective-permute-start | bytes 6291464 | tf_op jit(solution)/shard_map/ppermute | solution.py:384
  121.4 14.1 %copy-start.3 = (bf16[2,16,64,128]{3,2,1,0:T(8,128)(2,1)}, bf16[2,16,64,128]{3,2,1,0:T(8,128)(2,1)S(1)}, u32[]{:S(2)}) copy-start(bf16[2,16,64,128]{3,2,1,0:T(8,128)(2,1)S(1)} %get-tuple-element.39.late) | copy-start | bytes 1572868
  121.4 28.3 %collective-permute-start.1 = (bf16[2,16,64,128]{3,2,1,0:T(8,128)(2,1)S(1)}, bf16[2,16,64,128]{3,2,1,0:T(8,128)(2,1)S(1)}, u32[]{:S(2)}, u32[]{:S(2)}) collective-permute-start(bf16[2,16,64,128]{3,2,1,0:T(8,128)(2,1)S(1)} %get-tuple-element.39.late), channel_id=1, source_target_pairs={{0,16},{1,17},{2,18},{3,19},{4,20},{5,21},{6,22},{7,23},{8,24},{9,... | collective-permute-start | bytes 1572872 | tf_op jit(solution)/shard_map/ppermute | solution.py:400
  135.6 12.8 %copy-start.4 = (bf16[1,16,64,128]{3,2,1,0:T(8,128)(2,1)}, bf16[1,16,64,128]{3,2,1,0:T(8,128)(2,1)S(1)}, u32[]{:S(2)}) copy-start(bf16[1,16,64,128]{3,2,1,0:T(8,128)(2,1)S(1)} %get-tuple-element.40.early_a) | copy-start | bytes 786436
  135.6 14.1 %collective-permute-start.2 = (bf16[1,16,64,128]{3,2,1,0:T(8,128)(2,1)S(1)}, bf16[1,16,64,128]{3,2,1,0:T(8,128)(2,1)S(1)}, u32[]{:S(2)}, u32[]{:S(2)}) collective-permute-start(bf16[1,16,64,128]{3,2,1,0:T(8,128)(2,1)S(1)} %get-tuple-element.40.early_a), channel_id=1, source_target_pairs={{16,0},{17,1},{18,2},{19,3},{20,4},{21,5},{22,6},{23,7},{24,8},{25... | collective-permute-start | bytes 786440 | tf_op jit(solution)/shard_map/ppermute | solution.py:401
  148.4 1.3 copy-start.2
  149.7 9.2 %copy-start.5 = (bf16[1,16,64,128]{3,2,1,0:T(8,128)(2,1)}, bf16[1,16,64,128]{3,2,1,0:T(8,128)(2,1)S(1)}, u32[]{:S(2)}) copy-start(bf16[1,16,64,128]{3,2,1,0:T(8,128)(2,1)S(1)} %get-tuple-element.41.early_b) | copy-start | bytes 786436
  149.7 9.2 %copy-start.6 = (bf16[2,16,64,128]{3,2,1,0:T(8,128)(2,1)}, bf16[2,16,64,128]{3,2,1,0:T(8,128)(2,1)S(1)}, u32[]{:S(2)}) copy-start(bf16[2,16,64,128]{3,2,1,0:T(8,128)(2,1)S(1)} %collective-permute-done.1.got_late) | copy-start | bytes 1572868
  149.7 9.2 %copy-start.7 = (bf16[1,16,64,128]{3,2,1,0:T(8,128)(2,1)}, bf16[1,16,64,128]{3,2,1,0:T(8,128)(2,1)S(1)}, u32[]{:S(2)}) copy-start(bf16[1,16,64,128]{3,2,1,0:T(8,128)(2,1)S(1)} %collective-permute-done.2.got_a) | copy-start | bytes 786436
  149.7 9.2 %collective-permute-start.3 = (bf16[1,16,64,128]{3,2,1,0:T(8,128)(2,1)S(1)}, bf16[1,16,64,128]{3,2,1,0:T(8,128)(2,1)S(1)}, u32[]{:S(2)}, u32[]{:S(2)}) collective-permute-start(bf16[1,16,64,128]{3,2,1,0:T(8,128)(2,1)S(1)} %get-tuple-element.41.early_b), channel_id=1, source_target_pairs={{16,0},{17,1},{18,2},{19,3},{20,4},{21,5},{22,6},{23,7},{24,8},{25... | collective-permute-start | bytes 786440 | tf_op jit(solution)/shard_map/ppermute | solution.py:403
  158.9 0.7 copy-start.8
  159.6 44.7 %all-to-all-start.2 = ((bf16[32,128,256]{2,1,0:T(8,128)(2,1)}), bf16[32,128,256]{2,1,0:T(8,128)(2,1)S(1)}, u32[]{:S(2)}, u32[]{:S(2)}) async-start(bf16[32,128,256]{2,1,0:T(8,128)(2,1)} %copy-done.2), calls=%async_computation.2 | async-start | bytes 4194304 | tf_op jit(solution)/shard_map/all_to_all | solution.py:405
  175.8 8.4 %collective-permute-start.4 = (bf16[384,256]{1,0:T(8,128)(2,1)}, bf16[384,256]{1,0:T(8,128)(2,1)S(1)}, u32[]{:S(2)}, u32[]{:S(2)}) collective-permute-start(bf16[384,256]{1,0:T(8,128)(2,1)} %get-tuple-element.47), channel_id=1, source_target_pairs={{0,64},{16,80},{32,96},{48,112},{64,0},{80,16},{96,32},{112,48},{1... | collective-permute-start | bytes 589832 | tf_op jit(solution)/shard_map/ppermute | solution.py:413
  177.4 12.0 %collective-permute-start.5 = (bf16[384,256]{1,0:T(8,128)(2,1)}, bf16[384,256]{1,0:T(8,128)(2,1)S(1)}, u32[]{:S(2)}, u32[]{:S(2)}) collective-permute-start(bf16[384,256]{1,0:T(8,128)(2,1)} %get-tuple-element.48), channel_id=1, source_target_pairs={{0,32},{16,48},{32,64},{48,80},{64,96},{80,112},{96,0},{112,16},{1... | collective-permute-start | bytes 589832 | tf_op jit(solution)/shard_map/ppermute | solution.py:413
  177.7 28.6 %collective-permute-start.6 = (bf16[384,256]{1,0:T(8,128)(2,1)}, bf16[384,256]{1,0:T(8,128)(2,1)S(1)}, u32[]{:S(2)}, u32[]{:S(2)}) collective-permute-start(bf16[384,256]{1,0:T(8,128)(2,1)} %get-tuple-element.49), channel_id=1, source_target_pairs={{0,80},{16,64},{32,112},{48,96},{64,16},{80,0},{96,48},{112,32},{1... | collective-permute-start | bytes 589832 | tf_op jit(solution)/shard_map/ppermute | solution.py:413
  180.6 25.8 %collective-permute-start.7 = (bf16[384,256]{1,0:T(8,128)(2,1)}, bf16[384,256]{1,0:T(8,128)(2,1)S(1)}, u32[]{:S(2)}, u32[]{:S(2)}) collective-permute-start(bf16[384,256]{1,0:T(8,128)(2,1)} %get-tuple-element.50), channel_id=1, source_target_pairs={{0,48},{16,32},{32,80},{48,64},{64,112},{80,96},{96,16},{112,0},{1... | collective-permute-start | bytes 589832 | tf_op jit(solution)/shard_map/ppermute | solution.py:413
  181.6 24.8 %collective-permute-start.8 = (bf16[384,256]{1,0:T(8,128)(2,1)}, bf16[384,256]{1,0:T(8,128)(2,1)S(1)}, u32[]{:S(2)}, u32[]{:S(2)}) collective-permute-start(bf16[384,256]{1,0:T(8,128)(2,1)} %get-tuple-element.51), channel_id=1, source_target_pairs={{0,112},{16,96},{32,16},{48,0},{64,48},{80,32},{96,80},{112,64},{1... | collective-permute-start | bytes 589832 | tf_op jit(solution)/shard_map/ppermute | solution.py:413
  184.2 24.4 %collective-permute-start.9 = (bf16[384,256]{1,0:T(8,128)(2,1)}, bf16[384,256]{1,0:T(8,128)(2,1)S(1)}, u32[]{:S(2)}, u32[]{:S(2)}) collective-permute-start(bf16[384,256]{1,0:T(8,128)(2,1)} %get-tuple-element.52), channel_id=1, source_target_pairs={{0,16},{16,0},{32,48},{48,32},{64,80},{80,64},{96,112},{112,96},{1... | collective-permute-start | bytes 589832 | tf_op jit(solution)/shard_map/ppermute | solution.py:413
  189.4 19.1 %copy-start.9 = (bf16[384,256]{1,0:T(8,128)(2,1)S(1)}, bf16[384,256]{1,0:T(8,128)(2,1)}, u32[]{:S(2)}) copy-start(bf16[384,256]{1,0:T(8,128)(2,1)} %get-tuple-element.64) | copy-start | bytes 589828
  189.4 19.1 %collective-permute-start.10 = (bf16[384,256]{1,0:T(8,128)(2,1)}, bf16[384,256]{1,0:T(8,128)(2,1)}, u32[]{:S(2)}, u32[]{:S(2)}) collective-permute-start(bf16[384,256]{1,0:T(8,128)(2,1)} %get-tuple-element.53), channel_id=1, source_target_pairs={{0,96},{16,112},{32,0},{48,16},{64,32},{80,48},{96,64},{112,80},{1... | collective-permute-start | bytes 589832 | tf_op jit(solution)/shard_map/ppermute | solution.py:413
